TPU v7x, 32 devices: a whole 2x2x4 slice. The times are simulated.
32 devices in a mesh: dp: 8 (over z, y), mp: 4 (over x, core).
Axes of the slice: x: 2, y: 2, z: 4, core: 2. Of those that a mesh axis runs over, the one named last changes fastest.
Arguments:
- tokens: bfloat16 [8192, 2048], P('dp'), may hold values from -6 to 6
- cotangent: bfloat16 [8192, 2048], P('dp'), may hold values from -6 to 6
- query_weight: bfloat16 [2048, 2048], P('dp', 'mp'), may hold values from -0.125 to 0.125
- key_matrix: bfloat16 [2048, 1024], P('dp', 'mp'), may hold values from -0.125 to 0.125
- value_matrix: bfloat16 [2048, 1024], P('dp', 'mp'), may hold values from -0.125 to 0.125
- head_gate_weight: bfloat16 [2048, 16], P('dp', 'mp'), may hold values from -0.125 to 0.125
- out_weight: bfloat16 [2048, 2048], P('mp', 'dp'), may hold values from -3 to 3
- gate_weight: bfloat16 [2048, 6144], P('dp', 'mp'), may hold values from -0.125 to 0.125
- up_weight: bfloat16 [2048, 6144], P('dp', 'mp'), may hold values from -0.125 to 0.125
- down_weight: bfloat16 [6144, 2048], P('mp', 'dp'), may hold values from -0.078125 to 0.078125
- norm_attn: bfloat16 [2048], P('dp'), may hold values from 0.5 to 1.5
- norm_mlp: bfloat16 [2048], P('dp'), may hold values from 0.5 to 1.5
- norm_query: bfloat16 [128], replicated, may hold values from 0.25 to 1.75
- norm_key: bfloat16 [128], replicated, may hold values from 0.25 to 1.75
- cont_lengths: int32 [2, 3, 2, 4], replicated, may hold values from 1 to 256, 512 in all within a row
Outputs:
- layer_out: bfloat16 [8192, 2048], P('dp')
- tokens_grad: float32 [8192, 2048], P('dp')
- query_weight_grad: float32 [2048, 2048], P('dp', 'mp')
- key_weight_grad: float32 [2048, 1024], P('dp', 'mp')
- value_weight_grad: float32 [2048, 1024], P('dp', 'mp')
- head_gate_weight_grad: float32 [2048, 16], P('dp', 'mp')
- out_weight_grad: float32 [2048, 2048], P('mp', 'dp')
- gate_weight_grad: float32 [2048, 6144], P('dp', 'mp')
- up_weight_grad: float32 [2048, 6144], P('dp', 'mp')
- down_weight_grad: float32 [6144, 2048], P('mp', 'dp')
- norm_attn_grad: float32 [2048], P('dp')
- norm_mlp_grad: float32 [2048], P('dp')
- norm_query_grad: float32 [128], replicated
- norm_key_grad: float32 [128], replicated
Inputs may be any that keep to these rules, and one draw needn't show every extreme that they name: `cont_lengths`: each row holds the lengths of the 4 continuations of one device in one micro-batch, in order; a row sums to 512 and its longest length is exactly 256.
All inputs are finite; a program needn't handle non-finite values.
Results may differ from a plain program's by a relative error of at most 0.024.
Values may be sent and summed in bfloat16 or wider, within the bound.
No kernel may reach another device: no remote copies, remote signals or barrier semaphores. Data moves between devices by JAX's collectives and lax.ppermute only.
A program may use at most 256 MiB of HBM per device.

v0:
```python
import jax
import jax.numpy as jnp
from jax import lax
from jax.sharding import PartitionSpec as P

MICRO_BATCHES = 2
GROUP_DEVICES = 4


eps = 1e-06
rope_base = 1000000.0
masked = -1e30


def swapped(block, axis, apart):
    count = lax.axis_size(axis)
    route = []
    for low in range(count):
        high = low | 1 << apart
        if high != low and high < count:
            route += [(low, high), (high, low)]
    return lax.ppermute(block, axis, route)


def product(left_side, right_side):
    return jnp.dot(left_side, right_side, preferred_element_type=jnp.float32)


def by_transpose(left_side, right_side):
    return lax.dot_general(
        left_side, right_side, (((1,), (1,)), ((), ())), preferred_element_type=jnp.float32
    )


def transpose_by(left_side, right_side):
    return lax.dot_general(
        left_side, right_side, (((0,), (0,)), ((), ())), preferred_element_type=jnp.float32
    )


def recip_rms(values):
    return lax.rsqrt(jnp.mean(values * values, axis=-1, keepdims=True) + eps)


def rms_back(values, reciprocal, gain, gradient):
    scaled = gain * gradient
    cubed = reciprocal * reciprocal * reciprocal
    back = reciprocal * scaled - values * cubed * jnp.mean(scaled * values, axis=-1, keepdims=True)
    return (back, gradient * values * reciprocal)


def apply_rotary(values, cosine_rows, sine_table):
    half_dim = values.shape[-1] // 2
    leading = values[..., :half_dim]
    trailing = values[..., half_dim:]
    return jnp.concatenate(
        [
            leading * cosine_rows - trailing * sine_table,
            trailing * cosine_rows + leading * sine_table,
        ],
        axis=-1,
    )


def across_heads(values):
    return lax.psum(values.astype(jnp.bfloat16), "mp").astype(jnp.float32)


def layout(lengths, relative, row_count):
    seg_ends = jnp.cumsum(lengths, dtype=jnp.int32)
    starts = seg_ends - lengths
    row_ids = jnp.arange(row_count, dtype=jnp.int32)
    seg_index = jnp.sum(
        (row_ids[:, None] >= seg_ends[None, :]).astype(jnp.int32), axis=1, dtype=jnp.int32
    )
    seg_onehot = seg_index[:, None] == jnp.arange(lengths.shape[0], dtype=jnp.int32)[None, :]
    seg_start = jnp.sum(jnp.where(seg_onehot, starts[None, :], 0), axis=1, dtype=jnp.int32)
    prompt = relative == 0
    segment = jnp.where(prompt, 0, 1 + seg_index)
    position = jnp.where(prompt, row_ids, row_count + row_ids - seg_start)
    return (segment, position)


def scores_of(grouped_queries, gathered_keys, allowed, score_scale):
    unscaled_scores = (
        jnp.einsum(
            "mhzk,ihk->hzmi", grouped_queries, gathered_keys, preferred_element_type=jnp.float32
        )
        * score_scale
    )
    return jnp.where(allowed[None, None], unscaled_scores, masked)


def on_device(
    tokens,
    cotangent,
    query_weight,
    key_matrix,
    value_matrix,
    head_gate_weight,
    out_weight,
    gate_weight,
    up_weight,
    down_weight,
    norm_attn,
    norm_mlp,
    norm_query,
    norm_key,
    cont_lengths,
):
    dp_index = lax.axis_index("dp")
    offset = dp_index % GROUP_DEVICES
    group_index = dp_index // GROUP_DEVICES
    levels = GROUP_DEVICES.bit_length() - 1
    block_rows = tokens.shape[0] // MICRO_BATCHES
    head_dim = norm_query.shape[0]
    score_scale = head_dim ** (-0.5)
    gain_query = norm_query.astype(jnp.float32)
    key_gain = norm_key.astype(jnp.float32)
    inverse = jnp.power(rope_base, -jnp.arange(head_dim // 2, dtype=jnp.float32) * (2.0 / head_dim))
    outputs = []
    input_grads = []
    totals = None
    head_totals = None
    for micro_step in range(MICRO_BATCHES):
        current = (
            lax.all_gather(query_weight, "dp", axis=0, tiled=True),
            lax.all_gather(key_matrix, "dp", axis=0, tiled=True),
            lax.all_gather(value_matrix, "dp", axis=0, tiled=True),
            lax.all_gather(head_gate_weight, "dp", axis=0, tiled=True),
            lax.all_gather(out_weight, "dp", axis=1, tiled=True),
            lax.all_gather(gate_weight, "dp", axis=0, tiled=True),
            lax.all_gather(up_weight, "dp", axis=0, tiled=True),
            lax.all_gather(down_weight, "dp", axis=1, tiled=True),
            lax.all_gather(norm_attn, "dp", axis=0, tiled=True),
            lax.all_gather(norm_mlp, "dp", axis=0, tiled=True),
        )
        (
            query_full,
            key_full,
            value_full,
            head_gate_full,
            out_full,
            gate_full,
            up_full,
            down_full,
            gain_low_attn,
            gain_low_mlp,
        ) = current
        gain_attn = gain_low_attn.astype(jnp.float32)
        gain_mlp = gain_low_mlp.astype(jnp.float32)
        head_count = head_gate_full.shape[1]
        kv_heads = key_full.shape[1] // head_dim
        repeat_heads = head_count // kv_heads
        holder = GROUP_DEVICES - 1 if micro_step % 2 == 1 else 0
        relative = jnp.bitwise_xor(offset, holder)
        prompt = relative == 0
        lengths = cont_lengths[group_index, jnp.maximum(relative - 1, 0), micro_step]
        segment, position = layout(lengths, relative, block_rows)
        angles = position.astype(jnp.float32)[:, None] * inverse[None, :]
        cosine_rows = jnp.cos(angles)[:, None, :]
        sine_table = jnp.sin(angles)[:, None, :]
        own_mask = (segment[:, None] == segment[None, :]) & (position[None, :] <= position[:, None])
        far_mask = jnp.broadcast_to(jnp.logical_not(prompt), (block_rows, block_rows))
        allowed = jnp.concatenate([far_mask, own_mask], axis=1)
        inputs = tokens[micro_step * block_rows : (micro_step + 1) * block_rows].astype(jnp.float32)
        recip_one = recip_rms(inputs)
        normed_one = (inputs * recip_one * gain_attn).astype(jnp.bfloat16)
        query_proj = product(normed_one, query_full)
        projected_keys = product(normed_one, key_full)
        projected_values = product(normed_one, value_full)
        gate_logit = product(normed_one, head_gate_full)
        query_heads = query_proj.reshape(block_rows, head_count, head_dim)
        key_heads = projected_keys.reshape(block_rows, kv_heads, head_dim)
        recip_query = recip_rms(query_heads)
        recip_key = recip_rms(key_heads)
        rotated_queries = apply_rotary(
            query_heads * recip_query * gain_query, cosine_rows, sine_table
        ).astype(jnp.bfloat16)
        rotated_keys = apply_rotary(
            key_heads * recip_key * key_gain, cosine_rows, sine_table
        ).astype(jnp.bfloat16)
        values_lower = projected_values.reshape(block_rows, kv_heads, head_dim).astype(jnp.bfloat16)
        received = (rotated_keys, values_lower)
        for bit_level in range(levels):
            arrived = swapped((received[0], received[1]), "dp", bit_level)
            taking = relative // (1 << bit_level) == 1
            received = (
                jnp.where(taking, arrived[0], received[0]),
                jnp.where(taking, arrived[1], received[1]),
            )
        gathered_keys = jnp.concatenate([received[0], rotated_keys], axis=0)
        gathered_values = jnp.concatenate([received[1], values_lower], axis=0)
        grouped_queries = rotated_queries.reshape(block_rows, kv_heads, repeat_heads, head_dim)
        scores = scores_of(grouped_queries, gathered_keys, allowed, score_scale)
        row_peak = jnp.max(scores, axis=-1, keepdims=True)
        exponent = jnp.exp(scores - row_peak)
        row_total = jnp.sum(exponent, axis=-1, keepdims=True)
        probabilities_lower = (exponent / row_total).astype(jnp.bfloat16)
        log_total = row_peak + jnp.log(row_total)
        attended = jnp.einsum(
            "ycxu,uyi->xyci",
            probabilities_lower,
            gathered_values,
            preferred_element_type=jnp.float32,
        ).reshape(block_rows, head_count, head_dim)
        head_gate = jax.nn.sigmoid(gate_logit)
        gated_low = (
            (attended * head_gate[:, :, None])
            .reshape(block_rows, head_count * head_dim)
            .astype(jnp.bfloat16)
        )
        middle = inputs + across_heads(product(gated_low, out_full))
        recip_two = recip_rms(middle)
        normed_two = (middle * recip_two * gain_mlp).astype(jnp.bfloat16)
        gate_pre = product(normed_two, gate_full)
        up_pre = product(normed_two, up_full)
        sigmoid_gate = jax.nn.sigmoid(gate_pre)
        swish_gate = gate_pre * sigmoid_gate
        hidden_low = (swish_gate * up_pre).astype(jnp.bfloat16)
        mlp_out = across_heads(product(hidden_low, down_full))
        outputs.append((middle + mlp_out).astype(jnp.bfloat16))
        upstream = cotangent[micro_step * block_rows : (micro_step + 1) * block_rows].astype(
            jnp.float32
        )
        upstream_low = upstream.astype(jnp.bfloat16)
        hidden_grad = by_transpose(upstream_low, down_full)
        down_term = transpose_by(hidden_low, upstream_low)
        gate_grad = (
            hidden_grad * up_pre * sigmoid_gate * (1.0 + gate_pre * (1.0 - sigmoid_gate))
        ).astype(jnp.bfloat16)
        up_grad = (hidden_grad * swish_gate).astype(jnp.bfloat16)
        gate_term = transpose_by(normed_two, gate_grad)
        up_term = transpose_by(normed_two, up_grad)
        normed_two_grad = across_heads(
            by_transpose(gate_grad, gate_full) + by_transpose(up_grad, up_full)
        )
        middle_back, mlp_gain_terms = rms_back(middle, recip_two, gain_mlp, normed_two_grad)
        middle_grad = upstream + middle_back
        middle_low = middle_grad.astype(jnp.bfloat16)
        gated_grad = by_transpose(middle_low, out_full).reshape(block_rows, head_count, head_dim)
        out_term = transpose_by(gated_low, middle_low)
        attended_low = (gated_grad * head_gate[:, :, None]).astype(jnp.bfloat16)
        logit_grad = (
            jnp.sum(gated_grad * attended, axis=-1) * head_gate * (1.0 - head_gate)
        ).astype(jnp.bfloat16)
        again = scores_of(grouped_queries, gathered_keys, allowed, score_scale)
        probs_again = jnp.exp(again - log_total)
        group_gradient = attended_low.reshape(block_rows, kv_heads, repeat_heads, head_dim)
        prob_grad = jnp.einsum(
            "mhzk,ihk->hzmi", group_gradient, gathered_values, preferred_element_type=jnp.float32
        )
        scores_gradient = (
            probs_again * (prob_grad - jnp.sum(probs_again * prob_grad, axis=-1, keepdims=True))
        ).astype(jnp.bfloat16)
        query_rot_grad = (
            jnp.einsum(
                "ycxu,uyi->xyci", scores_gradient, gathered_keys, preferred_element_type=jnp.float32
            ).reshape(block_rows, head_count, head_dim)
            * score_scale
        )
        key_all_grad = (
            jnp.einsum(
                "jcuk,ujca->kja",
                scores_gradient,
                grouped_queries,
                preferred_element_type=jnp.float32,
            )
            * score_scale
        )
        value_all_grad = jnp.einsum(
            "jcuk,ujca->kja",
            probs_again.astype(jnp.bfloat16),
            group_gradient,
            preferred_element_type=jnp.float32,
        )
        returned = (key_all_grad[:block_rows], value_all_grad[:block_rows])
        for bit_level in reversed(range(levels)):
            arrived = (
                swapped(returned[0].astype(jnp.bfloat16), "dp", bit_level).astype(jnp.float32),
                swapped(returned[1].astype(jnp.bfloat16), "dp", bit_level).astype(jnp.float32),
            )
            adding = relative < 1 << bit_level
            returned = (
                jnp.where(adding, returned[0] + arrived[0], returned[0]),
                jnp.where(adding, returned[1] + arrived[1], returned[1]),
            )
        key_rot_grad = key_all_grad[block_rows:] + jnp.where(prompt, returned[0], 0.0)
        value_grad = value_all_grad[block_rows:] + jnp.where(prompt, returned[1], 0.0)
        query_heads_grad, query_gain_terms = rms_back(
            query_heads,
            recip_query,
            gain_query,
            apply_rotary(query_rot_grad, cosine_rows, -sine_table),
        )
        key_heads_grad, key_gain_terms = rms_back(
            key_heads, recip_key, key_gain, apply_rotary(key_rot_grad, cosine_rows, -sine_table)
        )
        query_low = query_heads_grad.reshape(block_rows, head_count * head_dim).astype(jnp.bfloat16)
        key_low = key_heads_grad.reshape(block_rows, kv_heads * head_dim).astype(jnp.bfloat16)
        value_low_grad = value_grad.reshape(block_rows, kv_heads * head_dim).astype(jnp.bfloat16)
        normed_one_grad = across_heads(
            by_transpose(query_low, query_full)
            + by_transpose(key_low, key_full)
            + by_transpose(value_low_grad, value_full)
            + by_transpose(logit_grad, head_gate_full)
        )
        input_back, attn_gain_terms = rms_back(inputs, recip_one, gain_attn, normed_one_grad)
        input_grads.append(middle_grad + input_back)
        terms = (
            transpose_by(normed_one, query_low),
            transpose_by(normed_one, key_low),
            transpose_by(normed_one, value_low_grad),
            transpose_by(normed_one, logit_grad),
            out_term,
            gate_term,
            up_term,
            down_term,
            jnp.sum(attn_gain_terms, axis=0),
            jnp.sum(mlp_gain_terms, axis=0),
        )
        head_terms = (jnp.sum(query_gain_terms, axis=(0, 1)), jnp.sum(key_gain_terms, axis=(0, 1)))
        if totals is None:
            totals = terms
            head_totals = head_terms
        else:
            totals = tuple(
                (jnp.add(left_side, right_side) for left_side, right_side in zip(totals, terms))
            )
            head_totals = tuple(
                (
                    jnp.add(left_side, right_side)
                    for left_side, right_side in zip(head_totals, head_terms)
                )
            )
    reduced = (
        lax.psum_scatter(
            totals[0].astype(jnp.bfloat16), "dp", scatter_dimension=0, tiled=True
        ).astype(jnp.float32),
        lax.psum_scatter(
            totals[1].astype(jnp.bfloat16), "dp", scatter_dimension=0, tiled=True
        ).astype(jnp.float32),
        lax.psum_scatter(
            totals[2].astype(jnp.bfloat16), "dp", scatter_dimension=0, tiled=True
        ).astype(jnp.float32),
        lax.psum_scatter(
            totals[3].astype(jnp.bfloat16), "dp", scatter_dimension=0, tiled=True
        ).astype(jnp.float32),
        lax.psum_scatter(
            totals[4].astype(jnp.bfloat16), "dp", scatter_dimension=1, tiled=True
        ).astype(jnp.float32),
        lax.psum_scatter(
            totals[5].astype(jnp.bfloat16), "dp", scatter_dimension=0, tiled=True
        ).astype(jnp.float32),
        lax.psum_scatter(
            totals[6].astype(jnp.bfloat16), "dp", scatter_dimension=0, tiled=True
        ).astype(jnp.float32),
        lax.psum_scatter(
            totals[7].astype(jnp.bfloat16), "dp", scatter_dimension=1, tiled=True
        ).astype(jnp.float32),
        lax.psum_scatter(
            totals[8].astype(jnp.bfloat16), "dp", scatter_dimension=0, tiled=True
        ).astype(jnp.float32),
        lax.psum_scatter(
            totals[9].astype(jnp.bfloat16), "dp", scatter_dimension=0, tiled=True
        ).astype(jnp.float32),
    )
    head_grads = lax.psum((head_totals[0], head_totals[1]), ("dp", "mp"))
    layer_out = jnp.concatenate(outputs, axis=0)
    tokens_grad = jnp.concatenate(input_grads, axis=0)
    return (
        layer_out,
        tokens_grad,
        reduced[0],
        reduced[1],
        reduced[2],
        reduced[3],
        reduced[4],
        reduced[5],
        reduced[6],
        reduced[7],
        reduced[8],
        reduced[9],
        head_grads[0],
        head_grads[1],
    )


def solution(mesh):
    placed = (
        P("dp", None),
        P("dp", None),
        P("dp", "mp"),
        P("dp", "mp"),
        P("dp", "mp"),
        P("dp", "mp"),
        P("mp", "dp"),
        P("dp", "mp"),
        P("dp", "mp"),
        P("mp", "dp"),
        P("dp"),
        P("dp"),
        P(),
        P(),
        P(),
    )
    return jax.shard_map(
        on_device,
        mesh=mesh,
        in_specs=placed,
        out_specs=(
            P("dp", None),
            P("dp", None),
            P("dp", "mp"),
            P("dp", "mp"),
            P("dp", "mp"),
            P("dp", "mp"),
            P("mp", "dp"),
            P("dp", "mp"),
            P("dp", "mp"),
            P("mp", "dp"),
            P("dp"),
            P("dp"),
            P(),
            P(),
        ),
        check_vma=False,
    )
```

profile of v0, /device:TPU:0, one launch (start us, length us, event | category | flops | bytes accessed | tf_op | source)
XLA Modules:
  0.0 1649.9 jit_solution(7662269726761656505)
XLA Ops:
  15.7 3.1 fusion.34
  18.8 22.3 %all-gather = bf16[8,1,256]{2,1,0:T(2,128)(2,1)S(1)} all-gather(bf16[1,1,256]{2,1,0:T(2,128)(2,1)S(1)} %reshape.592), channel_id=1, replica_groups=mesh['dp'=8,'mp'=4] {'dp'}, dimensions={0}, use_global_device_ids=true | all-gather | bytes 4608 | tf_op jit(solution)/shard_map/all_gather | solution.py:135
  41.7 26.0 %all_gather.44 = bf16[2048,4]{0,1:T(4,128)(2,1)S(1)} all-gather(bf16[256,4]{0,1:T(4,128)(2,1)S(1)} %copy-done.135), channel_id=1, replica_groups=mesh['dp'=8,'mp'=4] {'dp'}, dimensions={0}, use_global_device_ids=true | all-gather | bytes 18432 | tf_op jit(solution)/shard_map/all_gather | solution.py:130
  70.0 3.0 fusion.36
  79.6 3.6 multiply_reduce_fusion.8
  89.7 6.6 all-gather.10.cloned.1.call-done
  96.3 2.7 convolution_convert_fusion.5
  105.6 3.3 convolution_convert_fusion.4
  114.8 3.9 collective-permute-done.6
  125.6 4.9 collective-permute-done.1
  131.2 15.8 collective-permute-done.7
  147.8 9.3 collective-permute-done.5
  157.8 3.1 multiply_reduce_fusion.5
  166.6 3.6 fusion.136
  173.6 2.7 fusion.50
  184.9 25.4 %all-gather.16.cloned.1.call-done = bf16[512,2048]{1,0:T(8,128)(2,1)} async-done(((bf16[512,256]{1,0:T(8,128)(2,1)}), bf16[512,2048]{1,0:T(8,128)(2,1)}) %all-gather.16.cloned.1.call-update) | async-done | bytes 2097168 | tf_op jit(solution)/shard_map/all_gather | solution.py:131
  210.3 4.4 convolution_convert_fusion.3
  219.4 17.7 %all-gather.1 = bf16[8,1,256]{2,1,0:T(2,128)(2,1)S(1)} all-gather(bf16[1,1,256]{2,1,0:T(2,128)(2,1)S(1)} %reshape.594), channel_id=1, replica_groups=mesh['dp'=8,'mp'=4] {'dp'}, dimensions={0}, use_global_device_ids=true | all-gather | bytes 4608 | tf_op jit(solution)/shard_map/all_gather | solution.py:136
  237.1 64.1 %all-reduce.17.cloned.1.call-done = (bf16[512,2048]{1,0:T(8,128)(2,1)}, bf16[512,2048]{1,0:T(8,128)(2,1)}) async-done(((bf16[512,2048]{1,0:T(8,128)(2,1)}, bf16[512,2048]{1,0:T(8,128)(2,1)}), (bf16[512,2048]{1,0:T(8,128)(2,1)}, bf16[512,2048]{1,0:T(8,128)(2,1)})) %all-reduce.17.cloned.1.call-update) | async-done | bytes 4194320 | tf_op jit(solution)/shard_map/psum | solution.py:66
  301.3 5.0 multiply_reduce_fusion.1
  307.2 3.9 multiply_convert_fusion.1
  311.2 91.6 %all-gather.18.cloned.1.call-done = bf16[2048,1536]{1,0:T(8,128)(2,1)} async-done(((bf16[256,1536]{1,0:T(8,128)(2,1)}), bf16[2048,1536]{1,0:T(8,128)(2,1)}) %all-gather.18.cloned.1.call-update) | async-done | bytes 6291472 | tf_op jit(solution)/shard_map/all_gather | solution.py:132
  402.8 8.5 fusion.137
  411.3 91.2 %all-gather.20.cloned.1.call-done = bf16[2048,1536]{1,0:T(8,128)(2,1)} async-done(((bf16[256,1536]{1,0:T(8,128)(2,1)}), bf16[2048,1536]{1,0:T(8,128)(2,1)}) %all-gather.20.cloned.1.call-update) | async-done | bytes 6291472 | tf_op jit(solution)/shard_map/all_gather | solution.py:133
  502.4 8.7 fusion.138
  511.1 5.1 fusion.139
  516.2 5.1 fusion.140
  521.3 81.5 %all-gather.22.cloned.1.call-done = bf16[1536,2048]{1,0:T(8,128)(2,1)} async-done(((bf16[1536,256]{1,0:T(8,128)(2,1)}), bf16[1536,2048]{1,0:T(8,128)(2,1)}) %all-gather.22.cloned.1.call-update) | async-done | bytes 6291472 | tf_op jit(solution)/shard_map/all_gather | solution.py:134
  602.8 10.8 multiply_convert_fusion.4
  614.8 8.1 fusion.141
  623.0 7.9 multiply_convert_fusion.2
  630.9 6.2 fusion.145
  637.1 7.6 add_convert_fusion.8
  644.7 4.7 add_convert_fusion.6
  652.0 81.4 %all-reduce.15.cloned.1.call-done = (bf16[512,2048]{1,0:T(8,128)(2,1)}, bf16[512,2048]{1,0:T(8,128)(2,1)}) async-done(((bf16[512,2048]{1,0:T(8,128)(2,1)}, bf16[512,2048]{1,0:T(8,128)(2,1)}), (bf16[512,2048]{1,0:T(8,128)(2,1)}, bf16[512,2048]{1,0:T(8,128)(2,1)})) %all-reduce.15.cloned.1.call-update) | async-done | bytes 4194320 | tf_op jit(solution)/shard_map/psum | solution.py:66
  733.4 7.3 fusion.27
  740.8 6.9 fusion.24
  749.7 6.2 fusion.3
  765.6 2.8 fusion.71
  770.6 4.7 fusion.5
  787.0 5.7 collective-permute-done.10
  806.4 3.0 collective-permute-done.15
  829.2 3.6 fusion.93
  835.5 8.2 convolution_convert_fusion.2
  851.0 2.7 add_convert_fusion.4
  854.3 7.6 convolution_convert_fusion
  873.1 5.8 fusion.154
  878.9 5.6 add_convert_fusion.1
  884.6 5.7 fusion.153
  890.3 5.7 add_convert_fusion.2
  897.4 5.2 fusion.60
  902.7 7.2 add_convert_fusion
  913.4 40.5 %all-reduce.4 = (f32[128]{0:T(128)}, f32[128]{0:T(128)}) all-reduce(f32[128]{0:T(128)S(1)} %add.438, f32[128]{0:T(128)S(1)} %add.439), channel_id=1, replica_groups=mesh['dp'=8,'mp'=4] {'dp','mp'}, use_global_device_ids=true, to_apply=%region_56.57 | all-reduce | flops 256 | bytes 2048 | tf_op jit(solution)/shard_map/psum | solution.py:368
  955.6 22.2 %reduce-scatter.13.cloned.1.call-done = bf16[256,256]{1,0:T(8,128)(2,1)} async-done(((bf16[2048,256]{1,0:T(8,128)(2,1)}), bf16[256,256]{1,0:T(8,128)(2,1)}) %reduce-scatter.13.cloned.1.call-update) | async-done | bytes 131088 | tf_op jit(solution)/shard_map/reduce_scatter | solution.py:340
  979.4 69.4 %reduce-scatter.17.cloned.1.call-done = bf16[512,256]{1,0:T(8,128)(2,1)} async-done(((bf16[512,2048]{1,0:T(8,128)(2,1)}), bf16[512,256]{1,0:T(8,128)(2,1)}) %reduce-scatter.17.cloned.1.call-update) | async-done | bytes 262160 | tf_op jit(solution)/shard_map/reduce_scatter | solution.py:349
  1050.7 69.0 %reduce-scatter.11.cloned.1.call-done = bf16[256,512]{1,0:T(8,128)(2,1)} async-done(((bf16[2048,512]{1,0:T(8,128)(2,1)}), bf16[256,512]{1,0:T(8,128)(2,1)}) %reduce-scatter.11.cloned.1.call-update) | async-done | bytes 262160 | tf_op jit(solution)/shard_map/reduce_scatter | solution.py:337
  1121.5 154.5 %all-reduce.13.cloned.1.call-done = (bf16[512,2048]{1,0:T(8,128)(2,1)}, bf16[512,2048]{1,0:T(8,128)(2,1)}, bf16[512,2048]{1,0:T(8,128)(2,1)}, bf16[512,2048]{1,0:T(8,128)(2,1)}) async-done(((bf16[512,2048]{1,0:T(8,128)(2,1)}, bf16[512,2048]{1,0:T(8,128)(2,1)}, bf16[512,2048]{1,0:T(8,128)(2,1)}, bf16[512,2048]{1,0:T(8,128)(2,1)}), (bf16[512,2048]{1,0:T(8,128)(2,1)}, bf16[512,2048]{1,0:T(8,128)(2,1)}, ...) | async-done | bytes 8388624 | tf_op jit(solution)/shard_map/psum | solution.py:66
  1276.0 5.3 fusion.40
  1281.3 22.9 %all-reduce.5 = (bf16[2048]{0:T(1024)(128)(2,1)S(1)}, bf16[2048]{0:T(1024)(128)(2,1)S(1)}) all-reduce(bf16[2048]{0:T(1024)(128)(2,1)S(1)} %add_convert_fusion.16, bf16[2048]{0:T(1024)(128)(2,1)S(1)} %add_convert_fusion.15), channel_id=10, replica_groups=mesh['dp'=8,'mp'=4] {'dp'}, use_global_device_ids=true, to_apply=%region_48.49.clone | all-reduce | flops 4096 | bytes 16384
  1305.6 10.0 fusion.22
  1318.1 4.0 pad_maximum_fusion
  1322.1 75.9 %reduce-scatter.21.cloned.1.call-done = bf16[256,1536]{1,0:T(8,128)(2,1)} async-done(((bf16[2048,1536]{1,0:T(8,128)(2,1)}), bf16[256,1536]{1,0:T(8,128)(2,1)}) %reduce-scatter.21.cloned.1.call-update) | async-done | bytes 786448 | tf_op jit(solution)/shard_map/reduce_scatter | solution.py:355
  1400.5 118.5 %reduce-scatter.19.cloned.1.call-done = bf16[256,1536]{1,0:T(8,128)(2,1)} async-done(((bf16[2048,1536]{1,0:T(8,128)(2,1)}), bf16[256,1536]{1,0:T(8,128)(2,1)}) %reduce-scatter.19.cloned.1.call-update) | async-done | bytes 786448 | tf_op jit(solution)/shard_map/reduce_scatter | solution.py:352
  1521.4 119.0 %reduce-scatter.23.cloned.1.call-done = bf16[1536,256]{1,0:T(8,128)(2,1)} async-done(((bf16[1536,2048]{1,0:T(8,128)(2,1)}), bf16[1536,256]{1,0:T(8,128)(2,1)}) %reduce-scatter.23.cloned.1.call-update) | async-done | bytes 786448 | tf_op jit(solution)/shard_map/reduce_scatter | solution.py:358
  (550 shorter events, 174.4 us)
Async XLA Ops:
  7.2 33.9 %copy-start.139 = (bf16[128]{0:T(256)(128)(2,1)S(1)}, bf16[128]{0:T(256)(128)(2,1)}, u32[]{:S(2)}) copy-start(bf16[128]{0:T(256)(128)(2,1)} %param.28) | copy-start | bytes 772
  7.2 34.0 %copy-start.140 = (bf16[128]{0:T(256)(128)(2,1)S(1)}, bf16[128]{0:T(256)(128)(2,1)}, u32[]{:S(2)}) copy-start(bf16[128]{0:T(256)(128)(2,1)} %param.27) | copy-start | bytes 772
  7.2 34.5 %copy-start.135 = (bf16[256,4]{0,1:T(4,128)(2,1)S(1)}, bf16[256,4]{0,1:T(4,128)(2,1)}, u32[]{:S(2)}) copy-start(bf16[256,4]{0,1:T(4,128)(2,1)} %param.20) | copy-start | bytes 6148
  7.2 70.2 %all-gather.12.cloned.1.call-start = ((), (), s32[]{:S(2)}) async-start(), calls=%async_computation.9 | async-start | bytes 1179648 | tf_op jit(solution)/shard_map/all_gather | solution.py:128
  8.0 88.3 %all-gather.10.cloned.1.call-start = ((), (), s32[]{:S(2)}) async-start(), calls=%async_computation.8 | async-start | bytes 1179648 | tf_op jit(solution)/shard_map/all_gather | solution.py:129
  8.7 149.1 %all-gather.14.cloned.1.call-start = ((), (), s32[]{:S(2)}) async-start(), calls=%async_computation.10 | async-start | bytes 2359296 | tf_op jit(solution)/shard_map/all_gather | solution.py:127
  9.4 200.9 %all-gather.16.cloned.1.call-start = ((), (), s32[]{:S(2)}) async-start(), calls=%async_computation.11 | async-start | bytes 2359296 | tf_op jit(solution)/shard_map/all_gather | solution.py:131
  10.0 291.3 %all-reduce.17.cloned.1.call-start = ((), (), s32[]{:S(2)}) async-start(), calls=%async_computation.25 | async-start | bytes 8388608 | tf_op jit(solution)/shard_map/psum | solution.py:66
  14.0 56.0 %copy-start.73 = (f32[512,64]{0,1:T(8,128)}, f32[512,64]{0,1:T(8,128)S(1)}, u32[]{:S(2)}) copy-start(f32[512,64]{0,1:T(8,128)S(1)} %get-tuple-element.121) | copy-start | bytes 393220
  14.0 56.0 %copy-start.88 = (f32[512,64]{0,1:T(8,128)}, f32[512,64]{0,1:T(8,128)S(1)}, u32[]{:S(2)}) copy-start(f32[512,64]{0,1:T(8,128)S(1)} %get-tuple-element.120) | copy-start | bytes 393220
  14.0 56.0 %copy-start.90 = (f32[512,64]{0,1:T(8,128)}, f32[512,64]{0,1:T(8,128)S(1)}, u32[]{:S(2)}) copy-start(f32[512,64]{0,1:T(8,128)S(1)} %get-tuple-element.107) | copy-start | bytes 393220
  14.0 150.3 %copy-start.71 = (f32[512,64]{0,1:T(8,128)}, f32[512,64]{0,1:T(8,128)S(1)}, u32[]{:S(2)}) copy-start(f32[512,64]{0,1:T(8,128)S(1)} %get-tuple-element.108) | copy-start | bytes 393220
  41.1 31.9 %copy-start.109 = (f32[8,1,256]{2,1,0:T(1,128)}, f32[8,1,256]{2,1,0:T(1,128)S(1)}, u32[]{:S(2)}) copy-start(f32[8,1,256]{2,1,0:T(1,128)S(1)} %convert_element_type.428) | copy-start | bytes 24580
  41.2 44.6 %copy-start.133 = (f32[128]{0:T(128)}, f32[128]{0:T(128)S(1)}, u32[]{:S(2)}) copy-start(f32[128]{0:T(128)S(1)} %convert_element_type.332) | copy-start | bytes 1540
  73.0 84.8 %copy-start.4 = (bf16[512,2048]{1,0:T(8,128)(2,1)}, bf16[512,2048]{1,0:T(8,128)(2,1)S(1)}, u32[]{:S(2)}) copy-start(bf16[512,2048]{1,0:T(8,128)(2,1)S(1)} %get-tuple-element.64) | copy-start | bytes 6291460
  84.4 14.5 copy-start.39
  88.1 78.5 %copy-start.42 = (bf16[512,2,64]{2,0,1:T(8,128)(2,1)}, bf16[512,2,64]{2,0,1:T(8,128)(2,1)S(1)}, u32[]{:S(2)}) copy-start(bf16[512,2,64]{2,0,1:T(8,128)(2,1)S(1)} %get-tuple-element.90) | copy-start | bytes 393220
  88.1 13.2 copy-start.41
  89.7 21.1 %collective-permute-start.2 = (bf16[512,2,128]{2,0,1:T(8,128)(2,1)}, bf16[512,2,128]{2,0,1:T(8,128)(2,1)}, u32[]{:S(2)}, u32[]{:S(2)}) collective-permute-start(bf16[512,2,128]{2,0,1:T(8,128)(2,1)} %pad_maximum_fusion.8), channel_id=1, source_target_pairs={{0,4},{4,0},{8,12},{12,8},{16,20},{20,16},{24,28},{28,24},{1,5},{5... | collective-permute-start | bytes 786440 | tf_op jit(solution)/shard_map/ppermute | solution.py:22
  100.8 12.0 collective-permute-start
  102.6 19.7 %copy-start.47 = (bf16[512,2,64]{2,0,1:T(8,128)(2,1)}, bf16[512,2,64]{2,0,1:T(8,128)(2,1)S(1)}, u32[]{:S(2)}) copy-start(bf16[512,2,64]{2,0,1:T(8,128)(2,1)S(1)} %get-tuple-element.92) | copy-start | bytes 393220
  104.2 14.6 copy-start.51
  104.2 14.6 collective-permute-start.6
  110.1 50.8 %copy-start.66 = (bf16[512,2,128]{2,0,1:T(8,128)(2,1)}, bf16[512,2,128]{2,0,1:T(8,128)(2,1)S(1)}, u32[]{:S(2)}) copy-start(bf16[512,2,128]{2,0,1:T(8,128)(2,1)S(1)} %copy.216) | copy-start | bytes 786436
  110.1 12.2 collective-permute-start.4
  111.0 13.9 collective-permute-start.3
  113.7 16.8 %collective-permute-start.1 = (bf16[512,2,128]{2,0,1:T(8,128)(2,1)S(1)}, bf16[512,2,128]{2,0,1:T(8,128)(2,1)S(1)}, u32[]{:S(2)}, u32[]{:S(2)}) collective-permute-start(bf16[512,2,128]{2,0,1:T(8,128)(2,1)S(1)} %broadcast_select_fusion.5), channel_id=1, source_target_pairs={{0,8},{8,0},{4,12},{12,4},{16,24},{24,16},{20,28},{28,20},{1,9},{9... | collective-permute-start | bytes 786440 | tf_op jit(solution)/shard_map/ppermute | solution.py:22
  119.0 28.1 %collective-permute-start.7 = (bf16[512,2,128]{2,0,1:T(8,128)(2,1)S(1)}, bf16[512,2,128]{2,0,1:T(8,128)(2,1)S(1)}, u32[]{:S(2)}, u32[]{:S(2)}) collective-permute-start(bf16[512,2,128]{2,0,1:T(8,128)(2,1)S(1)} %broadcast_select_fusion), channel_id=1, source_target_pairs={{0,8},{8,0},{4,12},{12,4},{16,24},{24,16},{20,28},{28,20},{1,9},{9... | collective-permute-start | bytes 786440 | tf_op jit(solution)/shard_map/ppermute | solution.py:22
  122.3 34.8 %collective-permute-start.5 = (bf16[512,2,128]{2,0,1:T(8,128)(2,1)S(1)}, bf16[512,2,128]{2,0,1:T(8,128)(2,1)S(1)}, u32[]{:S(2)}, u32[]{:S(2)}) collective-permute-start(bf16[512,2,128]{2,0,1:T(8,128)(2,1)S(1)} %broadcast_select_fusion.1), channel_id=1, source_target_pairs={{0,8},{8,0},{4,12},{12,4},{16,24},{24,16},{20,28},{28,20},{1,9},{9... | collective-permute-start | bytes 786440 | tf_op jit(solution)/shard_map/ppermute | solution.py:22
  176.4 33.9 %copy-start.58 = (bf16[512,512]{0,1:T(8,128)(2,1)}, bf16[512,512]{0,1:T(8,128)(2,1)S(1)}, u32[]{:S(2)}) copy-start(bf16[512,512]{0,1:T(8,128)(2,1)S(1)} %fusion.89) | copy-start | bytes 1572868
  184.9 32.4 %copy-start.86 = (bf16[512,512]{0,1:T(8,128)(2,1)}, bf16[512,512]{0,1:T(8,128)(2,1)S(1)}, u32[]{:S(2)}) copy-start(bf16[512,512]{0,1:T(8,128)(2,1)S(1)} %fusion.88) | copy-start | bytes 1572868
  217.3 185.5 %all-gather.18.cloned.1.call-start = ((), (), s32[]{:S(2)}) async-start(), calls=%async_computation.12 | async-start | bytes 7077888 | tf_op jit(solution)/shard_map/all_gather | solution.py:132
  217.9 284.6 %all-gather.20.cloned.1.call-start = ((), (), s32[]{:S(2)}) async-start(), calls=%async_computation.13 | async-start | bytes 7077888 | tf_op jit(solution)/shard_map/all_gather | solution.py:133
  218.6 384.2 %all-gather.22.cloned.1.call-start = ((), (), s32[]{:S(2)}) async-start(), calls=%async_computation.14 | async-start | bytes 7077888 | tf_op jit(solution)/shard_map/all_gather | solution.py:134
  219.4 514.0 %all-reduce.15.cloned.1.call-start = ((), (), s32[]{:S(2)}) async-start(), calls=%async_computation.24 | async-start | bytes 8388608 | tf_op jit(solution)/shard_map/psum | solution.py:66
  502.4 13.8 slice-start.4
  613.7 23.4 %copy-start.144 = (bf16[512,1536]{1,0:T(8,128)(2,1)}, bf16[512,1536]{1,0:T(8,128)(2,1)S(1)}, u32[]{:S(2)}) copy-start(bf16[512,1536]{1,0:T(8,128)(2,1)S(1)} %get-tuple-element.54) | copy-start | bytes 4718596
  623.0 21.7 %slice-start.6 = ((s8[6291456]{0:T(1024)(128)(4,1)}), s8[2097152]{0:T(1024)(128)(4,1)S(1)}, s32[]{:S(2)}) async-start(s8[6291456]{0:T(1024)(128)(4,1)} %bitcast.404), calls=%async_computation.32 | async-start | bytes 4194304
  630.9 13.8 slice-start.7
  649.4 262.4 %reduce-scatter.25.cloned.1.call-start = ((), (), s32[]{:S(2)}) async-start(), calls=%async_computation.22 | async-start | bytes 589824
  762.9 17.5 %copy-start.31 = (f32[1024,2,128]{2,0,1:T(8,128)}, f32[1024,2,128]{2,0,1:T(8,128)S(1)}, u32[]{:S(2)}) copy-start(f32[1024,2,128]{2,0,1:T(8,128)S(1)} %fusion.67) | copy-start | bytes 3145732
  769.1 14.5 collective-permute-start.12
  777.6 23.4 %collective-permute-start.8 = (bf16[512,2,128]{2,0,1:T(8,128)(2,1)}, bf16[512,2,128]{2,0,1:T(8,128)(2,1)}, u32[]{:S(2)}, u32[]{:S(2)}) collective-permute-start(bf16[512,2,128]{2,0,1:T(8,128)(2,1)} %slice.231), channel_id=1, source_target_pairs={{0,8},{8,0},{4,12},{12,4},{16,24},{24,16},{20,28},{28,20},{1,9},{9... | collective-permute-start | bytes 786440 | tf_op jit(solution)/shard_map/ppermute | solution.py:22
  778.9 13.9 collective-permute-start.10
  781.1 16.4 collective-permute-start.14
  783.5 170.4 %reduce-scatter.15.cloned.1.call-start = ((), (), s32[]{:S(2)}) async-start(), calls=%async_computation.17 | async-start | bytes 1179648 | tf_op jit(solution)/shard_map/reduce_scatter | solution.py:343
  783.6 27.3 %copy-start.105 = (bf16[512,2,128]{2,0,1:T(8,128)(2,1)}, bf16[512,2,128]{2,0,1:T(8,128)(2,1)S(1)}, u32[]{:S(2)}) copy-start(bf16[512,2,128]{2,0,1:T(8,128)(2,1)S(1)} %collective-permute-done.12) | copy-start | bytes 786436
  785.5 29.8 %collective-permute-start.13 = (bf16[512,2,128]{2,0,1:T(8,128)(2,1)}, bf16[512,2,128]{2,0,1:T(8,128)(2,1)}, u32[]{:S(2)}, u32[]{:S(2)}) collective-permute-start(bf16[512,2,128]{2,0,1:T(8,128)(2,1)} %fusion.117), channel_id=1, source_target_pairs={{0,4},{4,0},{8,12},{12,8},{16,20},{20,16},{24,28},{28,24},{1,5},{5... | collective-permute-start | bytes 786440 | tf_op jit(solution)/shard_map/ppermute | solution.py:22
  793.8 9.6 collective-permute-start.11
  799.5 9.9 collective-permute-start.15
  802.9 13.7 collective-permute-start.9
  815.2 162.6 %reduce-scatter.13.cloned.1.call-start = ((), (), s32[]{:S(2)}) async-start(), calls=%async_computation.16 | async-start | bytes 1179648 | tf_op jit(solution)/shard_map/reduce_scatter | solution.py:340
  828.9 220.0 %reduce-scatter.17.cloned.1.call-start = ((), (), s32[]{:S(2)}) async-start(), calls=%async_computation.18 | async-start | bytes 2359296 | tf_op jit(solution)/shard_map/reduce_scatter | solution.py:349
  835.4 284.2 %reduce-scatter.11.cloned.1.call-start = ((), (), s32[]{:S(2)}) async-start(), calls=%async_computation.15 | async-start | bytes 2359296 | tf_op jit(solution)/shard_map/reduce_scatter | solution.py:337
  853.8 422.2 %all-reduce.13.cloned.1.call-start = ((), (), s32[]{:S(2)}) async-start(), calls=%async_computation.23 | async-start | bytes 16777216 | tf_op jit(solution)/shard_map/psum | solution.py:66
  872.8 525.2 %reduce-scatter.21.cloned.1.call-start = ((), (), s32[]{:S(2)}) async-start(), calls=%async_computation.20 | async-start | bytes 7077888 | tf_op jit(solution)/shard_map/reduce_scatter | solution.py:355
  884.5 634.5 %reduce-scatter.19.cloned.1.call-start = ((), (), s32[]{:S(2)}) async-start(), calls=%async_computation.19 | async-start | bytes 7077888 | tf_op jit(solution)/shard_map/reduce_scatter | solution.py:352
  896.0 744.4 %reduce-scatter.23.cloned.1.call-start = ((), (), s32[]{:S(2)}) async-start(), calls=%async_computation.21 | async-start | bytes 7077888 | tf_op jit(solution)/shard_map/reduce_scatter | solution.py:358
  909.8 366.1 %copy-start.110 = (f32[8,1,256]{2,1,0:T(1,128)S(1)}, f32[8,1,256]{2,1,0:T(1,128)}, u32[]{:S(2)}) copy-start(f32[8,1,256]{2,1,0:T(1,128)} %copy-done.109) | copy-start | bytes 24580
  909.9 366.1 %copy-start.124 = (f32[512]{0:T(512)S(1)}, f32[512]{0:T(512)}, u32[]{:S(2)}) copy-start(f32[512]{0:T(512)} %copy-done.123) | copy-start | bytes 6148
  909.9 366.1 %copy-start.126 = (f32[512]{0:T(512)S(1)}, f32[512]{0:T(512)}, u32[]{:S(2)}) copy-start(f32[512]{0:T(512)} %copy-done.125) | copy-start | bytes 6148
  1276.0 29.6 %copy-start.16 = (bf16[512,2048]{1,0:T(8,128)(2,1)S(1)}, bf16[512,2048]{1,0:T(8,128)(2,1)}, u32[]{:S(2)}) copy-start(bf16[512,2048]{1,0:T(8,128)(2,1)} %get-tuple-element.44) | copy-start | bytes 6291460
  1276.0 29.6 %copy-start.129 = (f32[512]{0:T(512)S(1)}, f32[512]{0:T(512)}, u32[]{:S(2)}) copy-start(f32[512]{0:T(512)} %get-tuple-element.114) | copy-start | bytes 6148
  1276.0 29.6 %copy-start.130 = (f32[512]{0:T(512)S(1)}, f32[512]{0:T(512)}, u32[]{:S(2)}) copy-start(f32[512]{0:T(512)} %get-tuple-element.148) | copy-start | bytes 6148
  (130 other events, 503.4 us)
Sparse Core Ops, SparseCore 0:
  10.2 43.0 all-gather.11
  55.4 40.8 all-gather.9
  98.4 58.3 all-gather.13
  158.7 51.5 all-gather.15
  217.4 83.8 all-reduce.16
  303.6 99.1 all-gather.17
  405.2 97.2 all-gather.19
  504.7 98.1 all-gather.21
  649.5 83.8 all-reduce.14
  783.7 62.0 reduce-scatter.24
  849.6 62.4 reduce-scatter.14
  915.3 62.4 reduce-scatter.12
  981.7 67.0 reduce-scatter.16
  1052.7 66.9 reduce-scatter.10
  1123.0 152.9 all-reduce.12
  1279.8 118.1 reduce-scatter.20
  1401.9 117.0 reduce-scatter.18
  1522.9 117.4 reduce-scatter.22
where the time goes:
time: 1650 us
  waiting for transfers between devices  1120 us (68%)
  matrix products  203 us (12%)
  blocking collectives  129 us (8%)
  other arithmetic  114 us (7%)
  local copies, waits for them, and re-layouts  43.4 us (3%)
  starting transfers between devices  20.6 us (1%)
  between operations  17.4 us (1%)
    psum x3, waiting for transfers between devices, across_heads(): return lax.psum(values.astype(jnp.bfloat16), 'mp').astype(jnp.float32)  300 us
    reduce_scatter x1, waiting for transfers between devices, on_device(): lax.psum_scatter(totals[7].astype(jnp.bfloat16), 'dp', scatter_dimension=...  119 us
    reduce_scatter x1, waiting for transfers between devices, on_device(): lax.psum_scatter(totals[5].astype(jnp.bfloat16), 'dp', scatter_dimension=...  118 us
    all_gather x1, waiting for transfers between devices, on_device(): lax.all_gather(gate_weight, 'dp', axis=0, tiled=True)  91.6 us
    all_gather x1, waiting for transfers between devices, on_device(): lax.all_gather(up_weight, 'dp', axis=0, tiled=True)  91.2 us
    all_gather x1, waiting for transfers between devices, on_device(): lax.all_gather(down_weight, 'dp', axis=1, tiled=True)  81.5 us
    reduce_scatter x1, waiting for transfers between devices, on_device(): lax.psum_scatter(totals[6].astype(jnp.bfloat16), 'dp', scatter_dimension=...  75.9 us
    reduce_scatter x1, waiting for transfers between devices, on_device(): lax.psum_scatter(totals[4].astype(jnp.bfloat16), 'dp', scatter_dimension=...  69.4 us
  transfers between devices with their start and end apart: 34, of which 23 were waited for; matrix products, arithmetic and copies ran while one was open for 15% of the time, Pallas kernels for 0%

commit v1 on v0

v1 whole, which is shorter than its diff:
```python
import jax
import jax.numpy as jnp
from jax import lax
from jax.sharding import PartitionSpec as P

MICRO_BATCHES = 2
GROUP_DEVICES = 4

eps = 1e-06
rope_base = 1000000.0
masked = -1e30
f32 = jnp.float32
bf16 = jnp.bfloat16


def product(left_side, right_side):
    return jnp.dot(left_side, right_side, preferred_element_type=f32)


def by_transpose(left_side, right_side):
    return lax.dot_general(
        left_side, right_side, (((1,), (1,)), ((), ())), preferred_element_type=f32
    )


def transpose_by(left_side, right_side):
    return lax.dot_general(
        left_side, right_side, (((0,), (0,)), ((), ())), preferred_element_type=f32
    )


def recip_rms(values):
    return lax.rsqrt(jnp.mean(values * values, axis=-1, keepdims=True) + eps)


def rms_back(values, reciprocal, gain, gradient):
    scaled = gain * gradient
    cubed = reciprocal * reciprocal * reciprocal
    back = reciprocal * scaled - values * cubed * jnp.mean(scaled * values, axis=-1, keepdims=True)
    return (back, gradient * values * reciprocal)


def apply_rotary(values, cosine_rows, sine_table):
    half_dim = values.shape[-1] // 2
    leading = values[..., :half_dim]
    trailing = values[..., half_dim:]
    return jnp.concatenate(
        [
            leading * cosine_rows - trailing * sine_table,
            trailing * cosine_rows + leading * sine_table,
        ],
        axis=-1,
    )


def layout(lengths, relative, row_count):
    seg_ends = jnp.cumsum(lengths, dtype=jnp.int32)
    starts = seg_ends - lengths
    row_ids = jnp.arange(row_count, dtype=jnp.int32)
    seg_index = jnp.sum(
        (row_ids[:, None] >= seg_ends[None, :]).astype(jnp.int32), axis=1, dtype=jnp.int32
    )
    seg_onehot = seg_index[:, None] == jnp.arange(lengths.shape[0], dtype=jnp.int32)[None, :]
    seg_start = jnp.sum(jnp.where(seg_onehot, starts[None, :], 0), axis=1, dtype=jnp.int32)
    prompt = relative == 0
    segment = jnp.where(prompt, 0, 1 + seg_index)
    position = jnp.where(prompt, row_ids, row_count + row_ids - seg_start)
    return (segment, position)


def ring_order(count):
    return list(range(0, count, 2)) + list(range(count - 1, 0, -2))


def ring_step(block, count, forward):
    order = ring_order(count)
    turn = 1 if forward else -1
    route = [(order[i], order[(i + turn) % count]) for i in range(count)]
    return lax.ppermute(block, "dp", route)


def after(block, *earlier):
    return lax.optimization_barrier((block,) + earlier)[0]


def ring_gather(block, count, far_forward, gate=None):
    half = count // 2
    ahead, behind = [block], [block]
    if gate is not None:
        ahead[0] = behind[0] = after(block, gate)
    for step in range(1, half + 1):
        if step < half or far_forward:
            ahead.append(ring_step(ahead[-1], count, True))
        if step < half or not far_forward:
            behind.append(ring_step(behind[-1], count, False))
    slots = [ahead[step] for step in range(half - 1, -1, -1)]
    slots += [behind[step] for step in range(1, half)]
    slots.append(ahead[half] if far_forward else behind[half])
    return slots, (ahead, behind)


def ring_scatter(chunk, count, far_forward):
    half = count // 2
    own = half - 1
    ahead = behind = None
    for step in range(half, 0, -1):
        if step < half or far_forward:
            slot = own + step
            part = chunk(slot)
            if ahead is not None:
                part = part + ahead.astype(f32)
            ahead = ring_step(part.astype(bf16), count, True)
        if step < half or not far_forward:
            slot = own - step if step < half else count - 1
            part = chunk(slot)
            if behind is not None:
                part = part + behind.astype(f32)
            behind = ring_step(part.astype(bf16), count, False)
    return chunk(own) + ahead.astype(f32) + behind.astype(f32)


def swap_core(block):
    return lax.ppermute(block, "mp", [(i, i ^ 1) for i in range(lax.axis_size("mp"))])


def swap_x(block):
    return lax.ppermute(block, "mp", [(i, i ^ 2) for i in range(lax.axis_size("mp"))])


def sum_devices(values, levels_mp):
    for level in levels_mp:
        values = values + lax.ppermute(
            values, "mp", [(i, i ^ level) for i in range(lax.axis_size("mp"))]
        )
    count = lax.axis_size("dp")
    level = 1
    while level < count:
        values = values + lax.ppermute(values, "dp", [(i, i ^ level) for i in range(count)])
        level *= 2
    return values


def across(other_part, own_part):
    chip = (own_part + swap_core(other_part.astype(bf16)).astype(f32)).astype(bf16)
    return chip.astype(f32) + swap_x(chip).astype(f32)


def group_route(apart, sources):
    count = lax.axis_size("dp")
    route = []
    for base in range(0, count, GROUP_DEVICES):
        route += [(base + s, base + (s ^ apart)) for s in sources]
    return route


def scores_of(grouped_queries, gathered_keys, allowed, score_scale):
    unscaled_scores = (
        jnp.einsum("mhzk,ihk->hzmi", grouped_queries, gathered_keys, preferred_element_type=f32)
        * score_scale
    )
    return jnp.where(allowed[None, None], unscaled_scores, masked)


def on_device(
    tokens,
    cotangent,
    query_weight,
    key_matrix,
    value_matrix,
    head_gate_weight,
    out_weight,
    gate_weight,
    up_weight,
    down_weight,
    norm_attn,
    norm_mlp,
    norm_query,
    norm_key,
    cont_lengths,
):
    count = lax.axis_size("dp")
    dp_index = lax.axis_index("dp")
    core = lax.axis_index("mp") % 2
    place = jnp.where(dp_index % 2 == 0, dp_index // 2, count - 1 - dp_index // 2)
    offset = dp_index % GROUP_DEVICES
    group_index = dp_index // GROUP_DEVICES
    total_rows, width = tokens.shape
    block_rows = total_rows // MICRO_BATCHES
    own_rows = block_rows // 2
    depth = width // count
    head_dim = norm_query.shape[0]
    head_count = head_gate_weight.shape[1]
    query_cols = query_weight.shape[1]
    key_cols = key_matrix.shape[1]
    kv_heads = key_cols // head_dim
    repeat_heads = head_count // kv_heads
    hidden_units = gate_weight.shape[1]
    score_scale = head_dim ** (-0.5)
    gain_query = norm_query.astype(f32)
    key_gain = norm_key.astype(f32)
    first_place = (place + count - (count // 2 - 1)) % count
    order = ring_order(count)

    extra = 128
    packed = jnp.concatenate(
        [
            query_weight,
            key_matrix,
            value_matrix,
            head_gate_weight,
            norm_attn[:, None],
            norm_mlp[:, None],
            jnp.zeros((depth, extra - head_count - 2), bf16),
        ],
        axis=1,
    )
    in_slots, in_steps = ring_gather(packed, count, False)
    out_slots, out_steps = ring_gather(out_weight, count, False, in_steps[0][1])
    gate_slots, gate_steps = ring_gather(gate_weight, count, True, in_steps[0][2])
    up_slots, up_steps = ring_gather(up_weight, count, False, in_steps[0][3])
    down_slots, _ = ring_gather(down_weight, count, True, gate_steps[0][2])
    in_full = jnp.concatenate(in_slots, axis=0)
    out_full = jnp.concatenate(out_slots, axis=1)
    gate_up_full = jnp.concatenate(
        [jnp.concatenate([g, u], axis=1) for g, u in zip(gate_slots, up_slots)], axis=0
    )
    down_full = jnp.concatenate(down_slots, axis=1)
    first_gain = query_cols + 2 * key_cols + head_count
    gain_attn = in_full[:, first_gain].astype(f32)[None, :]
    gain_mlp = in_full[:, first_gain + 1].astype(f32)[None, :]

    def columns_in(block):
        ring = [block[:, i * depth : (i + 1) * depth] for i in order]
        return lax.dynamic_slice_in_dim(
            jnp.concatenate(ring + ring, axis=1), first_place * depth, width, axis=1
        )

    def columns_out(block):
        twice = jnp.concatenate([block, block], axis=1)
        back = lax.dynamic_slice_in_dim(
            twice, ((count - first_place) % count) * depth, width, axis=1
        )
        where_of = {device: i for i, device in enumerate(order)}
        return jnp.concatenate(
            [back[:, where_of[i] * depth : (where_of[i] + 1) * depth] for i in range(count)],
            axis=1,
        )

    def rows_in(block):
        halves = block.reshape((MICRO_BATCHES, 2, own_rows) + block.shape[1:])
        swapped = jnp.concatenate([halves[:, 1:], halves[:, :1]], axis=1)
        return jnp.where(core == 0, halves, swapped).reshape(block.shape)

    def rows_out(own, other):
        low = jnp.where(core == 0, own, other)
        high = jnp.where(core == 0, other, own)
        return jnp.stack([low, high], axis=1).reshape(total_rows, width)

    inputs_low = columns_in(rows_in(tokens))
    upstream_low = columns_in(rows_in(cotangent))
    inputs = inputs_low.astype(f32)

    inverse = jnp.power(rope_base, -jnp.arange(head_dim // 2, dtype=f32) * (2.0 / head_dim))
    relatives, segments, positions = [], [], []
    for micro in range(MICRO_BATCHES):
        holder = GROUP_DEVICES - 1 if micro % 2 == 1 else 0
        relative = jnp.bitwise_xor(offset, holder)
        lengths = cont_lengths[group_index, jnp.maximum(relative - 1, 0), micro]
        segment, position = layout(lengths, relative, block_rows)
        relatives.append(relative)
        segments.append(segment)
        positions.append(position)
    segment = rows_in(jnp.concatenate(segments))
    position = rows_in(jnp.concatenate(positions))
    angles = position.astype(f32)[:, None] * inverse[None, :]
    cosine_rows = jnp.cos(angles)[:, None, :]
    sine_table = jnp.sin(angles)[:, None, :]

    recip_one = recip_rms(inputs)
    normed_one = (inputs * recip_one * gain_attn).astype(bf16)
    projected = product(normed_one, in_full)
    query_heads = projected[:, :query_cols].reshape(total_rows, head_count, head_dim)
    key_heads = projected[:, query_cols : query_cols + key_cols].reshape(
        total_rows, kv_heads, head_dim
    )
    values_lower = projected[:, query_cols + key_cols : query_cols + 2 * key_cols].astype(bf16)
    gate_logit = projected[:, query_cols + 2 * key_cols : query_cols + 2 * key_cols + head_count]
    recip_query = recip_rms(query_heads)
    recip_key = recip_rms(key_heads)
    rotated_queries = apply_rotary(
        query_heads * recip_query * gain_query, cosine_rows, sine_table
    ).astype(bf16)
    rotated_keys = (
        apply_rotary(key_heads * recip_key * key_gain, cosine_rows, sine_table)
        .astype(bf16)
        .reshape(total_rows, key_cols)
    )
    own_kv = jnp.concatenate([rotated_keys, values_lower], axis=1)

    first_kv, second_kv = own_kv[:block_rows], own_kv[block_rows:]
    sent = jnp.where(offset == 0, first_kv, second_kv)
    by_one = lax.ppermute(sent, "dp", group_route(1, (0, 3)))
    by_two = lax.ppermute(sent, "dp", group_route(2, (0, 3)))
    by_both = lax.ppermute(by_one, "dp", group_route(2, (1, 2)))
    far_kv = [
        jnp.where(offset == 1, by_one, jnp.where(offset == 2, by_two, by_both)),
        jnp.where(offset == 2, by_one, jnp.where(offset == 1, by_two, by_both)),
    ]

    head_gate = jax.nn.sigmoid(gate_logit)
    attention = []
    for micro in range(MICRO_BATCHES):
        rows = slice(micro * block_rows, (micro + 1) * block_rows)
        seg, pos = segment[rows], position[rows]
        own_mask = (seg[:, None] == seg[None, :]) & (pos[None, :] <= pos[:, None])
        far_mask = jnp.broadcast_to(
            jnp.logical_not(relatives[micro] == 0), (block_rows, block_rows)
        )
        allowed = jnp.concatenate([far_mask, own_mask], axis=1)
        all_kv = jnp.concatenate([far_kv[micro], own_kv[rows]], axis=0)
        gathered_keys = all_kv[:, :key_cols].reshape(2 * block_rows, kv_heads, head_dim)
        gathered_values = all_kv[:, key_cols:].reshape(2 * block_rows, kv_heads, head_dim)
        grouped_queries = rotated_queries[rows].reshape(
            block_rows, kv_heads, repeat_heads, head_dim
        )
        scores = scores_of(grouped_queries, gathered_keys, allowed, score_scale)
        row_peak = jnp.max(scores, axis=-1, keepdims=True)
        exponent = jnp.exp(scores - row_peak)
        row_total = jnp.sum(exponent, axis=-1, keepdims=True)
        probabilities_lower = (exponent / row_total).astype(bf16)
        log_total = row_peak + jnp.log(row_total)
        attended = jnp.einsum(
            "ycxu,uyi->xyci", probabilities_lower, gathered_values, preferred_element_type=f32
        ).reshape(block_rows, head_count, head_dim)
        gated_low = (
            (attended * head_gate[rows][:, :, None])
            .reshape(block_rows, head_count * head_dim)
            .astype(bf16)
        )
        attention.append(
            (allowed, gathered_keys, gathered_values, grouped_queries, log_total, attended, gated_low)
        )

    middles, recips_two, norms_two = [], [], []
    for micro in range(MICRO_BATCHES):
        base = micro * block_rows
        gated_low = attention[micro][6]
        summed = across(
            product(gated_low[own_rows:], out_full), product(gated_low[:own_rows], out_full)
        )
        middle = inputs[base : base + own_rows] + summed
        recip_two = recip_rms(middle)
        own_norm = (middle * recip_two * gain_mlp).astype(bf16)
        middles.append(middle)
        recips_two.append(recip_two)
        norms_two += [own_norm, swap_core(own_norm)]
    normed_two = jnp.concatenate(norms_two, axis=0)
    pre = product(normed_two, gate_up_full)
    gate_pre, up_pre = pre[:, :hidden_units], pre[:, hidden_units:]
    sigmoid_gate = jax.nn.sigmoid(gate_pre)
    swish_gate = gate_pre * sigmoid_gate
    hidden_low = (swish_gate * up_pre).astype(bf16)
    down_grad = ring_scatter(
        lambda slot: transpose_by(hidden_low, upstream_low[:, slot * depth : (slot + 1) * depth]),
        count,
        True,
    )
    hidden_grad = by_transpose(upstream_low, down_full)
    gate_grad = (
        hidden_grad * up_pre * sigmoid_gate * (1.0 + gate_pre * (1.0 - sigmoid_gate))
    ).astype(bf16)
    up_grad = (hidden_grad * swish_gate).astype(bf16)
    gate_up_grad = jnp.concatenate([gate_grad, up_grad], axis=1)
    gate_weight_grad = ring_scatter(
        lambda slot: transpose_by(normed_two[:, slot * depth : (slot + 1) * depth], gate_grad),
        count,
        True,
    )
    up_weight_grad = ring_scatter(
        lambda slot: transpose_by(normed_two[:, slot * depth : (slot + 1) * depth], up_grad),
        count,
        False,
    )
    layer_rows, middle_grads, middle_lows = [], [], []
    mlp_gain_grad = 0.0
    for micro in range(MICRO_BATCHES):
        base = micro * block_rows
        own, other = slice(base, base + own_rows), slice(base + own_rows, base + block_rows)
        summed = across(
            by_transpose(gate_up_grad[other], gate_up_full),
            by_transpose(gate_up_grad[own], gate_up_full),
        )
        middle_back, gain_terms = rms_back(middles[micro], recips_two[micro], gain_mlp, summed)
        mlp_gain_grad = mlp_gain_grad + jnp.sum(gain_terms, axis=0)
        middle_grad = upstream_low[own].astype(f32) + middle_back
        middle_grads.append(middle_grad)
        own_low = middle_grad.astype(bf16)
        middle_lows += [own_low, swap_core(own_low)]
    middle_low = jnp.concatenate(middle_lows, axis=0)
    for micro in range(MICRO_BATCHES):
        base = micro * block_rows
        own, other = slice(base, base + own_rows), slice(base + own_rows, base + block_rows)
        mlp_out = across(product(hidden_low[other], down_full), product(hidden_low[own], down_full))
        layer_rows.append(columns_out((middles[micro] + mlp_out).astype(bf16)))
    layer_own = jnp.stack(layer_rows)
    layer_out = rows_out(layer_own, swap_core(layer_own))

    gated_all = jnp.concatenate([a[6] for a in attention], axis=0)
    out_weight_grad = ring_scatter(
        lambda slot: transpose_by(gated_all, middle_low[:, slot * depth : (slot + 1) * depth]),
        count,
        False,
    )
    logit_grads, query_rot_grads, key_grads, value_grads = [], [], [], []
    for micro in range(MICRO_BATCHES):
        rows = slice(micro * block_rows, (micro + 1) * block_rows)
        (allowed, gathered_keys, gathered_values, grouped_queries, log_total, attended, _) = (
            attention[micro]
        )
        gate = head_gate[rows]
        gated_grad = by_transpose(middle_low[rows], out_full).reshape(
            block_rows, head_count, head_dim
        )
        attended_low = (gated_grad * gate[:, :, None]).astype(bf16)
        logit_grads.append(
            (jnp.sum(gated_grad * attended, axis=-1) * gate * (1.0 - gate)).astype(bf16)
        )
        again = scores_of(grouped_queries, gathered_keys, allowed, score_scale)
        probs_again = jnp.exp(again - log_total)
        group_gradient = attended_low.reshape(block_rows, kv_heads, repeat_heads, head_dim)
        prob_grad = jnp.einsum(
            "mhzk,ihk->hzmi", group_gradient, gathered_values, preferred_element_type=f32
        )
        scores_gradient = (
            probs_again * (prob_grad - jnp.sum(probs_again * prob_grad, axis=-1, keepdims=True))
        ).astype(bf16)
        query_rot_grads.append(
            jnp.einsum(
                "ycxu,uyi->xyci", scores_gradient, gathered_keys, preferred_element_type=f32
            ).reshape(block_rows, head_count, head_dim)
            * score_scale
        )
        key_grads.append(
            jnp.einsum(
                "jcuk,ujca->kja", scores_gradient, grouped_queries, preferred_element_type=f32
            ).reshape(2 * block_rows, key_cols)
            * score_scale
        )
        value_grads.append(
            jnp.einsum(
                "jcuk,ujca->kja",
                probs_again.astype(bf16),
                group_gradient,
                preferred_element_type=f32,
            ).reshape(2 * block_rows, key_cols)
        )
    far_grads = [
        jnp.concatenate([k[:block_rows], v[:block_rows]], axis=1)
        for k, v in zip(key_grads, value_grads)
    ]
    by_both = lax.ppermute(
        jnp.where(offset == 3, far_grads[0], far_grads[1]).astype(bf16),
        "dp",
        group_route(2, (0, 3)),
    ).astype(f32)
    by_two = lax.ppermute(
        jnp.where(offset == 2, far_grads[0], far_grads[1]).astype(bf16),
        "dp",
        group_route(2, (1, 2)),
    ).astype(f32)
    by_one = lax.ppermute(
        (jnp.where(offset == 1, far_grads[0], far_grads[1]) + by_both).astype(bf16),
        "dp",
        group_route(1, (1, 2)),
    ).astype(f32)
    arrived = by_one + by_two
    key_rot_grads, value_lows = [], []
    for micro in range(MICRO_BATCHES):
        prompt = relatives[micro] == 0
        back = jnp.where(prompt, arrived, 0.0)
        key_rot_grads.append(key_grads[micro][block_rows:] + back[:, :key_cols])
        value_lows.append((value_grads[micro][block_rows:] + back[:, key_cols:]).astype(bf16))
    query_grad, query_gain_terms = rms_back(
        query_heads,
        recip_query,
        gain_query,
        apply_rotary(jnp.concatenate(query_rot_grads, axis=0), cosine_rows, -sine_table),
    )
    key_grad, key_gain_terms = rms_back(
        key_heads,
        recip_key,
        key_gain,
        apply_rotary(
            jnp.concatenate(key_rot_grads, axis=0).reshape(total_rows, kv_heads, head_dim),
            cosine_rows,
            -sine_table,
        ),
    )
    head_gains = jnp.stack(
        [jnp.sum(query_gain_terms, axis=(0, 1)), jnp.sum(key_gain_terms, axis=(0, 1))]
    )
    head_gains = sum_devices(head_gains, (1, 2))
    in_grad = jnp.concatenate(
        [
            query_grad.reshape(total_rows, query_cols).astype(bf16),
            key_grad.reshape(total_rows, key_cols).astype(bf16),
            jnp.concatenate(value_lows, axis=0),
            jnp.concatenate(logit_grads, axis=0),
            jnp.zeros((total_rows, extra - head_count), bf16),
        ],
        axis=1,
    )
    in_weight_grad = ring_scatter(
        lambda slot: transpose_by(normed_one[:, slot * depth : (slot + 1) * depth], in_grad),
        count,
        False,
    )
    attn_gain_grad = 0.0
    input_rows = []
    for micro in range(MICRO_BATCHES):
        base = micro * block_rows
        own, other = slice(base, base + own_rows), slice(base + own_rows, base + block_rows)
        summed = across(
            by_transpose(in_grad[other], in_full), by_transpose(in_grad[own], in_full)
        )
        input_back, gain_terms = rms_back(inputs[own], recip_one[own], gain_attn, summed)
        attn_gain_grad = attn_gain_grad + jnp.sum(gain_terms, axis=0)
        input_rows.append(columns_out(middle_grads[micro] + input_back))
    input_own = jnp.stack(input_rows)
    tokens_grad = rows_out(input_own, swap_core(input_own))
    gains = columns_out(jnp.stack([attn_gain_grad, mlp_gain_grad]))
    gains = sum_devices(gains, (1,))
    gains = lax.dynamic_slice_in_dim(gains, dp_index * depth, depth, axis=1)
    return (
        layer_out,
        tokens_grad,
        in_weight_grad[:, :query_cols],
        in_weight_grad[:, query_cols : query_cols + key_cols],
        in_weight_grad[:, query_cols + key_cols : query_cols + 2 * key_cols],
        in_weight_grad[:, query_cols + 2 * key_cols : query_cols + 2 * key_cols + head_count],
        out_weight_grad,
        gate_weight_grad,
        up_weight_grad,
        down_grad,
        gains[0],
        gains[1],
        head_gains[0],
        head_gains[1],
    )


def solution(mesh):
    rows, weight, turned = P("dp", None), P("dp", "mp"), P("mp", "dp")
    weights = (weight, weight, weight, weight, turned, weight, weight, turned)
    placed = (rows, rows) + weights + (P("dp"), P("dp"), P(), P())
    return jax.shard_map(
        on_device, mesh=mesh, in_specs=placed + (P(),), out_specs=placed, check_vma=False
    )
```

time: 1650 us -> 951 us (0.58)
  waiting for transfers between devices: 1120 us -> 352 us
  blocking collectives: 129 us -> 0 us
  starting transfers between devices: 20.6 us -> 113 us
  local copies, waits for them, and re-layouts: 43.4 us -> 126 us
  other arithmetic: 114 us -> 133 us
    reduce_scatter x7 -> x0, waiting for transfers between devices: 474 us -> none  [the longest x1 119 us: on_device(): lax.psum_scatter(totals[7].astype(jnp.bfloat16), 'dp', scatter_dimension=...]
    ppermute x16 -> x107, waiting for transfers between devices: 46.7 us -> 352 us  [the longest x70 213 us: ring_step(): return lax.ppermute(block, 'dp', route)]
    psum x3 -> x0, waiting for transfers between devices: 300 us -> none  [across_heads(): return lax.psum(values.astype(jnp.bfloat16), 'mp').astype(jnp.float32)]
    all_gather x7 -> x0, waiting for transfers between devices: 296 us -> none  [the longest x1 91.6 us: on_device(): lax.all_gather(gate_weight, 'dp', axis=0, tiled=True)]
    ppermute x16 -> x107, starting transfers between devices: 18.9 us -> 113 us  [the longest x70 78.9 us: ring_step(): return lax.ppermute(block, 'dp', route)]
    all_gather x3 -> x0, blocking collectives: 66 us -> none  [the longest x1 26 us: on_device(): lax.all_gather(head_gate_weight, 'dp', axis=0, tiled=True)]
    psum x1 -> x0, blocking collectives: 40.5 us -> none  [on_device(): head_grads = lax.psum((head_totals[0], head_totals[1]), ('dp', 'mp'))]
    slice x4 -> x28, local copies, waits for them, and re-layouts: 3.08 us -> 31.5 us  [the longest x4 6.26 us: on_device(): value_grads[micro][block_rows:] + back[:, key_cols:]]
  transfers between devices with their start and end apart: 34 -> 107, of which waited for: 23 -> 42; matrix products, arithmetic and copies ran while one was open for 15% -> 38% of each run, Pallas kernels for 0% -> 0%
where the time goes in v1:
time: 951 us; the launch traced here: 940 us
  waiting for transfers between devices  352 us (37%)
  matrix products  212 us (22%)
  other arithmetic  133 us (14%)
  local copies, waits for them, and re-layouts  126 us (13%)
  starting transfers between devices  113 us (12%)
    ppermute x70, waiting for transfers between devices, ring_step(): return lax.ppermute(block, 'dp', route)  213 us
    ppermute x8, waiting for transfers between devices, swap_x(): lax.ppermute(block, 'mp', [(i, i ^ 2) for i in range(lax.axis_size('mp'))])  111 us
    ppermute x70, starting transfers between devices, ring_step(): return lax.ppermute(block, 'dp', route)  78.9 us
    dot_general x40, matrix products, transpose_by(): lax.dot_general(left_side, right_side, (((0,), (0,)), ((), ())), preferre...  70.9 us
    dot_general x11, matrix products, by_transpose(): lax.dot_general(left_side, right_side, (((1,), (1,)), ((), ())), preferre...  67.1 us
    dot_general x10, matrix products, product(): return jnp.dot(left_side, right_side, preferred_element_type=f32)  47.6 us
    unnamed x385, local copies, waits for them, and re-layouts  38.1 us
  transfers between devices with their start and end apart: 107, of which 42 were waited for; matrix products, arithmetic and copies ran while one was open for 38% of the time, Pallas kernels for 0%

profile of v1, /device:TPU:0, one launch (start us, length us, event | category | flops | bytes accessed | tf_op | source)
XLA Modules:
  0.0 939.5 jit_solution(2062212127857434510)
XLA Ops:
  4.2 3.1 collective-permute-start
  39.3 6.6 dynamic-slice_convert_fusion
  52.5 3.2 collective-permute-done.10
  61.5 11.1 %collective-permute-done.11 = bf16[512,256]{1,0:T(8,128)(2,1)S(1)} collective-permute-done((bf16[512,256]{1,0:T(8,128)(2,1)S(1)}, bf16[512,256]{1,0:T(8,128)(2,1)S(1)}, u32[]{:S(2)}, u32[]{:S(2)}) %collective-permute-start.11) | collective-permute-done | bytes 262176 | tf_op jit(solution)/shard_map/ppermute | solution.py:79
  74.3 3.1 fusion.188
  88.0 30.9 %collective-permute-done.16 = bf16[512,256]{1,0:T(8,128)(2,1)S(1)} collective-permute-done((bf16[512,256]{1,0:T(8,128)(2,1)S(1)}, bf16[512,256]{1,0:T(8,128)(2,1)S(1)}, u32[]{:S(2)}, u32[]{:S(2)}) %collective-permute-start.16) | collective-permute-done | bytes 262176 | tf_op jit(solution)/shard_map/ppermute | solution.py:79
  126.2 23.7 %collective-permute-done.6 = bf16[256,1152]{1,0:T(8,128)(2,1)S(1)} collective-permute-done((bf16[256,1152]{1,0:T(8,128)(2,1)S(1)}, bf16[256,1152]{1,0:T(8,128)(2,1)S(1)}, u32[]{:S(2)}, u32[]{:S(2)}) %collective-permute-start.6) | collective-permute-done | bytes 589856 | tf_op jit(solution)/shard_map/ppermute | solution.py:79
  150.6 4.2 multiply_convert_fusion
  154.8 5.6 fusion.233
  170.7 3.1 multiply_multiply_fusion.1
  179.4 3.2 collective-permute-start.7
  204.8 4.2 collective-permute-start.31
  251.0 16.4 %collective-permute-done.25 = bf16[256,1536]{1,0:T(8,128)(2,1)S(1)} collective-permute-done((bf16[256,1536]{1,0:T(8,128)(2,1)}, bf16[256,1536]{1,0:T(8,128)(2,1)S(1)}, u32[]{:S(2)}, u32[]{:S(2)}) %collective-permute-start.25) | collective-permute-done | bytes 786464 | tf_op jit(solution)/shard_map/ppermute | solution.py:79
  269.6 14.5 %collective-permute-done.28 = bf16[256,1536]{1,0:T(8,128)(2,1)S(1)} collective-permute-done((bf16[256,1536]{1,0:T(8,128)(2,1)}, bf16[256,1536]{1,0:T(8,128)(2,1)S(1)}, u32[]{:S(2)}, u32[]{:S(2)}) %collective-permute-start.28) | collective-permute-done | bytes 786464 | tf_op jit(solution)/shard_map/ppermute | solution.py:79
  297.3 14.3 %collective-permute-done.41 = bf16[1536,256]{1,0:T(8,128)(2,1)S(1)} collective-permute-done((bf16[1536,256]{1,0:T(8,128)(2,1)}, bf16[1536,256]{1,0:T(8,128)(2,1)S(1)}, u32[]{:S(2)}, u32[]{:S(2)}) %collective-permute-start.41) | collective-permute-done | bytes 786464 | tf_op jit(solution)/shard_map/ppermute | solution.py:79
  318.0 10.4 %collective-permute-done.36 = bf16[256,1536]{1,0:T(8,128)(2,1)S(1)} collective-permute-done((bf16[256,1536]{1,0:T(8,128)(2,1)S(1)}, bf16[256,1536]{1,0:T(8,128)(2,1)S(1)}, u32[]{:S(2)}, u32[]{:S(2)}) %collective-permute-start.36) | collective-permute-done | bytes 786464 | tf_op jit(solution)/shard_map/ppermute | solution.py:79
  332.9 8.4 collective-permute-done.21
  341.2 15.0 %collective-permute-done.18 = bf16[256,2048]{1,0:T(8,128)(2,1)S(1)} collective-permute-done((bf16[256,2048]{1,0:T(8,128)(2,1)S(1)}, bf16[256,2048]{1,0:T(8,128)(2,1)S(1)}, u32[]{:S(2)}, u32[]{:S(2)}) %collective-permute-start.18) | collective-permute-done | bytes 1048608 | tf_op jit(solution)/shard_map/ppermute | solution.py:127
  364.4 17.8 %fusion.215 = f32[1024,3072]{1,0:T(8,128)} fusion(bf16[2048,3072]{1,0:T(8,128)(2,1)} %maximum_dynamic-update-slice_fusion, bf16[256,2048]{1,0:T(8,128)(2,1)S(1)} %collective-permute-done.22, bf16[256,2048]{1,0:T(8,128)(2,1)S(1)} %get-tuple-element.203, bf16[256,2048]{1,0:T(8,128)(2,1)S(1)} %collective-permute-done.19, ...), kind=kOutput, calls=%fused_computation.553 | convolution fusion | flops 12901679104 | bytes 29360128 | tf_op jit(solution)/shard_map/dot_general | solution.py:17
  382.2 16.8 %multiply_convert_fusion.2 = (bf16[1024,1536]{1,0:T(8,128)(2,1)S(1)}, bf16[1024,1536]{1,0:T(8,128)(2,1)}, bf16[1024,1536]{1,0:T(8,128)(2,1)}) fusion(f32[1024,3072]{1,0:T(8,128)} %fusion.215, bf16[1536,2048]{1,0:T(8,128)(2,1)} %copy-done.108, bf16[1024,4096]{1,0:T(8,128)(2,1)} %slice_dynamic-update-slice_fusion.7, s32[]{:T(128)S(6)} %select_n.258), kind=kOutput, calls=%fused_computation.32 | convolution fusion | flops 6466043904 | bytes 32505860 | tf_op jit(solution)/shard_map/dot_general | solution.py:21
  399.0 7.0 convolution_convert_fusion.12
  406.0 3.9 convolution_convert_fusion.13
  409.9 8.4 convolution_convert_fusion.14
  418.4 9.3 convolution_convert_fusion.15
  427.7 3.2 convolution_convert_fusion.4
  433.0 3.5 fusion.120
  436.5 3.2 fusion.122
  439.7 3.2 fusion.124
  442.9 3.4 fusion.113
  455.3 14.3 %collective-permute-done.84 = bf16[256,1536]{1,0:T(8,128)(2,1)S(1)} collective-permute-done((bf16[256,1536]{1,0:T(8,128)(2,1)S(1)}, bf16[256,1536]{1,0:T(8,128)(2,1)S(1)}, u32[]{:S(2)}, u32[]{:S(2)}) %collective-permute-start.84) | collective-permute-done | bytes 786464 | tf_op jit(solution)/shard_map/ppermute | solution.py:79
  475.5 11.0 %collective-permute-done.77 = bf16[256,1536]{1,0:T(8,128)(2,1)S(1)} collective-permute-done((bf16[256,1536]{1,0:T(8,128)(2,1)S(1)}, bf16[256,1536]{1,0:T(8,128)(2,1)S(1)}, u32[]{:S(2)}, u32[]{:S(2)}) %collective-permute-start.77) | collective-permute-done | bytes 786464 | tf_op jit(solution)/shard_map/ppermute | solution.py:79
  491.5 10.9 %collective-permute-done.91 = bf16[1536,256]{1,0:T(8,128)(2,1)S(1)} collective-permute-done((bf16[1536,256]{1,0:T(8,128)(2,1)S(1)}, bf16[1536,256]{1,0:T(8,128)(2,1)S(1)}, u32[]{:S(2)}, u32[]{:S(2)}) %collective-permute-start.91) | collective-permute-done | bytes 786464 | tf_op jit(solution)/shard_map/ppermute | solution.py:79
  510.5 8.5 fusion.24
  519.5 8.7 fusion.23
  530.0 5.1 fusion.40
  535.5 5.3 fusion.39
  551.5 7.9 collective-permute-done.78
  573.5 24.0 %collective-permute-done.53 = bf16[256,2048]{1,0:T(8,128)(2,1)S(1)} collective-permute-done((bf16[256,2048]{1,0:T(8,128)(2,1)S(1)}, bf16[256,2048]{1,0:T(8,128)(2,1)S(1)}, u32[]{:S(2)}, u32[]{:S(2)}) %collective-permute-start.53) | collective-permute-done | bytes 1048608 | tf_op jit(solution)/shard_map/ppermute | solution.py:127
  599.2 20.8 %collective-permute-done.45 = bf16[256,2048]{1,0:T(8,128)(2,1)S(1)} collective-permute-done((bf16[256,2048]{1,0:T(8,128)(2,1)S(1)}, bf16[256,2048]{1,0:T(8,128)(2,1)S(1)}, u32[]{:S(2)}, u32[]{:S(2)}) %collective-permute-start.45) | collective-permute-done | bytes 1048608 | tf_op jit(solution)/shard_map/ppermute | solution.py:127
  621.4 17.9 %collective-permute-done.50 = bf16[256,2048]{1,0:T(8,128)(2,1)S(1)} collective-permute-done((bf16[256,2048]{1,0:T(8,128)(2,1)S(1)}, bf16[256,2048]{1,0:T(8,128)(2,1)S(1)}, u32[]{:S(2)}, u32[]{:S(2)}) %collective-permute-start.50) | collective-permute-done | bytes 1048608 | tf_op jit(solution)/shard_map/ppermute | solution.py:127
  644.2 4.9 fusion.216
  651.6 3.9 collective-permute-done.89
  674.2 4.2 fusion
  686.8 4.7 fusion.2
  695.2 6.6 pad_maximum_fusion.6
  713.1 7.4 multiply_subtract_fusion
  745.7 3.7 collective-permute-start.55
  754.3 3.7 fusion.22
  761.7 5.5 collective-permute-done.70
  772.1 4.4 collective-permute-done.74
  778.7 5.4 collective-permute-done.80
  786.9 3.5 fusion.21
  810.8 3.9 concatenate.226
  814.7 4.0 convolution_convert_fusion.10
  818.8 4.0 convolution_convert_fusion.11
  836.7 5.8 collective-permute-done.104
  842.9 3.2 collective-permute-done.105
  851.2 6.0 collective-permute-done.61
  859.1 19.1 %collective-permute-done.59 = bf16[256,2048]{1,0:T(8,128)(2,1)S(1)} collective-permute-done((bf16[256,2048]{1,0:T(8,128)(2,1)S(1)}, bf16[256,2048]{1,0:T(8,128)(2,1)S(1)}, u32[]{:S(2)}, u32[]{:S(2)}) %collective-permute-start.59) | collective-permute-done | bytes 1048608 | tf_op jit(solution)/shard_map/ppermute | solution.py:127
  889.9 3.1 collective-permute-done.98
  894.7 7.8 collective-permute-done.68
  913.7 7.2 collective-permute-done.100
  929.6 4.4 select_bitcast_fusion.1
  935.1 4.0 copy.301
  (818 shorter events, 409.7 us)
Async XLA Ops:
  4.2 42.3 %collective-permute-start = (bf16[256,1152]{1,0:T(8,128)(2,1)S(1)}, bf16[256,1152]{1,0:T(8,128)(2,1)S(1)}, u32[]{:S(2)}, u32[]{:S(2)}) collective-permute-start(bf16[256,1152]{1,0:T(8,128)(2,1)S(1)} %concatenate.181), channel_id=1, source_target_pairs={{0,8},{8,16},{16,24},{24,28},{28,20},{20,12},{12,4},{4,0},{1,9},{9... | collective-permute-start | bytes 1769480 | tf_op jit(solution)/shard_map/ppermute | solution.py:79
  7.3 44.0 %collective-permute-start.3 = (bf16[256,1152]{1,0:T(8,128)(2,1)S(1)}, bf16[256,1152]{1,0:T(8,128)(2,1)S(1)}, u32[]{:S(2)}, u32[]{:S(2)}) collective-permute-start(bf16[256,1152]{1,0:T(8,128)(2,1)S(1)} %concatenate.181), channel_id=1, source_target_pairs={{0,4},{8,0},{16,8},{24,16},{28,24},{20,28},{12,20},{4,12},{1,5},{9... | collective-permute-start | bytes 1769480 | tf_op jit(solution)/shard_map/ppermute | solution.py:79
  49.3 28.4 %collective-permute-start.1 = (bf16[256,1152]{1,0:T(8,128)(2,1)S(1)}, bf16[256,1152]{1,0:T(8,128)(2,1)}, u32[]{:S(2)}, u32[]{:S(2)}) collective-permute-start(bf16[256,1152]{1,0:T(8,128)(2,1)S(1)} %collective-permute-done), channel_id=1, source_target_pairs={{0,8},{8,16},{16,24},{24,28},{28,20},{20,12},{12,4},{4,0},{1,9},{9... | collective-permute-start | bytes 1769480 | tf_op jit(solution)/shard_map/ppermute | solution.py:79
  52.4 27.3 %collective-permute-start.4 = (bf16[256,1152]{1,0:T(8,128)(2,1)S(1)}, bf16[256,1152]{1,0:T(8,128)(2,1)}, u32[]{:S(2)}, u32[]{:S(2)}) collective-permute-start(bf16[256,1152]{1,0:T(8,128)(2,1)S(1)} %collective-permute-done.3), channel_id=1, source_target_pairs={{0,4},{8,0},{16,8},{24,16},{28,24},{20,28},{12,20},{4,12},{1,5},{9... | collective-permute-start | bytes 1769480 | tf_op jit(solution)/shard_map/ppermute | solution.py:79
  77.7 46.6 %collective-permute-start.23 = (bf16[256,1536]{1,0:T(8,128)(2,1)}, bf16[256,1536]{1,0:T(8,128)(2,1)}, u32[]{:S(2)}, u32[]{:S(2)}) collective-permute-start(bf16[256,1536]{1,0:T(8,128)(2,1)} %param.22), channel_id=1, source_target_pairs={{0,8},{8,16},{16,24},{24,28},{28,20},{20,12},{12,4},{4,0},{1,9},{9... | collective-permute-start | bytes 2359304 | tf_op jit(solution)/shard_map/ppermute | solution.py:79
  79.4 113.7 %collective-permute-start.29 = (bf16[256,1536]{1,0:T(8,128)(2,1)}, bf16[256,1536]{1,0:T(8,128)(2,1)}, u32[]{:S(2)}, u32[]{:S(2)}) collective-permute-start(bf16[256,1536]{1,0:T(8,128)(2,1)} %param.22), channel_id=1, source_target_pairs={{0,4},{8,0},{16,8},{24,16},{28,24},{20,28},{12,20},{4,12},{1,5},{9... | collective-permute-start | bytes 2359304 | tf_op jit(solution)/shard_map/ppermute | solution.py:79
  79.7 39.2 %collective-permute-start.2 = (bf16[256,1152]{1,0:T(8,128)(2,1)}, bf16[256,1152]{1,0:T(8,128)(2,1)S(1)}, u32[]{:S(2)}, u32[]{:S(2)}) collective-permute-start(bf16[256,1152]{1,0:T(8,128)(2,1)} %collective-permute-done.1), channel_id=1, source_target_pairs={{0,8},{8,16},{16,24},{24,28},{28,20},{20,12},{12,4},{4,0},{1,9},{9... | collective-permute-start | bytes 1769480 | tf_op jit(solution)/shard_map/ppermute | solution.py:79
  81.5 40.9 %collective-permute-start.5 = (bf16[256,1152]{1,0:T(8,128)(2,1)}, bf16[256,1152]{1,0:T(8,128)(2,1)S(1)}, u32[]{:S(2)}, u32[]{:S(2)}) collective-permute-start(bf16[256,1152]{1,0:T(8,128)(2,1)} %collective-permute-done.4), channel_id=1, source_target_pairs={{0,4},{8,0},{16,8},{24,16},{28,24},{20,28},{12,20},{4,12},{1,5},{9... | collective-permute-start | bytes 1769480 | tf_op jit(solution)/shard_map/ppermute | solution.py:79
  86.7 32.3 %collective-permute-start.16 = (bf16[512,256]{1,0:T(8,128)(2,1)S(1)}, bf16[512,256]{1,0:T(8,128)(2,1)S(1)}, u32[]{:S(2)}, u32[]{:S(2)}) collective-permute-start(bf16[512,256]{1,0:T(8,128)(2,1)S(1)} %collective-permute-done.15), channel_id=1, source_target_pairs={{0,4},{8,0},{16,8},{24,16},{28,24},{20,28},{12,20},{4,12},{1,5},{9... | collective-permute-start | bytes 786440 | tf_op jit(solution)/shard_map/ppermute | solution.py:79
  119.0 85.8 %collective-permute-start.26 = (bf16[256,1536]{1,0:T(8,128)(2,1)}, bf16[256,1536]{1,0:T(8,128)(2,1)}, u32[]{:S(2)}, u32[]{:S(2)}) collective-permute-start(bf16[256,1536]{1,0:T(8,128)(2,1)} %param.23), channel_id=1, source_target_pairs={{0,8},{8,16},{16,24},{24,28},{28,20},{20,12},{12,4},{4,0},{1,9},{9... | collective-permute-start | bytes 2359304 | tf_op jit(solution)/shard_map/ppermute | solution.py:79
  120.6 88.4 %collective-permute-start.30 = (bf16[256,1536]{1,0:T(8,128)(2,1)}, bf16[256,1536]{1,0:T(8,128)(2,1)}, u32[]{:S(2)}, u32[]{:S(2)}) collective-permute-start(bf16[256,1536]{1,0:T(8,128)(2,1)} %param.23), channel_id=1, source_target_pairs={{0,4},{8,0},{16,8},{24,16},{28,24},{20,28},{12,20},{4,12},{1,5},{9... | collective-permute-start | bytes 2359304 | tf_op jit(solution)/shard_map/ppermute | solution.py:79
  122.4 27.5 %collective-permute-start.6 = (bf16[256,1152]{1,0:T(8,128)(2,1)S(1)}, bf16[256,1152]{1,0:T(8,128)(2,1)S(1)}, u32[]{:S(2)}, u32[]{:S(2)}) collective-permute-start(bf16[256,1152]{1,0:T(8,128)(2,1)S(1)} %collective-permute-done.5), channel_id=1, source_target_pairs={{0,4},{8,0},{16,8},{24,16},{28,24},{20,28},{12,20},{4,12},{1,5},{9... | collective-permute-start | bytes 1769480 | tf_op jit(solution)/shard_map/ppermute | solution.py:79
  124.3 84.7 %collective-permute-start.24 = (bf16[256,1536]{1,0:T(8,128)(2,1)}, bf16[256,1536]{1,0:T(8,128)(2,1)}, u32[]{:S(2)}, u32[]{:S(2)}) collective-permute-start(bf16[256,1536]{1,0:T(8,128)(2,1)} %collective-permute-done.23), channel_id=1, source_target_pairs={{0,8},{8,16},{16,24},{24,28},{28,20},{20,12},{12,4},{4,0},{1,9},{9... | collective-permute-start | bytes 2359304 | tf_op jit(solution)/shard_map/ppermute | solution.py:79
  204.8 42.0 %collective-permute-start.31 = (bf16[256,1536]{1,0:T(8,128)(2,1)}, bf16[256,1536]{1,0:T(8,128)(2,1)}, u32[]{:S(2)}, u32[]{:S(2)}) collective-permute-start(bf16[256,1536]{1,0:T(8,128)(2,1)} %collective-permute-done.29), channel_id=1, source_target_pairs={{0,4},{8,0},{16,8},{24,16},{28,24},{20,28},{12,20},{4,12},{1,5},{9... | collective-permute-start | bytes 2359304 | tf_op jit(solution)/shard_map/ppermute | solution.py:79
  209.0 37.8 %collective-permute-start.27 = (bf16[256,1536]{1,0:T(8,128)(2,1)}, bf16[256,1536]{1,0:T(8,128)(2,1)}, u32[]{:S(2)}, u32[]{:S(2)}) collective-permute-start(bf16[256,1536]{1,0:T(8,128)(2,1)} %collective-permute-done.26), channel_id=1, source_target_pairs={{0,8},{8,16},{16,24},{24,28},{28,20},{20,12},{12,4},{4,0},{1,9},{9... | collective-permute-start | bytes 2359304 | tf_op jit(solution)/shard_map/ppermute | solution.py:79
  209.0 41.1 %collective-permute-start.32 = (bf16[256,1536]{1,0:T(8,128)(2,1)}, bf16[256,1536]{1,0:T(8,128)(2,1)}, u32[]{:S(2)}, u32[]{:S(2)}) collective-permute-start(bf16[256,1536]{1,0:T(8,128)(2,1)} %collective-permute-done.30), channel_id=1, source_target_pairs={{0,4},{8,0},{16,8},{24,16},{28,24},{20,28},{12,20},{4,12},{1,5},{9... | collective-permute-start | bytes 2359304 | tf_op jit(solution)/shard_map/ppermute | solution.py:79
  211.1 56.5 %collective-permute-start.37 = (bf16[1536,256]{1,0:T(8,128)(2,1)}, bf16[1536,256]{1,0:T(8,128)(2,1)}, u32[]{:S(2)}, u32[]{:S(2)}) collective-permute-start(bf16[1536,256]{1,0:T(8,128)(2,1)} %param.24), channel_id=1, source_target_pairs={{0,8},{8,16},{16,24},{24,28},{28,20},{20,12},{12,4},{4,0},{1,9},{9... | collective-permute-start | bytes 2359304 | tf_op jit(solution)/shard_map/ppermute | solution.py:79
  211.1 56.4 %collective-permute-start.40 = (bf16[1536,256]{1,0:T(8,128)(2,1)}, bf16[1536,256]{1,0:T(8,128)(2,1)}, u32[]{:S(2)}, u32[]{:S(2)}) collective-permute-start(bf16[1536,256]{1,0:T(8,128)(2,1)} %param.24), channel_id=1, source_target_pairs={{0,4},{8,0},{16,8},{24,16},{28,24},{20,28},{12,20},{4,12},{1,5},{9... | collective-permute-start | bytes 2359304 | tf_op jit(solution)/shard_map/ppermute | solution.py:79
  246.9 37.2 %collective-permute-start.28 = (bf16[256,1536]{1,0:T(8,128)(2,1)}, bf16[256,1536]{1,0:T(8,128)(2,1)S(1)}, u32[]{:S(2)}, u32[]{:S(2)}) collective-permute-start(bf16[256,1536]{1,0:T(8,128)(2,1)} %collective-permute-done.27), channel_id=1, source_target_pairs={{0,8},{8,16},{16,24},{24,28},{28,20},{20,12},{12,4},{4,0},{1,9},{9... | collective-permute-start | bytes 2359304 | tf_op jit(solution)/shard_map/ppermute | solution.py:79
  250.1 40.2 %collective-permute-start.33 = (bf16[256,1536]{1,0:T(8,128)(2,1)}, bf16[256,1536]{1,0:T(8,128)(2,1)S(1)}, u32[]{:S(2)}, u32[]{:S(2)}) collective-permute-start(bf16[256,1536]{1,0:T(8,128)(2,1)} %collective-permute-done.31), channel_id=1, source_target_pairs={{0,4},{8,0},{16,8},{24,16},{28,24},{20,28},{12,20},{4,12},{1,5},{9... | collective-permute-start | bytes 2359304 | tf_op jit(solution)/shard_map/ppermute | solution.py:79
  267.5 27.3 %collective-permute-start.34 = (bf16[256,1536]{1,0:T(8,128)(2,1)}, bf16[256,1536]{1,0:T(8,128)(2,1)S(1)}, u32[]{:S(2)}, u32[]{:S(2)}) collective-permute-start(bf16[256,1536]{1,0:T(8,128)(2,1)} %collective-permute-done.32), channel_id=1, source_target_pairs={{0,4},{8,0},{16,8},{24,16},{28,24},{20,28},{12,20},{4,12},{1,5},{9... | collective-permute-start | bytes 2359304 | tf_op jit(solution)/shard_map/ppermute | solution.py:79
  267.5 45.7 %collective-permute-start.20 = (bf16[256,2048]{1,0:T(8,128)(2,1)S(1)}, bf16[256,2048]{1,0:T(8,128)(2,1)S(1)}, u32[]{:S(2)}, u32[]{:S(2)}) collective-permute-start(bf16[256,2048]{1,0:T(8,128)(2,1)S(1)} %convolution_convert_fusion.2), channel_id=1, source_target_pairs={{0,1},{1,0},{2,3},{3,2},{4,5},{5,4},{6,7},{7,6},{8,9},{9,8},{10,11... | collective-permute-start | bytes 3145736 | tf_op jit(solution)/shard_map/ppermute | solution.py:123
  267.5 28.8 %collective-permute-start.38 = (bf16[1536,256]{1,0:T(8,128)(2,1)}, bf16[1536,256]{1,0:T(8,128)(2,1)S(1)}, u32[]{:S(2)}, u32[]{:S(2)}) collective-permute-start(bf16[1536,256]{1,0:T(8,128)(2,1)} %collective-permute-done.37), channel_id=1, source_target_pairs={{0,8},{8,16},{16,24},{24,28},{28,20},{20,12},{12,4},{4,0},{1,9},{9... | collective-permute-start | bytes 2359304 | tf_op jit(solution)/shard_map/ppermute | solution.py:79
  284.1 27.5 %collective-permute-start.41 = (bf16[1536,256]{1,0:T(8,128)(2,1)}, bf16[1536,256]{1,0:T(8,128)(2,1)S(1)}, u32[]{:S(2)}, u32[]{:S(2)}) collective-permute-start(bf16[1536,256]{1,0:T(8,128)(2,1)} %collective-permute-done.40), channel_id=1, source_target_pairs={{0,4},{8,0},{16,8},{24,16},{28,24},{20,28},{12,20},{4,12},{1,5},{9... | collective-permute-start | bytes 2359304 | tf_op jit(solution)/shard_map/ppermute | solution.py:79
  290.3 24.7 %collective-permute-start.17 = (bf16[256,2048]{1,0:T(8,128)(2,1)S(1)}, bf16[256,2048]{1,0:T(8,128)(2,1)S(1)}, u32[]{:S(2)}, u32[]{:S(2)}) collective-permute-start(bf16[256,2048]{1,0:T(8,128)(2,1)S(1)} %convolution_convert_fusion.3), channel_id=1, source_target_pairs={{0,1},{1,0},{2,3},{3,2},{4,5},{5,4},{6,7},{7,6},{8,9},{9,8},{10,11... | collective-permute-start | bytes 3145736 | tf_op jit(solution)/shard_map/ppermute | solution.py:123
  294.8 22.6 %collective-permute-start.35 = (bf16[256,1536]{1,0:T(8,128)(2,1)S(1)}, bf16[256,1536]{1,0:T(8,128)(2,1)S(1)}, u32[]{:S(2)}, u32[]{:S(2)}) collective-permute-start(bf16[256,1536]{1,0:T(8,128)(2,1)S(1)} %collective-permute-done.25), channel_id=1, source_target_pairs={{0,8},{8,16},{16,24},{24,28},{28,20},{20,12},{12,4},{4,0},{1,9},{9... | collective-permute-start | bytes 2359304 | tf_op jit(solution)/shard_map/ppermute | solution.py:79
  296.3 32.0 %collective-permute-start.36 = (bf16[256,1536]{1,0:T(8,128)(2,1)S(1)}, bf16[256,1536]{1,0:T(8,128)(2,1)S(1)}, u32[]{:S(2)}, u32[]{:S(2)}) collective-permute-start(bf16[256,1536]{1,0:T(8,128)(2,1)S(1)} %collective-permute-done.34), channel_id=1, source_target_pairs={{0,4},{8,0},{16,8},{24,16},{28,24},{20,28},{12,20},{4,12},{1,5},{9... | collective-permute-start | bytes 2359304 | tf_op jit(solution)/shard_map/ppermute | solution.py:79
  313.2 47.0 %collective-permute-start.42 = (bf16[1536,256]{1,0:T(8,128)(2,1)S(1)}, bf16[1536,256]{1,0:T(8,128)(2,1)S(1)}, u32[]{:S(2)}, u32[]{:S(2)}) collective-permute-start(bf16[1536,256]{1,0:T(8,128)(2,1)S(1)} %collective-permute-done.41), channel_id=1, source_target_pairs={{0,4},{8,0},{16,8},{24,16},{28,24},{20,28},{12,20},{4,12},{1,5},{9... | collective-permute-start | bytes 2359304 | tf_op jit(solution)/shard_map/ppermute | solution.py:79
  315.0 26.2 %collective-permute-start.21 = (bf16[256,2048]{1,0:T(8,128)(2,1)S(1)}, bf16[256,2048]{1,0:T(8,128)(2,1)S(1)}, u32[]{:S(2)}, u32[]{:S(2)}) collective-permute-start(bf16[256,2048]{1,0:T(8,128)(2,1)S(1)} %fusion.28), channel_id=1, source_target_pairs={{0,2},{1,3},{2,0},{3,1},{4,6},{5,7},{6,4},{7,5},{8,10},{9,11},{10,... | collective-permute-start | bytes 3145736 | tf_op jit(solution)/shard_map/ppermute | solution.py:127
  317.4 38.9 %collective-permute-start.18 = (bf16[256,2048]{1,0:T(8,128)(2,1)S(1)}, bf16[256,2048]{1,0:T(8,128)(2,1)S(1)}, u32[]{:S(2)}, u32[]{:S(2)}) collective-permute-start(bf16[256,2048]{1,0:T(8,128)(2,1)S(1)} %fusion.27), channel_id=1, source_target_pairs={{0,2},{1,3},{2,0},{3,1},{4,6},{5,7},{6,4},{7,5},{8,10},{9,11},{10,... | collective-permute-start | bytes 3145736 | tf_op jit(solution)/shard_map/ppermute | solution.py:127
  329.7 30.6 %collective-permute-start.43 = (bf16[1536,256]{1,0:T(8,128)(2,1)S(1)}, bf16[1536,256]{1,0:T(8,128)(2,1)S(1)}, u32[]{:S(2)}, u32[]{:S(2)}) collective-permute-start(bf16[1536,256]{1,0:T(8,128)(2,1)S(1)} %collective-permute-done.39), channel_id=1, source_target_pairs={{0,8},{8,16},{16,24},{24,28},{28,20},{20,12},{12,4},{4,0},{1,9},{9... | collective-permute-start | bytes 2359304 | tf_op jit(solution)/shard_map/ppermute | solution.py:79
  450.6 22.1 %collective-permute-start.87 = (bf16[256,1536]{1,0:T(8,128)(2,1)S(1)}, bf16[256,1536]{1,0:T(8,128)(2,1)S(1)}, u32[]{:S(2)}, u32[]{:S(2)}) collective-permute-start(bf16[256,1536]{1,0:T(8,128)(2,1)S(1)} %convolution_convert_fusion.6), channel_id=1, source_target_pairs={{0,4},{8,0},{16,8},{24,16},{28,24},{20,28},{12,20},{4,12},{1,5},{9... | collective-permute-start | bytes 2359304 | tf_op jit(solution)/shard_map/ppermute | solution.py:79
  453.4 33.2 %collective-permute-start.77 = (bf16[256,1536]{1,0:T(8,128)(2,1)S(1)}, bf16[256,1536]{1,0:T(8,128)(2,1)S(1)}, u32[]{:S(2)}, u32[]{:S(2)}) collective-permute-start(bf16[256,1536]{1,0:T(8,128)(2,1)S(1)} %convolution_convert_fusion.9), channel_id=1, source_target_pairs={{0,8},{8,16},{16,24},{24,28},{28,20},{20,12},{12,4},{4,0},{1,9},{9... | collective-permute-start | bytes 2359304 | tf_op jit(solution)/shard_map/ppermute | solution.py:79
  454.8 73.5 %collective-permute-start.46 = (bf16[256,2048]{1,0:T(8,128)(2,1)}, bf16[256,2048]{1,0:T(8,128)(2,1)}, u32[]{:S(2)}, u32[]{:S(2)}) collective-permute-start(bf16[256,2048]{1,0:T(8,128)(2,1)} %convolution_convert_fusion.12), channel_id=1, source_target_pairs={{0,1},{1,0},{2,3},{3,2},{4,5},{5,4},{6,7},{7,6},{8,9},{9,8},{10,11... | collective-permute-start | bytes 3145736 | tf_op jit(solution)/shard_map/ppermute | solution.py:123
  454.8 54.0 %collective-permute-start.52 = (bf16[256,2048]{1,0:T(8,128)(2,1)S(1)}, bf16[256,2048]{1,0:T(8,128)(2,1)S(1)}, u32[]{:S(2)}, u32[]{:S(2)}) collective-permute-start(bf16[256,2048]{1,0:T(8,128)(2,1)S(1)} %convolution_convert_fusion.14), channel_id=1, source_target_pairs={{0,1},{1,0},{2,3},{3,2},{4,5},{5,4},{6,7},{7,6},{8,9},{9,8},{10,11... | collective-permute-start | bytes 3145736 | tf_op jit(solution)/shard_map/ppermute | solution.py:123
  472.7 29.6 %collective-permute-start.91 = (bf16[1536,256]{1,0:T(8,128)(2,1)S(1)}, bf16[1536,256]{1,0:T(8,128)(2,1)S(1)}, u32[]{:S(2)}, u32[]{:S(2)}) collective-permute-start(bf16[1536,256]{1,0:T(8,128)(2,1)S(1)} %convolution_convert_fusion.5), channel_id=1, source_target_pairs={{0,8},{8,16},{16,24},{24,28},{28,20},{20,12},{12,4},{4,0},{1,9},{9... | collective-permute-start | bytes 2359304 | tf_op jit(solution)/shard_map/ppermute | solution.py:79
  489.6 45.5 %collective-permute-start.44 = (bf16[256,2048]{1,0:T(8,128)(2,1)}, bf16[256,2048]{1,0:T(8,128)(2,1)}, u32[]{:S(2)}, u32[]{:S(2)}) collective-permute-start(bf16[256,2048]{1,0:T(8,128)(2,1)} %convolution_convert_fusion.13), channel_id=1, source_target_pairs={{0,1},{1,0},{2,3},{3,2},{4,5},{5,4},{6,7},{7,6},{8,9},{9,8},{10,11... | collective-permute-start | bytes 3145736 | tf_op jit(solution)/shard_map/ppermute | solution.py:123
  505.3 62.6 %collective-permute-start.92 = (bf16[1536,256]{1,0:T(8,128)(2,1)}, bf16[1536,256]{1,0:T(8,128)(2,1)}, u32[]{:S(2)}, u32[]{:S(2)}) collective-permute-start(bf16[1536,256]{1,0:T(8,128)(2,1)} %add_convert_fusion.7), channel_id=1, source_target_pairs={{0,8},{8,16},{16,24},{24,28},{28,20},{20,12},{12,4},{4,0},{1,9},{9... | collective-permute-start | bytes 2359304 | tf_op jit(solution)/shard_map/ppermute | solution.py:79
  508.9 61.0 %collective-permute-start.96 = (bf16[1536,256]{1,0:T(8,128)(2,1)}, bf16[1536,256]{1,0:T(8,128)(2,1)}, u32[]{:S(2)}, u32[]{:S(2)}) collective-permute-start(bf16[1536,256]{1,0:T(8,128)(2,1)} %add_convert_fusion.4), channel_id=1, source_target_pairs={{0,4},{8,0},{16,8},{24,16},{28,24},{20,28},{12,20},{4,12},{1,5},{9... | collective-permute-start | bytes 2359304 | tf_op jit(solution)/shard_map/ppermute | solution.py:79
  519.1 23.9 %collective-permute-start.85 = (bf16[256,1536]{1,0:T(8,128)(2,1)}, bf16[256,1536]{1,0:T(8,128)(2,1)}, u32[]{:S(2)}, u32[]{:S(2)}) collective-permute-start(bf16[256,1536]{1,0:T(8,128)(2,1)} %fusion.35), channel_id=1, source_target_pairs={{0,8},{8,16},{16,24},{24,28},{28,20},{20,12},{12,4},{4,0},{1,9},{9... | collective-permute-start | bytes 2359304 | tf_op jit(solution)/shard_map/ppermute | solution.py:79
  535.1 24.3 %collective-permute-start.78 = (bf16[256,1536]{1,0:T(8,128)(2,1)S(1)}, bf16[256,1536]{1,0:T(8,128)(2,1)S(1)}, u32[]{:S(2)}, u32[]{:S(2)}) collective-permute-start(bf16[256,1536]{1,0:T(8,128)(2,1)S(1)} %copy-done.125), channel_id=1, source_target_pairs={{0,8},{8,16},{16,24},{24,28},{28,20},{20,12},{12,4},{4,0},{1,9},{9... | collective-permute-start | bytes 2359304 | tf_op jit(solution)/shard_map/ppermute | solution.py:79
  543.0 21.5 %collective-permute-start.82 = (bf16[256,1536]{1,0:T(8,128)(2,1)S(1)}, bf16[256,1536]{1,0:T(8,128)(2,1)S(1)}, u32[]{:S(2)}, u32[]{:S(2)}) collective-permute-start(bf16[256,1536]{1,0:T(8,128)(2,1)S(1)} %copy-done.126), channel_id=1, source_target_pairs={{0,4},{8,0},{16,8},{24,16},{28,24},{20,28},{12,20},{4,12},{1,5},{9... | collective-permute-start | bytes 2359304 | tf_op jit(solution)/shard_map/ppermute | solution.py:79
  549.0 94.8 %collective-permute-start.47 = (bf16[256,2048]{1,0:T(8,128)(2,1)S(1)}, bf16[256,2048]{1,0:T(8,128)(2,1)S(1)}, u32[]{:S(2)}, u32[]{:S(2)}) collective-permute-start(bf16[256,2048]{1,0:T(8,128)(2,1)S(1)} %fusion.40), channel_id=1, source_target_pairs={{0,2},{1,3},{2,0},{3,1},{4,6},{5,7},{6,4},{7,5},{8,10},{9,11},{10,... | collective-permute-start | bytes 3145736 | tf_op jit(solution)/shard_map/ppermute | solution.py:127
  559.4 38.2 %collective-permute-start.53 = (bf16[256,2048]{1,0:T(8,128)(2,1)S(1)}, bf16[256,2048]{1,0:T(8,128)(2,1)S(1)}, u32[]{:S(2)}, u32[]{:S(2)}) collective-permute-start(bf16[256,2048]{1,0:T(8,128)(2,1)S(1)} %fusion.24), channel_id=1, source_target_pairs={{0,2},{1,3},{2,0},{3,1},{4,6},{5,7},{6,4},{7,5},{8,10},{9,11},{10,... | collective-permute-start | bytes 3145736 | tf_op jit(solution)/shard_map/ppermute | solution.py:127
  564.5 55.5 %collective-permute-start.45 = (bf16[256,2048]{1,0:T(8,128)(2,1)S(1)}, bf16[256,2048]{1,0:T(8,128)(2,1)S(1)}, u32[]{:S(2)}, u32[]{:S(2)}) collective-permute-start(bf16[256,2048]{1,0:T(8,128)(2,1)S(1)} %fusion.39), channel_id=1, source_target_pairs={{0,2},{1,3},{2,0},{3,1},{4,6},{5,7},{6,4},{7,5},{8,10},{9,11},{10,... | collective-permute-start | bytes 3145736 | tf_op jit(solution)/shard_map/ppermute | solution.py:127
  567.9 71.3 %collective-permute-start.50 = (bf16[256,2048]{1,0:T(8,128)(2,1)S(1)}, bf16[256,2048]{1,0:T(8,128)(2,1)S(1)}, u32[]{:S(2)}, u32[]{:S(2)}) collective-permute-start(bf16[256,2048]{1,0:T(8,128)(2,1)S(1)} %fusion.23), channel_id=1, source_target_pairs={{0,2},{1,3},{2,0},{3,1},{4,6},{5,7},{6,4},{7,5},{8,10},{9,11},{10,... | collective-permute-start | bytes 3145736 | tf_op jit(solution)/shard_map/ppermute | solution.py:127
  569.9 92.4 %collective-permute-start.93 = (bf16[1536,256]{1,0:T(8,128)(2,1)S(1)}, bf16[1536,256]{1,0:T(8,128)(2,1)S(1)}, u32[]{:S(2)}, u32[]{:S(2)}) collective-permute-start(bf16[1536,256]{1,0:T(8,128)(2,1)S(1)} %add_convert_fusion.6), channel_id=1, source_target_pairs={{0,8},{8,16},{16,24},{24,28},{28,20},{20,12},{12,4},{4,0},{1,9},{9... | collective-permute-start | bytes 2359304 | tf_op jit(solution)/shard_map/ppermute | solution.py:79
  597.6 148.0 %collective-permute-start.97 = (bf16[1536,256]{1,0:T(8,128)(2,1)}, bf16[1536,256]{1,0:T(8,128)(2,1)}, u32[]{:S(2)}, u32[]{:S(2)}) collective-permute-start(bf16[1536,256]{1,0:T(8,128)(2,1)} %add_convert_fusion.3), channel_id=1, source_target_pairs={{0,4},{8,0},{16,8},{24,16},{28,24},{20,28},{12,20},{4,12},{1,5},{9... | collective-permute-start | bytes 2359304 | tf_op jit(solution)/shard_map/ppermute | solution.py:79
  620.1 132.1 %collective-permute-start.86 = (bf16[256,1536]{1,0:T(8,128)(2,1)}, bf16[256,1536]{1,0:T(8,128)(2,1)}, u32[]{:S(2)}, u32[]{:S(2)}) collective-permute-start(bf16[256,1536]{1,0:T(8,128)(2,1)} %fusion.34), channel_id=1, source_target_pairs={{0,8},{8,16},{16,24},{24,28},{28,20},{20,12},{12,4},{4,0},{1,9},{9... | collective-permute-start | bytes 2359304 | tf_op jit(solution)/shard_map/ppermute | solution.py:79
  659.9 117.5 %collective-permute-start.83 = (bf16[256,1536]{1,0:T(8,128)(2,1)}, bf16[256,1536]{1,0:T(8,128)(2,1)}, u32[]{:S(2)}, u32[]{:S(2)}) collective-permute-start(bf16[256,1536]{1,0:T(8,128)(2,1)} %fusion.32), channel_id=1, source_target_pairs={{0,4},{8,0},{16,8},{24,16},{28,24},{20,28},{12,20},{4,12},{1,5},{9... | collective-permute-start | bytes 2359304 | tf_op jit(solution)/shard_map/ppermute | solution.py:79
  663.4 82.2 %collective-permute-start.94 = (bf16[1536,256]{1,0:T(8,128)(2,1)}, bf16[1536,256]{1,0:T(8,128)(2,1)}, u32[]{:S(2)}, u32[]{:S(2)}) collective-permute-start(bf16[1536,256]{1,0:T(8,128)(2,1)} %add_convert_fusion.5), channel_id=1, source_target_pairs={{0,8},{8,16},{16,24},{24,28},{28,20},{20,12},{12,4},{4,0},{1,9},{9... | collective-permute-start | bytes 2359304 | tf_op jit(solution)/shard_map/ppermute | solution.py:79
  670.9 81.3 %collective-permute-start.90 = (bf16[256,1536]{1,0:T(8,128)(2,1)}, bf16[256,1536]{1,0:T(8,128)(2,1)}, u32[]{:S(2)}, u32[]{:S(2)}) collective-permute-start(bf16[256,1536]{1,0:T(8,128)(2,1)} %fusion.36), channel_id=1, source_target_pairs={{0,4},{8,0},{16,8},{24,16},{28,24},{20,28},{12,20},{4,12},{1,5},{9... | collective-permute-start | bytes 2359304 | tf_op jit(solution)/shard_map/ppermute | solution.py:79
  745.6 87.7 %collective-permute-start.48 = (bf16[2,256,2048]{2,1,0:T(8,128)(2,1)}, bf16[2,256,2048]{2,1,0:T(8,128)(2,1)}, u32[]{:S(2)}, u32[]{:S(2)}) collective-permute-start(bf16[2,256,2048]{2,1,0:T(8,128)(2,1)} %pad_maximum_fusion.8), channel_id=1, source_target_pairs={{0,1},{1,0},{2,3},{3,2},{4,5},{5,4},{6,7},{7,6},{8,9},{9,8},{10,11... | collective-permute-start | bytes 6291464 | tf_op jit(solution)/shard_map/ppermute | solution.py:123
  745.7 24.6 %collective-permute-start.55 = (bf16[512,512]{1,0:T(8,128)(2,1)S(1)}, bf16[512,512]{1,0:T(8,128)(2,1)S(1)}, u32[]{:S(2)}, u32[]{:S(2)}) collective-permute-start(bf16[512,512]{1,0:T(8,128)(2,1)S(1)} %get-tuple-element.163), channel_id=1, source_target_pairs={{0,8},{12,4},{16,24},{28,20},{1,9},{13,5},{17,25},{29,21},{2,10},{... | collective-permute-start | bytes 1572872 | tf_op jit(solution)/shard_map/ppermute | solution.py:461
  760.6 23.5 %collective-permute-start.80 = (bf16[256,1536]{1,0:T(8,128)(2,1)S(1)}, bf16[256,1536]{1,0:T(8,128)(2,1)S(1)}, u32[]{:S(2)}, u32[]{:S(2)}) collective-permute-start(bf16[256,1536]{1,0:T(8,128)(2,1)S(1)} %copy-done.124), channel_id=1, source_target_pairs={{0,8},{8,16},{16,24},{24,28},{28,20},{20,12},{12,4},{4,0},{1,9},{9... | collective-permute-start | bytes 2359304 | tf_op jit(solution)/shard_map/ppermute | solution.py:79
  770.3 23.0 %collective-permute-start.57 = (bf16[512,512]{1,0:T(8,128)(2,1)S(1)}, bf16[512,512]{1,0:T(8,128)(2,1)S(1)}, u32[]{:S(2)}, u32[]{:S(2)}) collective-permute-start(bf16[512,512]{1,0:T(8,128)(2,1)S(1)} %get-tuple-element.164), channel_id=1, source_target_pairs={{4,12},{8,0},{20,28},{24,16},{5,13},{9,1},{21,29},{25,17},{6,14},{... | collective-permute-start | bytes 1572872 | tf_op jit(solution)/shard_map/ppermute | solution.py:466
  828.1 22.0 %collective-permute-start.66 = (bf16[256,1152]{1,0:T(8,128)(2,1)S(1)}, bf16[256,1152]{1,0:T(8,128)(2,1)S(1)}, u32[]{:S(2)}, u32[]{:S(2)}) collective-permute-start(bf16[256,1152]{1,0:T(8,128)(2,1)S(1)} %convolution_convert_fusion), channel_id=1, source_target_pairs={{0,4},{8,0},{16,8},{24,16},{28,24},{20,28},{12,20},{4,12},{1,5},{9... | collective-permute-start | bytes 1769480 | tf_op jit(solution)/shard_map/ppermute | solution.py:79
  831.0 26.1 %collective-permute-start.61 = (bf16[256,2048]{1,0:T(8,128)(2,1)S(1)}, bf16[256,2048]{1,0:T(8,128)(2,1)S(1)}, u32[]{:S(2)}, u32[]{:S(2)}) collective-permute-start(bf16[256,2048]{1,0:T(8,128)(2,1)S(1)} %fusion.26), channel_id=1, source_target_pairs={{0,2},{1,3},{2,0},{3,1},{4,6},{5,7},{6,4},{7,5},{8,10},{9,11},{10,... | collective-permute-start | bytes 3145736 | tf_op jit(solution)/shard_map/ppermute | solution.py:127
  833.3 44.9 %collective-permute-start.59 = (bf16[256,2048]{1,0:T(8,128)(2,1)S(1)}, bf16[256,2048]{1,0:T(8,128)(2,1)S(1)}, u32[]{:S(2)}, u32[]{:S(2)}) collective-permute-start(bf16[256,2048]{1,0:T(8,128)(2,1)S(1)} %fusion.25), channel_id=1, source_target_pairs={{0,2},{1,3},{2,0},{3,1},{4,6},{5,7},{6,4},{7,5},{8,10},{9,11},{10,... | collective-permute-start | bytes 3145736 | tf_op jit(solution)/shard_map/ppermute | solution.py:127
  846.1 60.7 %collective-permute-start.72 = (bf16[512,256]{1,0:T(8,128)(2,1)S(1)}, bf16[512,256]{1,0:T(8,128)(2,1)S(1)}, u32[]{:S(2)}, u32[]{:S(2)}) collective-permute-start(bf16[512,256]{1,0:T(8,128)(2,1)S(1)} %copy-done.128), channel_id=1, source_target_pairs={{0,8},{8,16},{16,24},{24,28},{28,20},{20,12},{12,4},{4,0},{1,9},{9... | collective-permute-start | bytes 786440 | tf_op jit(solution)/shard_map/ppermute | solution.py:79
  846.1 62.5 %collective-permute-start.76 = (bf16[512,256]{1,0:T(8,128)(2,1)S(1)}, bf16[512,256]{1,0:T(8,128)(2,1)S(1)}, u32[]{:S(2)}, u32[]{:S(2)}) collective-permute-start(bf16[512,256]{1,0:T(8,128)(2,1)S(1)} %copy-done.127), channel_id=1, source_target_pairs={{0,4},{8,0},{16,8},{24,16},{28,24},{20,28},{12,20},{4,12},{1,5},{9... | collective-permute-start | bytes 786440 | tf_op jit(solution)/shard_map/ppermute | solution.py:79
  850.2 38.5 %collective-permute-start.64 = (bf16[256,1152]{1,0:T(8,128)(2,1)S(1)}, bf16[256,1152]{1,0:T(8,128)(2,1)S(1)}, u32[]{:S(2)}, u32[]{:S(2)}) collective-permute-start(bf16[256,1152]{1,0:T(8,128)(2,1)S(1)} %add_convert_fusion.12), channel_id=1, source_target_pairs={{0,8},{8,16},{16,24},{24,28},{28,20},{20,12},{12,4},{4,0},{1,9},{9... | collective-permute-start | bytes 1769480 | tf_op jit(solution)/shard_map/ppermute | solution.py:79
  857.1 28.6 %collective-permute-start.67 = (bf16[256,1152]{1,0:T(8,128)(2,1)S(1)}, bf16[256,1152]{1,0:T(8,128)(2,1)S(1)}, u32[]{:S(2)}, u32[]{:S(2)}) collective-permute-start(bf16[256,1152]{1,0:T(8,128)(2,1)S(1)} %add_convert_fusion.10), channel_id=1, source_target_pairs={{0,4},{8,0},{16,8},{24,16},{28,24},{20,28},{12,20},{4,12},{1,5},{9... | collective-permute-start | bytes 1769480 | tf_op jit(solution)/shard_map/ppermute | solution.py:79
  885.8 43.8 %collective-permute-start.62 = (f32[2,256,2048]{2,1,0:T(8,128)}, f32[2,256,2048]{2,1,0:T(8,128)}, u32[]{:S(2)}, u32[]{:S(2)}) collective-permute-start(f32[2,256,2048]{2,1,0:T(8,128)} %pad_maximum_fusion.5), channel_id=1, source_target_pairs={{0,1},{1,0},{2,3},{3,2},{4,5},{5,4},{6,7},{7,6},{8,9},{9,8},{10,11... | collective-permute-start | bytes 12582920 | tf_op jit(solution)/shard_map/ppermute | solution.py:123
  (192 other events, 2741.8 us)

commit v2 on v1

v2 whole, which is shorter than its diff:
```python
import functools

import jax
import jax.numpy as jnp
from jax import lax
from jax.experimental import pallas as pl
from jax.experimental.pallas import tpu as pltpu
from jax.sharding import PartitionSpec as P

MICRO_BATCHES = 2
GROUP_DEVICES = 4

eps = 1e-06
rope_base = 1000000.0
masked = -1e30
f32 = jnp.float32
bf16 = jnp.bfloat16


def product(left_side, right_side):
    return jnp.dot(left_side, right_side, preferred_element_type=f32)


def by_transpose(left_side, right_side):
    return lax.dot_general(
        left_side, right_side, (((1,), (1,)), ((), ())), preferred_element_type=f32
    )


def transpose_by(left_side, right_side):
    return lax.dot_general(
        left_side, right_side, (((0,), (0,)), ((), ())), preferred_element_type=f32
    )


def recip_rms(values):
    return lax.rsqrt(jnp.mean(values * values, axis=-1, keepdims=True) + eps)


def rms_back(values, reciprocal, gain, gradient):
    scaled = gain * gradient
    cubed = reciprocal * reciprocal * reciprocal
    back = reciprocal * scaled - values * cubed * jnp.mean(scaled * values, axis=-1, keepdims=True)
    return (back, gradient * values * reciprocal)


def layout(lengths, relative, row_count):
    seg_ends = jnp.cumsum(lengths, dtype=jnp.int32)
    starts = seg_ends - lengths
    row_ids = jnp.arange(row_count, dtype=jnp.int32)
    seg_index = jnp.sum(
        (row_ids[:, None] >= seg_ends[None, :]).astype(jnp.int32), axis=1, dtype=jnp.int32
    )
    seg_onehot = seg_index[:, None] == jnp.arange(lengths.shape[0], dtype=jnp.int32)[None, :]
    seg_start = jnp.sum(jnp.where(seg_onehot, starts[None, :], 0), axis=1, dtype=jnp.int32)
    prompt = relative == 0
    segment = jnp.where(prompt, 0, 1 + seg_index)
    position = jnp.where(prompt, row_ids, row_count + row_ids - seg_start)
    return (segment, position)


def ring_order(count):
    return list(range(0, count, 2)) + list(range(count - 1, 0, -2))


def ring_step(block, count, forward):
    places = ring_order(count)
    turn = 1 if forward else -1
    route = [(places[i], places[(i + turn) % count]) for i in range(count)]
    return lax.ppermute(block, "dp", route)


class Gather:
    def __init__(self, block, count):
        self.count = count
        self.left = count // 2
        self.cut = (block.shape[1] // 256) * 128
        self.held = [[block], [block]]
        self.flying = []

    def issue(self):
        if self.left:
            self.left -= 1
            ahead, behind = self.held[0][-1], self.held[1][-1]
            if not self.left:
                ahead, behind = ahead[:, : self.cut], behind[:, self.cut :]
            self.flying = [
                (0, ring_step(ahead, self.count, True)),
                (1, ring_step(behind, self.count, False)),
            ]

    def land(self, arrays):
        for (way, _), array in zip(self.flying, arrays):
            self.held[way].append(array)
        self.flying = []

    def gathered(self, first, end):
        ahead, behind = self.held
        half = self.count // 2
        near = [ahead[step] for step in range(half - 1, -1, -1)]
        near += [behind[step] for step in range(1, half)]
        near.append(jnp.concatenate([ahead[half], behind[half]], axis=1))
        return jnp.concatenate([block[:, first:end] for block in near], axis=0)


class Scatter:
    def __init__(self, chunk, count, split=True):
        half = count // 2
        self.count, self.chunk, self.split = count, chunk, split
        self.own = half - 1
        self.left = half
        self.got = [None, None]
        self.flying = []

    def issue(self, *values):
        parts = []
        if self.left == self.count // 2:
            far = self.chunk(self.own + self.left).astype(bf16)
            cut = far.shape[1] // 256 * 128 or far.shape[1] // 2
            if self.split:
                parts = [(0, far[:, :cut]), (1, far[:, cut:])]
            else:
                ahead = self.chunk(self.own + self.left - 1).astype(bf16)
                parts = [(0, ahead), (1, far)]
        elif self.left > 0:
            late = 0 if self.split else 1
            for way, slot in ((0, self.own + self.left - late), (1, self.own - self.left)):
                if slot == self.own:
                    self.kept = self.got[way]
                    continue
                part, got = self.chunk(slot), self.got[way].astype(f32)
                lack = part.shape[1] - got.shape[1]
                if lack:
                    got = jnp.pad(got, ((0, 0), ((0, lack), (lack, 0))[way]))
                parts.append((way, (part + got).astype(bf16)))
        self.left -= 1
        if parts and values:
            tied = lax.optimization_barrier(tuple(part for _, part in parts) + values)
            parts = [(way, part) for (way, _), part in zip(parts, tied)]
            values = tied[len(parts) :]
        self.flying = [(way, ring_step(part, self.count, way == 0)) for way, part in parts]
        return values

    def land(self, arrays):
        for (way, _), array in zip(self.flying, arrays):
            self.got[way] = array
        self.flying = []

    def total(self):
        if not self.split:
            self.got[0] = self.kept
        return self.chunk(self.own) + self.got[0].astype(f32) + self.got[1].astype(f32)


def single(values):
    return values[0] if len(values) == 1 else values


def pump(ring, *values):
    arrays = [array for _, array in ring.flying]
    if arrays and values:
        tied = lax.optimization_barrier(tuple(arrays) + values)
        arrays, values = list(tied[: len(arrays)]), tied[len(arrays) :]
    ring.land(arrays)
    if isinstance(ring, Scatter):
        values = ring.issue(*values)
    else:
        ring.issue()
    return single(values)


def settle(ring, *values):
    arrays = [array for _, array in ring.flying]
    tied = lax.optimization_barrier(tuple(arrays) + values)
    ring.land(list(tied[: len(arrays)]))
    return single(tied[len(arrays) :])


def drain(ring, *values):
    while ring.flying or ring.left > 0:
        values = pump(ring, *values)
        values = values if isinstance(values, tuple) else (values,)
    return single(values)


def order(*values):
    return lax.optimization_barrier(values)


def swap_core(block):
    return lax.ppermute(block, "mp", [(i, i ^ 1) for i in range(lax.axis_size("mp"))])


def swap_x(block):
    return lax.ppermute(block, "mp", [(i, i ^ 2) for i in range(lax.axis_size("mp"))])


def swap_dp(block, level):
    count = lax.axis_size("dp")
    return lax.ppermute(block, "dp", [(i, i ^ level) for i in range(count)])


def chip_sum(other_part, own_part):
    return (own_part + swap_core(other_part.astype(bf16)).astype(f32)).astype(bf16)


def across(other_part, own_part):
    chip = chip_sum(other_part, own_part)
    return chip.astype(f32) + swap_x(chip).astype(f32)


def group_route(apart, sources):
    count = lax.axis_size("dp")
    route = []
    for base in range(0, count, GROUP_DEVICES):
        route += [(base + s, base + (s ^ apart)) for s in sources]
    return route

def by_row(*shape):
    return pl.BlockSpec(shape, lambda i, *rest: (i,) + (0,) * (len(shape) - 1))


def at_row(place, *shape):
    return pl.BlockSpec(shape, lambda i, *rest: (place,) + (0,) * (len(shape) - 1))


def whole(*shape):
    return pl.BlockSpec(shape, lambda *at: (0,) * len(shape))


def turned(values, cosine, sine):
    return values * cosine + pltpu.roll(values, values.shape[-1] // 2, 1) * sine


def bring_kernel(columns_ref, core_ref, in_ref, out_ref):
    core = core_ref[0]
    out_ref[:, 0:1] = in_ref[:, pl.ds(core, 1)]
    out_ref[:, 1:2] = in_ref[:, pl.ds(1 - core, 1)]


def place_kernel(columns_ref, core_ref, own_ref, other_ref, out_ref):
    core = core_ref[0]
    out_ref[:, pl.ds(core, 1)] = own_ref[...][:, None]
    out_ref[:, pl.ds(1 - core, 1)] = other_ref[...][:, None]


def heads_kernel(sizes, proj_ref, cos_ref, sin_ref, gain_ref, q_ref, kv_ref, gate_ref):
    query_cols, key_cols, head_dim = sizes
    cosine, sine = cos_ref[...], sin_ref[...]
    for start in range(0, query_cols + key_cols, head_dim):
        values = proj_ref[:, start : start + head_dim]
        gain = gain_ref[0:1] if start < query_cols else gain_ref[1:2]
        low = turned(values * recip_rms(values) * gain, cosine, sine).astype(bf16)
        if start < query_cols:
            q_ref[:, start : start + head_dim] = low
        else:
            kv_ref[:, start - query_cols : start - query_cols + head_dim] = low
    values = proj_ref[:, query_cols + key_cols : query_cols + 2 * key_cols]
    kv_ref[:, key_cols:] = values.astype(bf16)
    gate_ref[...] = jax.nn.sigmoid(proj_ref[:, query_cols + 2 * key_cols :])


def attend_kernel(
    sizes, flag_ref, q_ref, kv_ref, far_ref, col_ref, row_ref, gate_ref, gated_ref, att_ref, lse_ref
):
    head_dim, key_cols, kv_heads, repeat_heads, scale = sizes
    no_far = jnp.where(flag_ref[pl.program_id(0)] == 1, masked, 0.0)
    columns, rows = col_ref[...], row_ref[0]
    own = (columns[:, 0:1] == rows[0:1]) & (rows[1:2] <= columns[:, 1:2])
    for kv_head in range(kv_heads):
        at = slice(kv_head * head_dim, (kv_head + 1) * head_dim)
        at_value = slice(key_cols + kv_head * head_dim, key_cols + (kv_head + 1) * head_dim)
        for head in range(kv_head * repeat_heads, (kv_head + 1) * repeat_heads):
            here = slice(head * head_dim, (head + 1) * head_dim)
            queries = q_ref[:, here]
            far = by_transpose(queries, far_ref[:, at]) * scale + no_far
            near = jnp.where(own, by_transpose(queries, kv_ref[:, at]) * scale, masked)
            peak = jnp.maximum(
                jnp.max(far, axis=-1, keepdims=True), jnp.max(near, axis=-1, keepdims=True)
            )
            far = jnp.exp(far - peak)
            near = jnp.exp(near - peak)
            total = jnp.sum(far, axis=-1, keepdims=True) + jnp.sum(near, axis=-1, keepdims=True)
            share = 1.0 / total
            attended = product((far * share).astype(bf16), far_ref[:, at_value]) + product(
                (near * share).astype(bf16), kv_ref[:, at_value]
            )
            att_ref[:, here] = attended
            gated_ref[:, here] = (attended * gate_ref[:, head : head + 1]).astype(bf16)
            lse_ref[:, head : head + 1] = peak + jnp.log(total)


def attend_back_kernel(
    sizes,
    flag_ref,
    q_ref,
    kv_ref,
    far_ref,
    col_ref,
    row_ref,
    gate_ref,
    att_ref,
    lse_ref,
    grad_ref,
    proj_ref,
    cos_ref,
    sin_ref,
    gain_ref,
    dq_ref,
    dfar_ref,
    dkv_ref,
    logit_ref,
    dgain_ref,
):
    micro, head_dim, key_cols, kv_heads, repeat_heads, scale = sizes
    no_far = jnp.where(flag_ref[micro] == 1, masked, 0.0)
    columns, rows = col_ref[...], row_ref[0]
    own = (columns[:, 0:1] == rows[0:1]) & (rows[1:2] <= columns[:, 1:2])
    cosine, sine, gain = cos_ref[...], sin_ref[...], gain_ref[0:1]
    logit_ref[...] = jnp.zeros_like(logit_ref)
    gain_sum = jnp.zeros((1, head_dim), f32)
    for kv_head in range(kv_heads):
        at = slice(kv_head * head_dim, (kv_head + 1) * head_dim)
        at_value = slice(key_cols + kv_head * head_dim, key_cols + (kv_head + 1) * head_dim)
        totals = [0.0, 0.0, 0.0, 0.0]
        for head in range(kv_head * repeat_heads, (kv_head + 1) * repeat_heads):
            here = slice(head * head_dim, (head + 1) * head_dim)
            queries = q_ref[:, here]
            gate = gate_ref[:, head : head + 1]
            gated_grad, attended = grad_ref[:, here], att_ref[:, here]
            weighted = jnp.sum(gated_grad * attended, axis=-1, keepdims=True)
            logit_ref[:, head : head + 1] = (weighted * gate * (1.0 - gate)).astype(bf16)
            low = (gated_grad * gate).astype(bf16)
            delta = jnp.sum(low.astype(f32) * attended, axis=-1, keepdims=True)
            log_total = lse_ref[:, head : head + 1]
            far = jnp.exp(by_transpose(queries, far_ref[:, at]) * scale + (no_far - log_total))
            near = by_transpose(queries, kv_ref[:, at]) * scale
            near = jnp.exp(jnp.where(own, near - log_total, masked))
            far_low = (far * (by_transpose(low, far_ref[:, at_value]) - delta)).astype(bf16)
            near_low = (near * (by_transpose(low, kv_ref[:, at_value]) - delta)).astype(bf16)
            totals[0] = totals[0] + transpose_by(far_low, queries)
            totals[1] = totals[1] + transpose_by(far.astype(bf16), low)
            totals[2] = totals[2] + transpose_by(near_low, queries)
            totals[3] = totals[3] + transpose_by(near.astype(bf16), low)
            back = (product(far_low, far_ref[:, at]) + product(near_low, kv_ref[:, at])) * scale
            values = proj_ref[:, here]
            back, terms = rms_back(
                values, recip_rms(values), gain, turned(back, cosine, -sine)
            )
            dq_ref[:, here] = back.astype(bf16)
            gain_sum = gain_sum + jnp.sum(terms, axis=0, keepdims=True)
        dfar_ref[:, at] = (totals[0] * scale).astype(bf16)
        dfar_ref[:, at_value] = totals[1].astype(bf16)
        dkv_ref[:, at] = totals[2] * scale
        dkv_ref[:, at_value] = totals[3]
    dgain_ref[...] = jnp.broadcast_to(gain_sum, dgain_ref.shape)


def join_kernel(
    sizes,
    flag_ref,
    dq_ref,
    dkv_ref,
    one_ref,
    two_ref,
    three_ref,
    logit_ref,
    proj_ref,
    cos_ref,
    sin_ref,
    gain_ref,
    out_ref,
    dgain_ref,
):
    micro, query_cols, key_cols, head_dim = sizes
    prompt = flag_ref[micro] == 1
    cosine, sine, gain = cos_ref[...], sin_ref[...], gain_ref[1:2]
    out_ref[:, :query_cols] = dq_ref[...]
    out_ref[:, query_cols + 2 * key_cols :] = logit_ref[...]
    gain_sum = jnp.zeros((1, head_dim), f32)
    for start in range(0, 2 * key_cols, head_dim):
        at = slice(start, start + head_dim)
        arrived = one_ref[:, at].astype(f32) + two_ref[:, at].astype(f32)
        arrived = arrived + three_ref[:, at].astype(f32)
        total = dkv_ref[:, at] + jnp.where(prompt, arrived, 0.0)
        if start < key_cols:
            values = proj_ref[:, at]
            total, terms = rms_back(
                values, recip_rms(values), gain, turned(total, cosine, -sine)
            )
            gain_sum = gain_sum + jnp.sum(terms, axis=0, keepdims=True)
        out_ref[:, query_cols + start : query_cols + start + head_dim] = total.astype(bf16)
    dgain_ref[...] = jnp.broadcast_to(gain_sum, dgain_ref.shape)


def cost(flops, nbytes, exps=0):
    return pl.CostEstimate(flops=flops, bytes_accessed=nbytes, transcendentals=exps)


vmem_bytes = 56 << 20


def on_device(
    tokens,
    cotangent,
    query_weight,
    key_matrix,
    value_matrix,
    head_gate_weight,
    out_weight,
    gate_weight,
    up_weight,
    down_weight,
    norm_attn,
    norm_mlp,
    norm_query,
    norm_key,
    cont_lengths,
):
    count = lax.axis_size("dp")
    dp_index = lax.axis_index("dp")
    core = lax.axis_index("mp") % 2
    place = jnp.where(dp_index % 2 == 0, dp_index // 2, count - 1 - dp_index // 2)
    offset = dp_index % GROUP_DEVICES
    group_index = dp_index // GROUP_DEVICES
    total_rows, width = tokens.shape
    block_rows = total_rows // MICRO_BATCHES
    own_rows = block_rows // 2
    depth = width // count
    head_dim = norm_query.shape[0]
    head_count = head_gate_weight.shape[1]
    query_cols = query_weight.shape[1]
    key_cols = key_matrix.shape[1]
    kv_heads = key_cols // head_dim
    repeat_heads = head_count // kv_heads
    hidden_units = gate_weight.shape[1]
    score_scale = head_dim ** (-0.5)
    gain_query = norm_query.astype(f32)
    key_gain = norm_key.astype(f32)
    first_place = (place + count - (count // 2 - 1)) % count
    places = ring_order(count)

    extra = 128
    lane = lax.broadcasted_iota(jnp.int32, (depth, extra), 1)
    small = jnp.pad(head_gate_weight, ((0, 0), (0, extra - head_count)))
    small = jnp.where(lane == head_count, norm_attn[:, None], small)
    small = jnp.where(lane == head_count + 1, norm_mlp[:, None], small)
    packed = jnp.concatenate([query_weight, key_matrix, value_matrix, small], axis=1)
    in_ring = Gather(jnp.concatenate([packed, out_weight.T], axis=1), count)
    in_ring.issue()

    params = pltpu.CompilerParams(vmem_limit_bytes=vmem_bytes)
    column_places = jnp.asarray(places, jnp.int32)[
        (first_place + jnp.arange(count, dtype=jnp.int32)) % count
    ]
    core_place = core.astype(jnp.int32)[None]

    def rows_in(block):
        halves = block.reshape((MICRO_BATCHES, 2, own_rows) + block.shape[1:])
        swapped = jnp.concatenate([halves[:, 1:], halves[:, :1]], axis=1)
        return jnp.where(core == 0, halves, swapped).reshape(block.shape)

    def bring(block, name):
        if depth % 128:
            ring = [block[:, i * depth : (i + 1) * depth] for i in places]
            block = lax.dynamic_slice_in_dim(
                jnp.concatenate(ring + ring, axis=1), first_place * depth, width, axis=1
            )
            return rows_in(block)
        shape = (MICRO_BATCHES, 2, own_rows, width)
        there = (MICRO_BATCHES, 2, own_rows, depth)
        return pl.pallas_call(
            bring_kernel,
            out_shape=jax.ShapeDtypeStruct(shape, block.dtype),
            grid_spec=pltpu.PrefetchScalarGridSpec(
                num_scalar_prefetch=2,
                grid=(count,),
                in_specs=[pl.BlockSpec(there, lambda i, cols, core: (0, 0, 0, cols[i]))],
                out_specs=pl.BlockSpec(there, lambda i, cols, core: (0, 0, 0, i)),
            ),
            compiler_params=params,
            cost_estimate=cost(0, 2 * block.size * block.dtype.itemsize),
            name=name,
        )(column_places, core_place, block.reshape(shape)).reshape(block.shape)

    def columns_back(block):
        back = lax.dynamic_slice_in_dim(
            jnp.concatenate([block, block], axis=-1),
            ((count - first_place) % count) * depth,
            width,
            axis=-1,
        )
        at = {device: i for i, device in enumerate(places)}
        return jnp.concatenate(
            [back[..., at[i] * depth : (at[i] + 1) * depth] for i in range(count)], axis=-1
        )

    def place_back(own, other, turned, name):
        if depth % 128:
            low = jnp.where(core == 0, own, other)
            high = jnp.where(core == 0, other, own)
            block = jnp.stack([low, high], axis=1).reshape(total_rows, width)
            return columns_back(block) if turned else block
        there = (MICRO_BATCHES, own_rows, depth)
        return pl.pallas_call(
            place_kernel,
            out_shape=jax.ShapeDtypeStruct((MICRO_BATCHES, 2, own_rows, width), own.dtype),
            grid_spec=pltpu.PrefetchScalarGridSpec(
                num_scalar_prefetch=2,
                grid=(count,),
                in_specs=[pl.BlockSpec(there, lambda i, cols, core: (0, 0, i))] * 2,
                out_specs=pl.BlockSpec(
                    (MICRO_BATCHES, 2, own_rows, depth),
                    lambda i, cols, core: (0, 0, 0, cols[i] if turned else i),
                ),
            ),
            compiler_params=params,
            cost_estimate=cost(1024, 1024),
            name=name,
        )(column_places, core_place, own, other).reshape(total_rows, width)

    inputs_low = bring(tokens, "bring_tokens")

    inverse = jnp.power(rope_base, -jnp.arange(head_dim // 2, dtype=f32) * (2.0 / head_dim))
    relatives, segments, positions = [], [], []
    for micro in range(MICRO_BATCHES):
        holder = GROUP_DEVICES - 1 if micro % 2 == 1 else 0
        relative = jnp.bitwise_xor(offset, holder)
        lengths = cont_lengths[group_index, jnp.maximum(relative - 1, 0), micro]
        segment, position = layout(lengths, relative, block_rows)
        relatives.append(relative)
        segments.append(segment)
        positions.append(position)
    segment = rows_in(jnp.concatenate(segments))
    position = rows_in(jnp.concatenate(positions))
    angles = position.astype(f32)[:, None] * inverse[None, :]
    inputs_low, angles = pump(in_ring, inputs_low, angles)
    inputs = inputs_low.astype(f32)
    recip_one = recip_rms(inputs)
    recip_one, cotangent, late_down = pump(in_ring, recip_one, cotangent, down_weight)
    mlp_block = jnp.concatenate([gate_weight, up_weight, late_down.T], axis=1)
    cosine, sine = jnp.cos(angles), jnp.sin(angles)
    cosine = jnp.concatenate([cosine, cosine], axis=1)
    sine = jnp.concatenate([-sine, sine], axis=1)
    spots = jnp.stack([segment, position])
    spot_cols = spots.T
    spot_rows = spots.reshape(2, MICRO_BATCHES, block_rows).transpose(1, 0, 2)
    prompts = jnp.stack([(r == 0).astype(jnp.int32) for r in relatives])
    head_gain = jnp.stack([gain_query, key_gain])

    recip_one, cosine, sine, mlp_block = pump(in_ring, recip_one, cosine, sine, mlp_block)
    recip_one, mlp_block = drain(in_ring, recip_one, mlp_block)
    mlp_ring = Gather(mlp_block, count)
    mlp_ring.issue()
    joined = packed.shape[1]
    in_full = in_ring.gathered(0, joined)
    out_turned = in_ring.gathered(joined, joined + query_cols)
    first_gain = query_cols + 2 * key_cols + head_count
    gain_attn = in_full[:, first_gain].astype(f32)[None, :]
    gain_mlp = in_full[:, first_gain + 1].astype(f32)[None, :]
    normed_one = (inputs * recip_one * gain_attn).astype(bf16)
    projected = product(normed_one, in_full)
    rotated_queries, own_kv, head_gate = pl.pallas_call(
        functools.partial(heads_kernel, (query_cols, key_cols, head_dim)),
        out_shape=(
            jax.ShapeDtypeStruct((total_rows, query_cols), bf16),
            jax.ShapeDtypeStruct((total_rows, 2 * key_cols), bf16),
            jax.ShapeDtypeStruct((total_rows, extra), f32),
        ),
        grid=(total_rows // own_rows,),
        in_specs=[
            by_row(own_rows, joined),
            by_row(own_rows, head_dim),
            by_row(own_rows, head_dim),
            whole(2, head_dim),
        ],
        out_specs=(
            by_row(own_rows, query_cols),
            by_row(own_rows, 2 * key_cols),
            by_row(own_rows, extra),
        ),
        compiler_params=params,
        cost_estimate=cost(total_rows * joined * 20, total_rows * joined * 7),
        name="heads",
    )(projected, cosine, sine, head_gain)

    first_kv, second_kv = own_kv[:block_rows], own_kv[block_rows:]
    sent = jnp.where(offset == 0, first_kv, second_kv)
    by_one = lax.ppermute(sent, "dp", group_route(1, (0, 3)))
    by_two = lax.ppermute(sent, "dp", group_route(2, (0, 3)))
    by_both = lax.ppermute(sent, "dp", group_route(3, (0, 3)))
    far_kv = [
        jnp.where(offset == 1, by_one, jnp.where(offset == 2, by_two, by_both)),
        jnp.where(offset == 2, by_one, jnp.where(offset == 1, by_two, by_both)),
    ]

    far_kv = jnp.concatenate(far_kv, axis=0)
    far_kv, cotangent = pump(mlp_ring, far_kv, cotangent)
    sizes = (head_dim, key_cols, kv_heads, repeat_heads, score_scale)
    pairs = total_rows * 2 * block_rows * query_cols
    gated_all, attended, log_totals = pl.pallas_call(
        functools.partial(attend_kernel, sizes),
        out_shape=(
            jax.ShapeDtypeStruct((total_rows, query_cols), bf16),
            jax.ShapeDtypeStruct((total_rows, query_cols), f32),
            jax.ShapeDtypeStruct((total_rows, extra), f32),
        ),
        grid_spec=pltpu.PrefetchScalarGridSpec(
            num_scalar_prefetch=1,
            grid=(MICRO_BATCHES, 2),
            in_specs=[
                pl.BlockSpec((own_rows, query_cols), lambda m, i, flag: (2 * m + i, 0)),
                pl.BlockSpec((block_rows, 2 * key_cols), lambda m, i, flag: (m, 0)),
                pl.BlockSpec((block_rows, 2 * key_cols), lambda m, i, flag: (m, 0)),
                pl.BlockSpec((own_rows, 2), lambda m, i, flag: (2 * m + i, 0)),
                pl.BlockSpec((1, 2, block_rows), lambda m, i, flag: (m, 0, 0)),
                pl.BlockSpec((own_rows, extra), lambda m, i, flag: (2 * m + i, 0)),
            ],
            out_specs=(
                pl.BlockSpec((own_rows, query_cols), lambda m, i, flag: (2 * m + i, 0)),
                pl.BlockSpec((own_rows, query_cols), lambda m, i, flag: (2 * m + i, 0)),
                pl.BlockSpec((own_rows, extra), lambda m, i, flag: (2 * m + i, 0)),
            ),
        ),
        compiler_params=params,
        cost_estimate=cost(4 * pairs, total_rows * query_cols * 12, pairs // head_dim),
        name="attend",
    )(prompts, rotated_queries, own_kv, far_kv, spot_cols, spot_rows, head_gate)

    gated_all, cotangent = order(gated_all, cotangent)
    upstream_low = bring(cotangent, "bring_cotangent")
    gated_all, upstream_low = pump(mlp_ring, gated_all, upstream_low)
    middles, recips_two, norms_two = [], [], []
    for micro in range(MICRO_BATCHES):
        base = micro * block_rows
        gated_low = gated_all[base : base + block_rows]
        summed = across(
            by_transpose(gated_low[own_rows:], out_turned),
            by_transpose(gated_low[:own_rows], out_turned),
        )
        middle = inputs[base : base + own_rows] + summed
        recip_two = recip_rms(middle)
        own_norm = (middle * recip_two * gain_mlp).astype(bf16)
        if micro == 0:
            own_norm = pump(mlp_ring, own_norm)
        middles.append(middle)
        recips_two.append(recip_two)
        norms_two += [own_norm, swap_core(own_norm)]
    normed_two = jnp.concatenate(norms_two, axis=0)
    normed_two = drain(mlp_ring, normed_two)
    gate_up_full = mlp_ring.gathered(0, 2 * hidden_units)
    down_turned = mlp_ring.gathered(2 * hidden_units, 3 * hidden_units)
    pre = product(normed_two, gate_up_full)
    gate_pre, up_pre = pre[:, :hidden_units], pre[:, hidden_units:]
    sigmoid_gate = jax.nn.sigmoid(gate_pre)
    swish_gate = gate_pre * sigmoid_gate
    hidden_low = (swish_gate * up_pre).astype(bf16)
    down_back = Scatter(
        lambda slot, left=hidden_low, right=upstream_low: transpose_by(
            left, right[:, slot * depth : (slot + 1) * depth]
        ),
        count,
        False,
    )
    (upstream_late,) = down_back.issue(upstream_low)
    hidden_grad = product(upstream_late, down_turned)
    gate_grad = (
        hidden_grad * up_pre * sigmoid_gate * (1.0 + gate_pre * (1.0 - sigmoid_gate))
    ).astype(bf16)
    up_grad = (hidden_grad * swish_gate).astype(bf16)
    gate_grad, up_grad = pump(down_back, gate_grad, up_grad)
    gate_up_grad = jnp.concatenate([gate_grad, up_grad], axis=1)
    partial = by_transpose(gate_up_grad, gate_up_full).astype(bf16)
    partial, gate_up_late = pump(down_back, partial, gate_up_grad)
    gate_up_back = Scatter(
        lambda slot, left=normed_two, right=gate_up_late: transpose_by(
            left[:, slot * depth : (slot + 1) * depth], right
        ),
        count,
    )
    parts = [partial[i * own_rows : (i + 1) * own_rows] for i in range(2 * MICRO_BATCHES)]
    from_other = swap_core(jnp.concatenate(parts[1::2]))
    chips = [
        (parts[2 * i].astype(f32) + from_other[i * own_rows : (i + 1) * own_rows].astype(f32)).astype(
            bf16
        )
        for i in range(MICRO_BATCHES)
    ]
    summed_parts = [part.astype(f32) + swap_x(part).astype(f32) for part in chips]
    (hidden_late,) = gate_up_back.issue(hidden_low)
    hidden_late = pump(down_back, hidden_late)
    parts = [hidden_late[i * own_rows : (i + 1) * own_rows] for i in range(2 * MICRO_BATCHES)]
    mlp_other = by_transpose(jnp.concatenate(parts[1::2]), down_turned).astype(bf16)
    mlp_own = by_transpose(jnp.concatenate(parts[::2]), down_turned).astype(bf16)
    mlp_out = across(mlp_other, mlp_own)

    middle_grads, middle_lows = [], []
    in_grads, query_gain, key_gain_sums, joins, far_grads, kv_grads = [], [], [], [], [], []
    for micro in range(MICRO_BATCHES):
        base = micro * block_rows
        own, other = slice(base, base + own_rows), slice(base + own_rows, base + block_rows)
        summed = summed_parts[micro]
        if micro == 0:
            summed = drain(down_back, summed)
            summed = pump(gate_up_back, summed)
        else:
            kv_grads[0], summed = pump(gate_up_back, kv_grads[0], summed)
        middle_back, _ = rms_back(middles[micro], recips_two[micro], gain_mlp, summed)
        middle_grad = upstream_low[own].astype(f32) + middle_back
        middle_grads.append(middle_grad)
        own_low = middle_grad.astype(bf16)
        middle_lows.append(jnp.concatenate([own_low, swap_core(own_low)], axis=0))
        gated_grad = product(middle_lows[micro], out_turned)
        query_grad, far_grad, kv_grad, logit_grad, query_terms = pl.pallas_call(
            functools.partial(attend_back_kernel, (micro,) + sizes),
            out_shape=(
                jax.ShapeDtypeStruct((block_rows, query_cols), bf16),
                jax.ShapeDtypeStruct((block_rows, 2 * key_cols), bf16),
                jax.ShapeDtypeStruct((block_rows, 2 * key_cols), f32),
                jax.ShapeDtypeStruct((block_rows, extra), bf16),
                jax.ShapeDtypeStruct((8, head_dim), f32),
            ),
            grid_spec=pltpu.PrefetchScalarGridSpec(
                num_scalar_prefetch=1,
                grid=(1,),
                in_specs=[
                    at_row(micro, block_rows, query_cols),
                    at_row(micro, block_rows, 2 * key_cols),
                    at_row(micro, block_rows, 2 * key_cols),
                    at_row(micro, block_rows, 2),
                    at_row(micro, 1, 2, block_rows),
                    at_row(micro, block_rows, extra),
                    at_row(micro, block_rows, query_cols),
                    at_row(micro, block_rows, extra),
                    at_row(0, block_rows, query_cols),
                    at_row(micro, block_rows, query_cols),
                    at_row(micro, block_rows, head_dim),
                    at_row(micro, block_rows, head_dim),
                    whole(2, head_dim),
                ],
                out_specs=(
                    at_row(0, block_rows, query_cols),
                    at_row(0, block_rows, 2 * key_cols),
                    at_row(0, block_rows, 2 * key_cols),
                    at_row(0, block_rows, extra),
                    at_row(0, 8, head_dim),
                ),
            ),
            compiler_params=params,
            cost_estimate=cost(
                5 * pairs, block_rows * query_cols * 30, pairs // head_dim // 2
            ),
            name="attend_back",
        )(
            prompts,
            rotated_queries,
            own_kv,
            far_kv,
            spot_cols,
            spot_rows,
            head_gate,
            attended,
            log_totals,
            gated_grad,
            projected,
            cosine,
            sine,
            head_gain,
        )
        query_gain.append(query_terms[0])
        far_grads.append(far_grad)
        joins.append((query_grad, logit_grad))
        kv_grads.append(kv_grad)
    far_grads[1] = settle(gate_up_back, far_grads[1])
    arrived = [
        lax.ppermute(
            jnp.where(offset == apart, far_grads[0], far_grads[1]),
            "dp",
            group_route(apart, (apart, (GROUP_DEVICES - 1) ^ apart)),
        )
        for apart in (1, 2, 3)
    ]
    mlp_out, kv_grads[1] = order(mlp_out, kv_grads[1])
    layer_own = (jnp.concatenate(middles) + mlp_out).astype(bf16)
    layer_own = layer_own.reshape(MICRO_BATCHES, own_rows, width)
    layer_out = place_back(layer_own, swap_core(layer_own), True, "place_layer")
    layer_out, kv_grads[0] = order(layer_out, kv_grads[0])
    *arrived, kv_grads[0], kv_grads[1] = pump(gate_up_back, *arrived, kv_grads[0], kv_grads[1])
    for micro in range(MICRO_BATCHES):
        query_grad, logit_grad = joins[micro]
        kv_grad = kv_grads[micro]
        in_grad, key_terms = pl.pallas_call(
            functools.partial(join_kernel, (micro, query_cols, key_cols, head_dim)),
            out_shape=(
                jax.ShapeDtypeStruct((block_rows, joined), bf16),
                jax.ShapeDtypeStruct((8, head_dim), f32),
            ),
            grid_spec=pltpu.PrefetchScalarGridSpec(
                num_scalar_prefetch=1,
                grid=(1,),
                in_specs=[
                    at_row(0, block_rows, query_cols),
                    at_row(0, block_rows, 2 * key_cols),
                    at_row(0, block_rows, 2 * key_cols),
                    at_row(0, block_rows, 2 * key_cols),
                    at_row(0, block_rows, 2 * key_cols),
                    at_row(0, block_rows, extra),
                    pl.BlockSpec(
                        (block_rows, key_cols),
                        lambda i, flag, micro=micro: (micro, query_cols // key_cols),
                    ),
                    at_row(micro, block_rows, head_dim),
                    at_row(micro, block_rows, head_dim),
                    whole(2, head_dim),
                ],
                out_specs=(at_row(0, block_rows, joined), at_row(0, 8, head_dim)),
            ),
            compiler_params=params,
            cost_estimate=cost(1024, 1024),
            name="join",
        )(
            prompts,
            query_grad,
            kv_grad,
            *arrived,
            logit_grad,
            projected,
            cosine,
            sine,
            head_gain,
        )
        in_grads.append(in_grad)
        key_gain_sums.append(key_terms[0])
    in_back = Scatter(
        lambda slot, right=jnp.concatenate(in_grads), middle_low=jnp.concatenate(
            middle_lows
        ): jnp.concatenate(
            [
                transpose_by(normed_one[:, slot * depth : (slot + 1) * depth], right),
                transpose_by(middle_low[:, slot * depth : (slot + 1) * depth], gated_all),
            ],
            axis=1,
        ),
        count,
    )
    in_grads = in_back.issue(*in_grads)
    query_gain, key_gain_sum = query_gain[0] + query_gain[1], key_gain_sums[0] + key_gain_sums[1]
    head_gains = jnp.stack([query_gain, key_gain_sum])
    head_gains = head_gains + swap_core(head_gains)
    head_gains = head_gains + swap_x(head_gains)
    first, second, head_gains = settle(gate_up_back, *in_grads, head_gains)
    first = by_transpose(first, in_full).astype(bf16)
    second = by_transpose(second, in_full).astype(bf16)
    chips = [chip_sum(partial[own_rows:], partial[:own_rows]) for partial in (first, second)]
    from_x = [swap_x(chip) for chip in chips]
    chips[1], head_gains = pump(in_back, chips[1], head_gains)
    level, turn = 1, 0
    while level < count // 2:
        arrived_gains, from_x[turn] = pump(in_back, swap_dp(head_gains, level), from_x[turn])
        head_gains = head_gains + arrived_gains
        level, turn = 2 * level, min(turn + 1, MICRO_BATCHES - 1)
    input_rows = []
    for micro in range(MICRO_BATCHES):
        own = slice(micro * block_rows, micro * block_rows + own_rows)
        summed = chips[micro].astype(f32) + from_x[micro].astype(f32)
        input_back, _ = rms_back(inputs[own], recip_one[own], gain_attn, summed)
        input_rows.append(middle_grads[micro] + input_back)
    input_own = jnp.stack(input_rows)
    tokens_grad = place_back(input_own, swap_core(input_own), True, "place_tokens")

    arrived_gains, tokens_grad = pump(in_back, swap_dp(head_gains, level), tokens_grad)
    head_gains = head_gains + arrived_gains
    tokens_grad = drain(in_back, tokens_grad)
    drain(gate_up_back)

    gate_up_grad = gate_up_back.total()
    in_total = in_back.total()
    in_weight_grad, out_weight_grad = in_total[:, :joined], in_total[:, joined:].T
    mlp_sum = jnp.sum(
        gate_up_grad[:, :hidden_units] * gate_weight.astype(f32)
        + gate_up_grad[:, hidden_units:] * up_weight.astype(f32),
        axis=1,
    )
    used = first_gain
    attn_sum = jnp.sum(in_weight_grad[:, :used] * packed[:, :used].astype(f32), axis=1)
    gains = jnp.stack([attn_sum, mlp_sum])
    for swap in (swap_core, swap_x):
        gains = gains + swap(gains)
    return (
        layer_out,
        tokens_grad,
        in_weight_grad[:, :query_cols],
        in_weight_grad[:, query_cols : query_cols + key_cols],
        in_weight_grad[:, query_cols + key_cols : query_cols + 2 * key_cols],
        in_weight_grad[:, query_cols + 2 * key_cols : query_cols + 2 * key_cols + head_count],
        out_weight_grad,
        gate_up_grad[:, :hidden_units],
        gate_up_grad[:, hidden_units:],
        down_back.total(),
        gains[0] / norm_attn.astype(f32),
        gains[1] / norm_mlp.astype(f32),
        head_gains[0],
        head_gains[1],
    )


def solution(mesh):
    rows, weight, turned = P("dp", None), P("dp", "mp"), P("mp", "dp")
    weights = (weight, weight, weight, weight, turned, weight, weight, turned)
    placed = (rows, rows) + weights + (P("dp"), P("dp"), P(), P())
    return jax.shard_map(
        on_device, mesh=mesh, in_specs=placed + (P(),), out_specs=placed, check_vma=False
    )
```

time: 951 us -> 717 us (0.75)
  Pallas kernels: 0 us -> 93 us
  waiting for transfers between devices: 352 us -> 262 us
  other arithmetic: 133 us -> 62.4 us
  matrix products: 212 us -> 150 us
  local copies, waits for them, and re-layouts: 126 us -> 64.5 us
  starting transfers between devices: 113 us -> 72.6 us
    pallas_call x0 -> x10, Pallas kernels: none -> 93 us  [the longest x2 31 us: on_device(): pl.pallas_call(functools.partial(attend_back_kernel, (micro,) + sizes), o...]
    ppermute x70 -> x39, waiting for transfers between devices: 213 us -> 123 us  [ring_step(): return lax.ppermute(block, 'dp', route)]
    ppermute x8 -> x9, waiting for transfers between devices: 111 us -> 74.2 us  [swap_x(): lax.ppermute(block, 'mp', [(i, i ^ 2) for i in range(lax.axis_size('mp'))])]
    ppermute x70 -> x39, starting transfers between devices: 78.9 us -> 43.4 us  [ring_step(): return lax.ppermute(block, 'dp', route)]
    ppermute x13 -> x7, waiting for transfers between devices: 25.6 us -> 56.1 us  [the longest x1 34.4 us: on_device(): by_both = lax.ppermute(sent, 'dp', group_route(3, (0, 3)))]
    dot_general x12 -> x0, matrix products: 26.4 us -> none  [the longest x2 5.96 us: on_device(): jnp.einsum('mhzk,ihk->hzmi', group_gradient, gathered_values, preferred_e...]
    slice x23 -> x11, local copies, waits for them, and re-layouts: 25.6 us -> 0.92 us  [the longest x4 0.22 us: issue(): ahead, behind = (ahead[:, :self.cut], behind[:, self.cut:])]
    dot_general x11 -> x9, matrix products: 67.1 us -> 43.6 us  [by_transpose(): lax.dot_general(left_side, right_side, (((1,), (1,)), ((), ())), preferre...]
  transfers between devices with their start and end apart: 107 -> 71, of which waited for: 42 -> 39; matrix products, arithmetic and copies ran while one was open for 38% -> 30% of each run, Pallas kernels for 0% -> 13%
where the time goes in v2:
time: 717 us; the launch traced here: 707 us
  waiting for transfers between devices  262 us (37%)
  matrix products  150 us (21%)
  Pallas kernels  93 us (13%)
  starting transfers between devices  72.6 us (10%)
  local copies, waits for them, and re-layouts  64.5 us (9%)
  other arithmetic  62.4 us (9%)
    ppermute x39, waiting for transfers between devices, ring_step(): return lax.ppermute(block, 'dp', route)  123 us
    ppermute x9, waiting for transfers between devices, swap_x(): lax.ppermute(block, 'mp', [(i, i ^ 2) for i in range(lax.axis_size('mp'))])  74.2 us
    dot_general x32, matrix products, transpose_by(): lax.dot_general(left_side, right_side, (((0,), (0,)), ((), ())), preferre...  59.8 us
    unnamed x223, local copies, waits for them, and re-layouts  52.6 us
    dot_general x5, matrix products, product(): return jnp.dot(left_side, right_side, preferred_element_type=f32)  46.1 us
    dot_general x9, matrix products, by_transpose(): lax.dot_general(left_side, right_side, (((1,), (1,)), ((), ())), preferre...  43.6 us
    ppermute x39, starting transfers between devices, ring_step(): return lax.ppermute(block, 'dp', route)  43.4 us
    ppermute x1, waiting for transfers between devices, on_device(): by_both = lax.ppermute(sent, 'dp', group_route(3, (0, 3)))  34.4 us
  transfers between devices with their start and end apart: 71, of which 39 were waited for; matrix products, arithmetic and copies ran while one was open for 30% of the time, Pallas kernels for 13%

profile of v2, /device:TPU:0, one launch (start us, length us, event | category | flops | bytes accessed | tf_op | source)
XLA Modules:
  0.0 706.6 jit_solution(9155545135429990749)
XLA Ops:
  9.7 3.0 collective-permute-start.1
  17.6 7.4 %bring_tokens.1 = bf16[2,2,256,2048]{3,2,1,0:T(8,128)(2,1)} custom-call(s32[8]{0:T(128)} %gather_fusion, s32[1]{0:T(128)} %bitcast.1.core_ref, bf16[2,2,256,2048]{3,2,1,0:T(8,128)(2,1)} %bitcast.144), custom_call_target="tpu_custom_call" | custom-call | bytes 8388608 | tf_op jit(solution)/shard_map/bring_tokens/pallas_call | solution.py:472
  25.8 6.2 collective-permute-done.1
  37.3 3.1 multiply_reduce_fusion
  40.4 12.7 %collective-permute-done.2 = bf16[256,1664]{1,0:T(8,128)(2,1)S(1)} collective-permute-done((bf16[256,1664]{1,0:T(8,128)(2,1)}, bf16[256,1664]{1,0:T(8,128)(2,1)S(1)}, u32[]{:S(2)}, u32[]{:S(2)}) %collective-permute-start.2) | collective-permute-done | bytes 852000 | tf_op jit(solution)/shard_map/ppermute | solution.py:70
  57.7 14.4 %collective-permute-done.4 = bf16[256,1664]{1,0:T(8,128)(2,1)S(1)} collective-permute-done((bf16[256,1664]{1,0:T(8,128)(2,1)S(1)}, bf16[256,1664]{1,0:T(8,128)(2,1)S(1)}, u32[]{:S(2)}, u32[]{:S(2)}) %collective-permute-start.4) | collective-permute-done | bytes 852000 | tf_op jit(solution)/shard_map/ppermute | solution.py:70
  81.2 4.6 collective-permute-done.7
  92.1 7.2 %fusion.118.proj_ref = f32[1024,1152]{1,0:T(8,128)} fusion(bf16[1024,2048]{1,0:T(8,128)(2,1)S(1)} %multiply_convert_fusion, bf16[2048,1152]{1,0:T(8,128)(2,1)S(1)} %fusion.40), kind=kOutput, calls=%fused_computation.311 | convolution fusion | flops 4831838208 | bytes 13631488 | tf_op jit(solution)/shard_map/dot_general | solution.py:21
  99.3 6.5 heads.1
  107.9 2.4 collective-permute-start.12
  110.3 2.5 collective-permute-start.11
  115.0 34.4 %collective-permute-done.12 = bf16[512,512]{1,0:T(8,128)(2,1)S(1)} collective-permute-done((bf16[512,512]{1,0:T(8,128)(2,1)}, bf16[512,512]{1,0:T(8,128)(2,1)S(1)}, u32[]{:S(2)}, u32[]{:S(2)}) %collective-permute-start.12) | collective-permute-done | bytes 524320 | tf_op jit(solution)/shard_map/ppermute | solution.py:591
  149.4 7.3 %collective-permute-done.11 = bf16[512,512]{1,0:T(8,128)(2,1)} collective-permute-done((bf16[512,512]{1,0:T(8,128)(2,1)}, bf16[512,512]{1,0:T(8,128)(2,1)}, u32[]{:S(2)}, u32[]{:S(2)}) %collective-permute-start.11) | collective-permute-done | bytes 524320 | tf_op jit(solution)/shard_map/ppermute | solution.py:590
  159.2 2.5 collective-permute-start.13
  170.1 14.0 %attend.1 = (bf16[1024,512]{1,0:T(8,128)(2,1)}, f32[1024,512]{1,0:T(8,128)}, f32[1024,128]{1,0:T(8,128)}) custom-call(s32[2]{0:T(128)} %add_convert_fusion.5.flag_ref, bf16[1024,512]{1,0:T(8,128)(2,1)} %get-tuple-element.185.q_ref, bf16[1024,512]{1,0:T(8,128)(2,1)} %get-tuple-element.181.kv_ref, bf16[1024,512]{1,0:T(8,128)(2,1)} %pad_maximum_fusion.6.far_ref, ...), custom_call_target="tpu_custom_call" | custom-call | flops 2147483648 | bytes 6291456 | tf_op jit(solution)/shard_map/attend/pallas_call | solution.py:601
  184.1 7.5 %bring_cotangent.1 = bf16[2,2,256,2048]{3,2,1,0:T(8,128)(2,1)} custom-call(s32[8]{0:T(128)} %gather_fusion, s32[1]{0:T(128)} %bitcast.1.core_ref, bf16[2,2,256,2048]{3,2,1,0:T(8,128)(2,1)} %bitcast.145), custom_call_target="tpu_custom_call" | custom-call | bytes 8388608 | tf_op jit(solution)/shard_map/bring_cotangent/pallas_call | solution.py:472
  191.7 12.7 %collective-permute-done.13 = bf16[256,4608]{0,1:T(8,128)(2,1)} collective-permute-done((bf16[256,4608]{0,1:T(8,128)(2,1)}, bf16[256,4608]{0,1:T(8,128)(2,1)}, u32[]{:S(2)}, u32[]{:S(2)}) %collective-permute-start.13) | collective-permute-done | bytes 2359328 | tf_op jit(solution)/shard_map/ppermute | solution.py:70
  211.6 2.5 collective-permute-start.19
  215.2 19.5 %collective-permute-done.16 = bf16[256,2048]{1,0:T(8,128)(2,1)S(1)} collective-permute-done((bf16[256,2048]{1,0:T(8,128)(2,1)S(1)}, bf16[256,2048]{1,0:T(8,128)(2,1)S(1)}, u32[]{:S(2)}, u32[]{:S(2)}) %collective-permute-start.16) | collective-permute-done | bytes 1048608 | tf_op jit(solution)/shard_map/ppermute | solution.py:195
  234.7 21.7 %collective-permute-done.18 = bf16[256,2048]{1,0:T(8,128)(2,1)S(1)} collective-permute-done((bf16[256,2048]{1,0:T(8,128)(2,1)S(1)}, bf16[256,2048]{1,0:T(8,128)(2,1)S(1)}, u32[]{:S(2)}, u32[]{:S(2)}) %collective-permute-start.18) | collective-permute-done | bytes 1048608 | tf_op jit(solution)/shard_map/ppermute | solution.py:195
  259.3 5.8 collective-permute-done.19
  276.1 2.8 slice_dynamic-update-slice_fusion.5
  278.9 2.8 slice_dynamic-update-slice_fusion.4
  283.1 2.8 slice_dynamic-update-slice_fusion.2
  285.8 2.8 slice_dynamic-update-slice_fusion.1
  292.3 4.8 collective-permute-done.22
  298.8 18.1 %fusion.119 = f32[1024,3072]{1,0:T(8,128)} fusion(bf16[1024,2048]{1,0:T(8,128)(2,1)S(1)} %pad_maximum_fusion, bf16[2048,3072]{0,1:T(8,128)(2,1)} %fusion.32), kind=kOutput, calls=%fused_computation.312 | convolution fusion | flops 12884901888 | bytes 29360128 | tf_op jit(solution)/shard_map/dot_general | solution.py:21
  316.9 5.7 multiply_convert_fusion.3
  329.2 15.0 %multiply_convert_fusion.1 = (bf16[1024,1536]{1,0:T(8,128)(2,1)}, bf16[1024,1536]{1,0:T(8,128)(2,1)}) fusion(f32[1024,3072]{1,0:T(8,128)} %fusion.119, bf16[1024,2048]{1,0:T(8,128)(2,1)S(1)} %bitcast.131, bf16[2048,1536]{0,1:T(8,128)(2,1)} %slice_dynamic-update-slice_fusion.7), kind=kOutput, calls=%fused_computation.3 | convolution fusion | flops 6462898176 | bytes 29360128 | tf_op jit(solution)/shard_map/dot_general | solution.py:21
  353.7 19.7 %convolution_convert_fusion.1 = bf16[1024,2048]{1,0:T(8,128)(2,1)} fusion(bf16[1024,3072]{1,0:T(8,128)(2,1)S(1)} %constant_dynamic-update-slice_fusion.7, bf16[2048,3072]{0,1:T(8,128)(2,1)} %fusion.32), kind=kOutput, calls=%fused_computation.30 | convolution fusion | flops 12886999040 | bytes 23068672 | tf_op jit(solution)/shard_map/dot_general | solution.py:25
  383.3 14.3 %collective-permute-done.29 = bf16[1536,256]{1,0:T(8,128)(2,1)S(1)} collective-permute-done((bf16[1536,256]{1,0:T(8,128)(2,1)S(1)}, bf16[1536,256]{1,0:T(8,128)(2,1)S(1)}, u32[]{:S(2)}, u32[]{:S(2)}) %collective-permute-start.29) | collective-permute-done | bytes 786464 | tf_op jit(solution)/shard_map/ppermute | solution.py:70
  403.1 6.8 convolution_convert_fusion.4
  410.0 15.1 %collective-permute-done.37 = bf16[256,2048]{1,0:T(8,128)(2,1)S(1)} collective-permute-done((bf16[256,2048]{1,0:T(8,128)(2,1)S(1)}, bf16[256,2048]{1,0:T(8,128)(2,1)S(1)}, u32[]{:S(2)}, u32[]{:S(2)}) %collective-permute-start.37) | collective-permute-done | bytes 1048608 | tf_op jit(solution)/shard_map/ppermute | solution.py:195
  426.6 5.1 collective-permute-done.35
  431.7 3.0 fusion.4
  434.8 3.0 fusion.5
  442.2 5.1 add_convert_fusion
  452.4 15.3 %attend_back.2 = (bf16[512,512]{1,0:T(8,128)(2,1)}, bf16[512,512]{1,0:T(8,128)(2,1)}, f32[512,512]{1,0:T(8,128)}, bf16[512,128]{1,0:T(8,128)(2,1)}, f32[8,128]{1,0:T(8,128)}) custom-call(s32[2]{0:T(128)} %add_convert_fusion.5.flag_ref, bf16[1024,512]{1,0:T(8,128)(2,1)} %get-tuple-element.185.q_ref, bf16[1024,512]{1,0:T(8,128)(2,1)} %get-tuple-element.181.kv_ref, ...), custom_call_target="tpu_custom_call" | custom-call | flops 2684354560 | bytes 7864320 | tf_op jit(solution)/shard_map/attend_back/pallas_call | solution.py:714
  467.7 9.6 %collective-permute-done.38 = bf16[256,3072]{1,0:T(8,128)(2,1)} collective-permute-done((bf16[256,3072]{1,0:T(8,128)(2,1)}, bf16[256,3072]{1,0:T(8,128)(2,1)}, u32[]{:S(2)}, u32[]{:S(2)}) %collective-permute-start.38) | collective-permute-done | bytes 1572896 | tf_op jit(solution)/shard_map/ppermute | solution.py:70
  478.6 4.8 fusion.3
  483.3 4.7 fusion.6
  488.7 3.2 fusion.107
  495.2 5.0 convert_add_fusion
  500.2 3.5 fusion.21.grad_ref
  503.7 15.8 %attend_back.3 = (bf16[512,512]{1,0:T(8,128)(2,1)}, bf16[512,512]{1,0:T(8,128)(2,1)}, f32[512,512]{1,0:T(8,128)}, bf16[512,128]{1,0:T(8,128)(2,1)}, f32[8,128]{1,0:T(8,128)}) custom-call(s32[2]{0:T(128)} %add_convert_fusion.5.flag_ref, bf16[1024,512]{1,0:T(8,128)(2,1)} %get-tuple-element.185.q_ref, bf16[1024,512]{1,0:T(8,128)(2,1)} %get-tuple-element.181.kv_ref, ...), custom_call_target="tpu_custom_call" | custom-call | flops 2684354560 | bytes 7864320 | tf_op jit(solution)/shard_map/attend_back/pallas_call | solution.py:714
  519.5 2.9 fusion.1
  522.5 2.8 pad_maximum_fusion.1
  532.9 2.6 collective-permute-start.48
  538.2 4.6 fusion.7
  542.8 4.6 fusion.8
  547.3 7.2 %place_layer.1 = bf16[2,2,256,2048]{3,2,1,0:T(8,128)(2,1)} custom-call(s32[8]{0:T(128)} %gather_fusion, s32[1]{0:T(128)} %bitcast.1.core_ref, bf16[2,256,2048]{2,1,0:T(8,128)(2,1)} %bitcast.139, bf16[2,256,2048]{2,1,0:T(8,128)(2,1)} %collective-permute-done.43.other_ref), custom_call_target="tpu_custom_call" | custom-call | flops 1024 | bytes 1024 | tf_op jit(solution)/shard_map/place_layer/pallas_call | solution.py:505
  554.6 6.1 collective-permute-done.46.one_ref
  562.7 4.7 join.2
  567.4 4.9 join.3
  580.2 18.0 %collective-permute-done.51 = bf16[256,3072]{1,0:T(8,128)(2,1)} collective-permute-done((bf16[256,3072]{1,0:T(8,128)(2,1)}, bf16[256,3072]{1,0:T(8,128)(2,1)}, u32[]{:S(2)}, u32[]{:S(2)}) %collective-permute-start.51) | collective-permute-done | bytes 1572896 | tf_op jit(solution)/shard_map/ppermute | solution.py:70
  598.2 5.9 convolution_convert_fusion.3
  604.3 3.2 convolution_convert_fusion.2
  620.8 12.9 %collective-permute-done.58 = f32[2,128]{1,0:T(2,128)S(1)} collective-permute-done((f32[2,128]{1,0:T(2,128)S(1)}, f32[2,128]{1,0:T(2,128)S(1)}, u32[]{:S(2)}, u32[]{:S(2)}) %collective-permute-start.58) | collective-permute-done | bytes 1056 | tf_op jit(solution)/shard_map/ppermute | solution.py:200
  644.6 14.2 %collective-permute-done.64 = bf16[256,2048]{1,0:T(8,128)(2,1)S(1)} collective-permute-done((bf16[256,2048]{1,0:T(8,128)(2,1)S(1)}, bf16[256,2048]{1,0:T(8,128)(2,1)S(1)}, u32[]{:S(2)}, u32[]{:S(2)}) %collective-permute-start.64) | collective-permute-done | bytes 1048608 | tf_op jit(solution)/shard_map/ppermute | solution.py:195
  665.5 3.0 copy-done.20
  668.9 3.2 fusion.9
  677.5 4.1 fusion.2
  685.1 9.7 %place_tokens.1 = f32[2,2,256,2048]{3,2,1,0:T(8,128)} custom-call(s32[8]{0:T(128)} %gather_fusion, s32[1]{0:T(128)} %bitcast.1.core_ref, f32[2,256,2048]{2,1,0:T(8,128)} %copy-done.15, f32[2,256,2048]{2,1,0:T(8,128)} %collective-permute-done.68.other_ref), custom_call_target="tpu_custom_call" | custom-call | flops 1024 | bytes 1024 | tf_op jit(solution)/shard_map/place_tokens/pallas_call | solution.py:505
  694.8 2.7 collective-permute-done.67
  (488 shorter events, 200.2 us)
Async XLA Ops:
  9.7 22.3 %collective-permute-start.1 = (bf16[256,1664]{1,0:T(8,128)(2,1)}, bf16[256,1664]{1,0:T(8,128)(2,1)}, u32[]{:S(2)}, u32[]{:S(2)}) collective-permute-start(bf16[256,1664]{1,0:T(8,128)(2,1)} %bitcast_dynamic-update-slice_fusion.1), channel_id=1, source_target_pairs={{0,4},{8,0},{16,8},{24,16},{28,24},{20,28},{12,20},{4,12},{1,5},{9... | collective-permute-start | bytes 2555912 | tf_op jit(solution)/shard_map/ppermute | solution.py:70
  12.7 20.7 %collective-permute-start = (bf16[256,1664]{1,0:T(8,128)(2,1)}, bf16[256,1664]{1,0:T(8,128)(2,1)}, u32[]{:S(2)}, u32[]{:S(2)}) collective-permute-start(bf16[256,1664]{1,0:T(8,128)(2,1)} %bitcast_dynamic-update-slice_fusion.1), channel_id=1, source_target_pairs={{0,8},{8,16},{16,24},{24,28},{28,20},{20,12},{12,4},{4,0},{1,9},{9... | collective-permute-start | bytes 2555912 | tf_op jit(solution)/shard_map/ppermute | solution.py:70
  33.4 19.7 %collective-permute-start.2 = (bf16[256,1664]{1,0:T(8,128)(2,1)}, bf16[256,1664]{1,0:T(8,128)(2,1)S(1)}, u32[]{:S(2)}, u32[]{:S(2)}) collective-permute-start(bf16[256,1664]{1,0:T(8,128)(2,1)} %collective-permute-done), channel_id=1, source_target_pairs={{0,8},{8,16},{16,24},{24,28},{28,20},{20,12},{12,4},{4,0},{1,9},{9... | collective-permute-start | bytes 2555912 | tf_op jit(solution)/shard_map/ppermute | solution.py:70
  33.7 19.7 %collective-permute-start.3 = (bf16[256,1664]{1,0:T(8,128)(2,1)}, bf16[256,1664]{1,0:T(8,128)(2,1)S(1)}, u32[]{:S(2)}, u32[]{:S(2)}) collective-permute-start(bf16[256,1664]{1,0:T(8,128)(2,1)} %collective-permute-done.1), channel_id=1, source_target_pairs={{0,4},{8,0},{16,8},{24,16},{28,24},{20,28},{12,20},{4,12},{1,5},{9... | collective-permute-start | bytes 2555912 | tf_op jit(solution)/shard_map/ppermute | solution.py:70
  53.5 18.6 %collective-permute-start.4 = (bf16[256,1664]{1,0:T(8,128)(2,1)S(1)}, bf16[256,1664]{1,0:T(8,128)(2,1)S(1)}, u32[]{:S(2)}, u32[]{:S(2)}) collective-permute-start(bf16[256,1664]{1,0:T(8,128)(2,1)S(1)} %collective-permute-done.2), channel_id=1, source_target_pairs={{0,8},{8,16},{16,24},{24,28},{28,20},{20,12},{12,4},{4,0},{1,9},{9... | collective-permute-start | bytes 2555912 | tf_op jit(solution)/shard_map/ppermute | solution.py:70
  55.0 18.2 %collective-permute-start.5 = (bf16[256,1664]{1,0:T(8,128)(2,1)S(1)}, bf16[256,1664]{1,0:T(8,128)(2,1)S(1)}, u32[]{:S(2)}, u32[]{:S(2)}) collective-permute-start(bf16[256,1664]{1,0:T(8,128)(2,1)S(1)} %collective-permute-done.3), channel_id=1, source_target_pairs={{0,4},{8,0},{16,8},{24,16},{28,24},{20,28},{12,20},{4,12},{1,5},{9... | collective-permute-start | bytes 2555912 | tf_op jit(solution)/shard_map/ppermute | solution.py:70
  73.3 7.8 %collective-permute-start.6 = (bf16[256,768]{1,0:T(8,128)(2,1)S(1)}, bf16[256,768]{1,0:T(8,128)(2,1)S(1)}, u32[]{:S(2)}, u32[]{:S(2)}) collective-permute-start(bf16[256,768]{1,0:T(8,128)(2,1)S(1)} %slice.383), channel_id=1, source_target_pairs={{0,8},{8,16},{16,24},{24,28},{28,20},{20,12},{12,4},{4,0},{1,9},{9... | collective-permute-start | bytes 1179656 | tf_op jit(solution)/shard_map/ppermute | solution.py:70
  75.0 10.7 %collective-permute-start.7 = (bf16[256,896]{1,0:T(8,128)(2,1)S(1)}, bf16[256,896]{1,0:T(8,128)(2,1)S(1)}, u32[]{:S(2)}, u32[]{:S(2)}) collective-permute-start(bf16[256,896]{1,0:T(8,128)(2,1)S(1)} %slice.384), channel_id=1, source_target_pairs={{0,4},{8,0},{16,8},{24,16},{28,24},{20,28},{12,20},{4,12},{1,5},{9... | collective-permute-start | bytes 1376264 | tf_op jit(solution)/shard_map/ppermute | solution.py:70
  85.7 73.5 %collective-permute-start.9 = (bf16[256,4608]{0,1:T(8,128)(2,1)S(1)}, bf16[256,4608]{0,1:T(8,128)(2,1)}, u32[]{:S(2)}, u32[]{:S(2)}) collective-permute-start(bf16[256,4608]{0,1:T(8,128)(2,1)S(1)} %pad_maximum_fusion.3), channel_id=1, source_target_pairs={{0,4},{8,0},{16,8},{24,16},{28,24},{20,28},{12,20},{4,12},{1,5},{9... | collective-permute-start | bytes 7077896 | tf_op jit(solution)/shard_map/ppermute | solution.py:70
  86.2 73.0 %collective-permute-start.8 = (bf16[256,4608]{0,1:T(8,128)(2,1)S(1)}, bf16[256,4608]{0,1:T(8,128)(2,1)}, u32[]{:S(2)}, u32[]{:S(2)}) collective-permute-start(bf16[256,4608]{0,1:T(8,128)(2,1)S(1)} %pad_maximum_fusion.3), channel_id=1, source_target_pairs={{0,8},{8,16},{16,24},{24,28},{28,20},{20,12},{12,4},{4,0},{1,9},{9... | collective-permute-start | bytes 7077896 | tf_op jit(solution)/shard_map/ppermute | solution.py:70
  107.9 41.5 %collective-permute-start.12 = (bf16[512,512]{1,0:T(8,128)(2,1)}, bf16[512,512]{1,0:T(8,128)(2,1)S(1)}, u32[]{:S(2)}, u32[]{:S(2)}) collective-permute-start(bf16[512,512]{1,0:T(8,128)(2,1)} %slice_select_fusion), channel_id=1, source_target_pairs={{0,12},{12,0},{16,28},{28,16},{1,13},{13,1},{17,29},{29,17},{2,14}... | collective-permute-start | bytes 1572872 | tf_op jit(solution)/shard_map/ppermute | solution.py:591
  110.3 46.3 %collective-permute-start.11 = (bf16[512,512]{1,0:T(8,128)(2,1)}, bf16[512,512]{1,0:T(8,128)(2,1)}, u32[]{:S(2)}, u32[]{:S(2)}) collective-permute-start(bf16[512,512]{1,0:T(8,128)(2,1)} %slice_select_fusion), channel_id=1, source_target_pairs={{0,8},{12,4},{16,24},{28,20},{1,9},{13,5},{17,25},{29,21},{2,10},{... | collective-permute-start | bytes 1572872 | tf_op jit(solution)/shard_map/ppermute | solution.py:590
  112.8 43.9 %collective-permute-start.10 = (bf16[512,512]{1,0:T(8,128)(2,1)}, bf16[512,512]{1,0:T(8,128)(2,1)}, u32[]{:S(2)}, u32[]{:S(2)}) collective-permute-start(bf16[512,512]{1,0:T(8,128)(2,1)} %slice_select_fusion), channel_id=1, source_target_pairs={{0,4},{12,8},{16,20},{28,24},{1,5},{13,9},{17,21},{29,25},{2,6},{1... | collective-permute-start | bytes 1572872 | tf_op jit(solution)/shard_map/ppermute | solution.py:589
  159.2 45.2 %collective-permute-start.13 = (bf16[256,4608]{0,1:T(8,128)(2,1)}, bf16[256,4608]{0,1:T(8,128)(2,1)}, u32[]{:S(2)}, u32[]{:S(2)}) collective-permute-start(bf16[256,4608]{0,1:T(8,128)(2,1)} %collective-permute-done.8), channel_id=1, source_target_pairs={{0,8},{8,16},{16,24},{24,28},{28,20},{20,12},{12,4},{4,0},{1,9},{9... | collective-permute-start | bytes 7077896 | tf_op jit(solution)/shard_map/ppermute | solution.py:70
  161.7 42.6 %collective-permute-start.14 = (bf16[256,4608]{0,1:T(8,128)(2,1)}, bf16[256,4608]{0,1:T(8,128)(2,1)}, u32[]{:S(2)}, u32[]{:S(2)}) collective-permute-start(bf16[256,4608]{0,1:T(8,128)(2,1)} %collective-permute-done.9), channel_id=1, source_target_pairs={{0,4},{8,0},{16,8},{24,16},{28,24},{20,28},{12,20},{4,12},{1,5},{9... | collective-permute-start | bytes 7077896 | tf_op jit(solution)/shard_map/ppermute | solution.py:70
  208.6 26.1 %collective-permute-start.16 = (bf16[256,2048]{1,0:T(8,128)(2,1)S(1)}, bf16[256,2048]{1,0:T(8,128)(2,1)S(1)}, u32[]{:S(2)}, u32[]{:S(2)}) collective-permute-start(bf16[256,2048]{1,0:T(8,128)(2,1)S(1)} %fusion.10), channel_id=1, source_target_pairs={{0,2},{1,3},{2,0},{3,1},{4,6},{5,7},{6,4},{7,5},{8,10},{9,11},{10,... | collective-permute-start | bytes 3145736 | tf_op jit(solution)/shard_map/ppermute | solution.py:195
  210.9 45.4 %collective-permute-start.18 = (bf16[256,2048]{1,0:T(8,128)(2,1)S(1)}, bf16[256,2048]{1,0:T(8,128)(2,1)S(1)}, u32[]{:S(2)}, u32[]{:S(2)}) collective-permute-start(bf16[256,2048]{1,0:T(8,128)(2,1)S(1)} %fusion.11), channel_id=1, source_target_pairs={{0,2},{1,3},{2,0},{3,1},{4,6},{5,7},{6,4},{7,5},{8,10},{9,11},{10,... | collective-permute-start | bytes 3145736 | tf_op jit(solution)/shard_map/ppermute | solution.py:195
  211.6 53.5 %collective-permute-start.19 = (bf16[256,4608]{0,1:T(8,128)(2,1)}, bf16[256,4608]{0,1:T(8,128)(2,1)S(1)}, u32[]{:S(2)}, u32[]{:S(2)}) collective-permute-start(bf16[256,4608]{0,1:T(8,128)(2,1)} %collective-permute-done.13), channel_id=1, source_target_pairs={{0,8},{8,16},{16,24},{24,28},{28,20},{20,12},{12,4},{4,0},{1,9},{9... | collective-permute-start | bytes 7077896 | tf_op jit(solution)/shard_map/ppermute | solution.py:70
  214.1 52.9 %collective-permute-start.20 = (bf16[256,4608]{0,1:T(8,128)(2,1)}, bf16[256,4608]{0,1:T(8,128)(2,1)S(1)}, u32[]{:S(2)}, u32[]{:S(2)}) collective-permute-start(bf16[256,4608]{0,1:T(8,128)(2,1)} %collective-permute-done.14), channel_id=1, source_target_pairs={{0,4},{8,0},{16,8},{24,16},{28,24},{20,28},{12,20},{4,12},{1,5},{9... | collective-permute-start | bytes 7077896 | tf_op jit(solution)/shard_map/ppermute | solution.py:70
  259.3 30.8 %collective-permute-start.24 = (bf16[256,2048]{1,0:T(8,128)(2,1)S(1)}, bf16[256,2048]{1,0:T(8,128)(2,1)S(1)}, u32[]{:S(2)}, u32[]{:S(2)}) collective-permute-start(bf16[256,2048]{1,0:T(8,128)(2,1)S(1)} %get-tuple-element.416), channel_id=1, source_target_pairs={{0,1},{1,0},{2,3},{3,2},{4,5},{5,4},{6,7},{7,6},{8,9},{9,8},{10,11... | collective-permute-start | bytes 3145736 | tf_op jit(solution)/shard_map/ppermute | solution.py:191
  268.6 23.2 %collective-permute-start.23 = (bf16[256,2048]{1,0:T(8,128)(2,1)S(1)}, bf16[256,2048]{1,0:T(8,128)(2,1)S(1)}, u32[]{:S(2)}, u32[]{:S(2)}) collective-permute-start(bf16[256,2048]{1,0:T(8,128)(2,1)S(1)} %get-tuple-element.197), channel_id=1, source_target_pairs={{0,1},{1,0},{2,3},{3,2},{4,5},{5,4},{6,7},{7,6},{8,9},{9,8},{10,11... | collective-permute-start | bytes 3145736 | tf_op jit(solution)/shard_map/ppermute | solution.py:191
  268.7 28.4 %collective-permute-start.22 = (bf16[256,2304]{0,1:T(8,128)(2,1)S(1)}, bf16[256,2304]{0,1:T(8,128)(2,1)S(1)}, u32[]{:S(2)}, u32[]{:S(2)}) collective-permute-start(bf16[256,2304]{0,1:T(8,128)(2,1)S(1)} %slice.411), channel_id=1, source_target_pairs={{0,4},{8,0},{16,8},{24,16},{28,24},{20,28},{12,20},{4,12},{1,5},{9... | collective-permute-start | bytes 3538952 | tf_op jit(solution)/shard_map/ppermute | solution.py:70
  269.0 28.4 %collective-permute-start.21 = (bf16[256,2304]{0,1:T(8,128)(2,1)S(1)}, bf16[256,2304]{0,1:T(8,128)(2,1)S(1)}, u32[]{:S(2)}, u32[]{:S(2)}) collective-permute-start(bf16[256,2304]{0,1:T(8,128)(2,1)S(1)} %slice.410), channel_id=1, source_target_pairs={{0,8},{8,16},{16,24},{24,28},{28,20},{20,12},{12,4},{4,0},{1,9},{9... | collective-permute-start | bytes 3538952 | tf_op jit(solution)/shard_map/ppermute | solution.py:70
  326.8 19.2 %collective-permute-start.25 = (bf16[1536,256]{1,0:T(8,128)(2,1)}, bf16[1536,256]{1,0:T(8,128)(2,1)S(1)}, u32[]{:S(2)}, u32[]{:S(2)}) collective-permute-start(bf16[1536,256]{1,0:T(8,128)(2,1)} %convolution_convert_fusion.10), channel_id=1, source_target_pairs={{0,8},{8,16},{16,24},{24,28},{28,20},{20,12},{12,4},{4,0},{1,9},{9... | collective-permute-start | bytes 2359304 | tf_op jit(solution)/shard_map/ppermute | solution.py:70
  328.4 19.0 %collective-permute-start.26 = (bf16[1536,256]{1,0:T(8,128)(2,1)S(1)}, bf16[1536,256]{1,0:T(8,128)(2,1)S(1)}, u32[]{:S(2)}, u32[]{:S(2)}) collective-permute-start(bf16[1536,256]{1,0:T(8,128)(2,1)S(1)} %convolution_convert_fusion.9), channel_id=1, source_target_pairs={{0,4},{8,0},{16,8},{24,16},{28,24},{20,28},{12,20},{4,12},{1,5},{9... | collective-permute-start | bytes 2359304 | tf_op jit(solution)/shard_map/ppermute | solution.py:70
  350.5 22.9 %collective-permute-start.27 = (bf16[1536,256]{1,0:T(8,128)(2,1)S(1)}, bf16[1536,256]{1,0:T(8,128)(2,1)S(1)}, u32[]{:S(2)}, u32[]{:S(2)}) collective-permute-start(bf16[1536,256]{1,0:T(8,128)(2,1)S(1)} %fusion.14), channel_id=1, source_target_pairs={{0,8},{8,16},{16,24},{24,28},{28,20},{20,12},{12,4},{4,0},{1,9},{9... | collective-permute-start | bytes 2359304 | tf_op jit(solution)/shard_map/ppermute | solution.py:70
  351.8 21.7 %collective-permute-start.28 = (bf16[1536,256]{1,0:T(8,128)(2,1)S(1)}, bf16[1536,256]{1,0:T(8,128)(2,1)S(1)}, u32[]{:S(2)}, u32[]{:S(2)}) collective-permute-start(bf16[1536,256]{1,0:T(8,128)(2,1)S(1)} %fusion.15), channel_id=1, source_target_pairs={{0,4},{8,0},{16,8},{24,16},{28,24},{20,28},{12,20},{4,12},{1,5},{9... | collective-permute-start | bytes 2359304 | tf_op jit(solution)/shard_map/ppermute | solution.py:70
  377.1 23.9 %collective-permute-start.36 = (bf16[512,2048]{1,0:T(8,128)(2,1)S(1)}, bf16[512,2048]{1,0:T(8,128)(2,1)S(1)}, u32[]{:S(2)}, u32[]{:S(2)}) collective-permute-start(bf16[512,2048]{1,0:T(8,128)(2,1)S(1)} %pad_maximum_fusion.4), channel_id=1, source_target_pairs={{0,1},{1,0},{2,3},{3,2},{4,5},{5,4},{6,7},{7,6},{8,9},{9,8},{10,11... | collective-permute-start | bytes 6291464 | tf_op jit(solution)/shard_map/ppermute | solution.py:191
  377.2 20.4 %collective-permute-start.29 = (bf16[1536,256]{1,0:T(8,128)(2,1)S(1)}, bf16[1536,256]{1,0:T(8,128)(2,1)S(1)}, u32[]{:S(2)}, u32[]{:S(2)}) collective-permute-start(bf16[1536,256]{1,0:T(8,128)(2,1)S(1)} %fusion.13), channel_id=1, source_target_pairs={{0,8},{8,16},{16,24},{24,28},{28,20},{20,12},{12,4},{4,0},{1,9},{9... | collective-permute-start | bytes 2359304 | tf_op jit(solution)/shard_map/ppermute | solution.py:70
  378.4 20.4 %collective-permute-start.30 = (bf16[1536,256]{1,0:T(8,128)(2,1)S(1)}, bf16[1536,256]{1,0:T(8,128)(2,1)S(1)}, u32[]{:S(2)}, u32[]{:S(2)}) collective-permute-start(bf16[1536,256]{1,0:T(8,128)(2,1)S(1)} %fusion.16), channel_id=1, source_target_pairs={{0,4},{8,0},{16,8},{24,16},{28,24},{20,28},{12,20},{4,12},{1,5},{9... | collective-permute-start | bytes 2359304 | tf_op jit(solution)/shard_map/ppermute | solution.py:70
  381.2 50.5 %collective-permute-start.33 = (bf16[256,1536]{1,0:T(8,128)(2,1)S(1)}, bf16[256,1536]{1,0:T(8,128)(2,1)S(1)}, u32[]{:S(2)}, u32[]{:S(2)}) collective-permute-start(bf16[256,1536]{1,0:T(8,128)(2,1)S(1)} %get-tuple-element.226), channel_id=1, source_target_pairs={{0,8},{8,16},{16,24},{24,28},{28,20},{20,12},{12,4},{4,0},{1,9},{9... | collective-permute-start | bytes 2359304 | tf_op jit(solution)/shard_map/ppermute | solution.py:70
  382.4 49.3 %collective-permute-start.34 = (bf16[256,1536]{1,0:T(8,128)(2,1)S(1)}, bf16[256,1536]{1,0:T(8,128)(2,1)S(1)}, u32[]{:S(2)}, u32[]{:S(2)}) collective-permute-start(bf16[256,1536]{1,0:T(8,128)(2,1)S(1)} %get-tuple-element.227), channel_id=1, source_target_pairs={{0,4},{8,0},{16,8},{24,16},{28,24},{20,28},{12,20},{4,12},{1,5},{9... | collective-permute-start | bytes 2359304 | tf_op jit(solution)/shard_map/ppermute | solution.py:70
  399.8 31.9 %collective-permute-start.35 = (bf16[1536,256]{1,0:T(8,128)(2,1)S(1)}, bf16[1536,256]{1,0:T(8,128)(2,1)S(1)}, u32[]{:S(2)}, u32[]{:S(2)}) collective-permute-start(bf16[1536,256]{1,0:T(8,128)(2,1)S(1)} %fusion.12), channel_id=1, source_target_pairs={{0,4},{8,0},{16,8},{24,16},{28,24},{20,28},{12,20},{4,12},{1,5},{9... | collective-permute-start | bytes 2359304 | tf_op jit(solution)/shard_map/ppermute | solution.py:70
  401.7 23.4 %collective-permute-start.37 = (bf16[256,2048]{1,0:T(8,128)(2,1)S(1)}, bf16[256,2048]{1,0:T(8,128)(2,1)S(1)}, u32[]{:S(2)}, u32[]{:S(2)}) collective-permute-start(bf16[256,2048]{1,0:T(8,128)(2,1)S(1)} %get-tuple-element.394), channel_id=1, source_target_pairs={{0,2},{1,3},{2,0},{3,1},{4,6},{5,7},{6,4},{7,5},{8,10},{9,11},{10,... | collective-permute-start | bytes 3145736 | tf_op jit(solution)/shard_map/ppermute | solution.py:195
  409.9 32.3 %collective-permute-start.31 = (bf16[512,2048]{1,0:T(8,128)(2,1)S(1)}, bf16[512,2048]{1,0:T(8,128)(2,1)S(1)}, u32[]{:S(2)}, u32[]{:S(2)}) collective-permute-start(bf16[512,2048]{1,0:T(8,128)(2,1)S(1)} %convolution_convert_fusion.4), channel_id=1, source_target_pairs={{0,1},{1,0},{2,3},{3,2},{4,5},{5,4},{6,7},{7,6},{8,9},{9,8},{10,11... | collective-permute-start | bytes 6291464 | tf_op jit(solution)/shard_map/ppermute | solution.py:191
  425.2 23.3 %collective-permute-start.41 = (bf16[256,2048]{1,0:T(8,128)(2,1)S(1)}, bf16[256,2048]{1,0:T(8,128)(2,1)S(1)}, u32[]{:S(2)}, u32[]{:S(2)}) collective-permute-start(bf16[256,2048]{1,0:T(8,128)(2,1)S(1)} %get-tuple-element.393), channel_id=1, source_target_pairs={{0,2},{1,3},{2,0},{3,1},{4,6},{5,7},{6,4},{7,5},{8,10},{9,11},{10,... | collective-permute-start | bytes 3145736 | tf_op jit(solution)/shard_map/ppermute | solution.py:195
  440.2 9.9 %collective-permute-start.40 = (bf16[256,2048]{1,0:T(8,128)(2,1)S(1)}, bf16[256,2048]{1,0:T(8,128)(2,1)S(1)}, u32[]{:S(2)}, u32[]{:S(2)}) collective-permute-start(bf16[256,2048]{1,0:T(8,128)(2,1)S(1)} %get-tuple-element.377), channel_id=1, source_target_pairs={{0,1},{1,0},{2,3},{3,2},{4,5},{5,4},{6,7},{7,6},{8,9},{9,8},{10,11... | collective-permute-start | bytes 3145736 | tf_op jit(solution)/shard_map/ppermute | solution.py:191
  440.2 37.1 %collective-permute-start.38 = (bf16[256,3072]{1,0:T(8,128)(2,1)}, bf16[256,3072]{1,0:T(8,128)(2,1)}, u32[]{:S(2)}, u32[]{:S(2)}) collective-permute-start(bf16[256,3072]{1,0:T(8,128)(2,1)} %fusion.4), channel_id=1, source_target_pairs={{0,8},{8,16},{16,24},{24,28},{28,20},{20,12},{12,4},{4,0},{1,9},{9... | collective-permute-start | bytes 4718600 | tf_op jit(solution)/shard_map/ppermute | solution.py:70
  441.7 36.8 %collective-permute-start.39 = (bf16[256,3072]{1,0:T(8,128)(2,1)}, bf16[256,3072]{1,0:T(8,128)(2,1)}, u32[]{:S(2)}, u32[]{:S(2)}) collective-permute-start(bf16[256,3072]{1,0:T(8,128)(2,1)} %fusion.5), channel_id=1, source_target_pairs={{0,4},{8,0},{16,8},{24,16},{28,24},{20,28},{12,20},{4,12},{1,5},{9... | collective-permute-start | bytes 4718600 | tf_op jit(solution)/shard_map/ppermute | solution.py:70
  447.3 47.9 %collective-permute-start.32 = (bf16[512,2048]{1,0:T(8,128)(2,1)}, bf16[512,2048]{1,0:T(8,128)(2,1)}, u32[]{:S(2)}, u32[]{:S(2)}) collective-permute-start(bf16[512,2048]{1,0:T(8,128)(2,1)} %add_convert_fusion), channel_id=1, source_target_pairs={{0,2},{1,3},{2,0},{3,1},{4,6},{5,7},{6,4},{7,5},{8,10},{9,11},{10,... | collective-permute-start | bytes 6291464 | tf_op jit(solution)/shard_map/ppermute | solution.py:195
  492.0 8.2 %collective-permute-start.42 = (bf16[256,2048]{1,0:T(8,128)(2,1)S(1)}, bf16[256,2048]{1,0:T(8,128)(2,1)}, u32[]{:S(2)}, u32[]{:S(2)}) collective-permute-start(bf16[256,2048]{1,0:T(8,128)(2,1)S(1)} %get-tuple-element.375), channel_id=1, source_target_pairs={{0,1},{1,0},{2,3},{3,2},{4,5},{5,4},{6,7},{7,6},{8,9},{9,8},{10,11... | collective-permute-start | bytes 3145736 | tf_op jit(solution)/shard_map/ppermute | solution.py:191
  492.0 39.6 %collective-permute-start.44 = (bf16[256,3072]{1,0:T(8,128)(2,1)}, bf16[256,3072]{1,0:T(8,128)(2,1)}, u32[]{:S(2)}, u32[]{:S(2)}) collective-permute-start(bf16[256,3072]{1,0:T(8,128)(2,1)} %fusion.3), channel_id=1, source_target_pairs={{0,8},{8,16},{16,24},{24,28},{28,20},{20,12},{12,4},{4,0},{1,9},{9... | collective-permute-start | bytes 4718600 | tf_op jit(solution)/shard_map/ppermute | solution.py:70
  492.4 39.3 %collective-permute-start.45 = (bf16[256,3072]{1,0:T(8,128)(2,1)}, bf16[256,3072]{1,0:T(8,128)(2,1)}, u32[]{:S(2)}, u32[]{:S(2)}) collective-permute-start(bf16[256,3072]{1,0:T(8,128)(2,1)} %fusion.6), channel_id=1, source_target_pairs={{0,4},{8,0},{16,8},{24,16},{28,24},{20,28},{12,20},{4,12},{1,5},{9... | collective-permute-start | bytes 4718600 | tf_op jit(solution)/shard_map/ppermute | solution.py:70
  522.4 25.0 %collective-permute-start.43 = (bf16[2,256,2048]{2,1,0:T(8,128)(2,1)S(1)}, bf16[2,256,2048]{2,1,0:T(8,128)(2,1)}, u32[]{:S(2)}, u32[]{:S(2)}) collective-permute-start(bf16[2,256,2048]{2,1,0:T(8,128)(2,1)S(1)} %bitcast.138), channel_id=1, source_target_pairs={{0,1},{1,0},{2,3},{3,2},{4,5},{5,4},{6,7},{7,6},{8,9},{9,8},{10,11... | collective-permute-start | bytes 6291464 | tf_op jit(solution)/shard_map/ppermute | solution.py:191
  532.9 21.7 %collective-permute-start.48 = (bf16[512,512]{1,0:T(8,128)(2,1)}, bf16[512,512]{1,0:T(8,128)(2,1)S(1)}, u32[]{:S(2)}, u32[]{:S(2)}) collective-permute-start(bf16[512,512]{1,0:T(8,128)(2,1)} %get-tuple-element.409), channel_id=1, source_target_pairs={{12,0},{0,12},{28,16},{16,28},{13,1},{1,13},{29,17},{17,29},{14,2}... | collective-permute-start | bytes 1572872 | tf_op jit(solution)/shard_map/ppermute | solution.py:776
  535.6 19.0 %collective-permute-start.47 = (bf16[512,512]{1,0:T(8,128)(2,1)}, bf16[512,512]{1,0:T(8,128)(2,1)S(1)}, u32[]{:S(2)}, u32[]{:S(2)}) collective-permute-start(bf16[512,512]{1,0:T(8,128)(2,1)} %get-tuple-element.410), channel_id=1, source_target_pairs={{8,0},{4,12},{24,16},{20,28},{9,1},{5,13},{25,17},{21,29},{10,2},{... | collective-permute-start | bytes 1572872 | tf_op jit(solution)/shard_map/ppermute | solution.py:776
  536.9 23.8 %collective-permute-start.46 = (bf16[512,512]{1,0:T(8,128)(2,1)}, bf16[512,512]{1,0:T(8,128)(2,1)S(1)}, u32[]{:S(2)}, u32[]{:S(2)}) collective-permute-start(bf16[512,512]{1,0:T(8,128)(2,1)} %get-tuple-element.411), channel_id=1, source_target_pairs={{4,0},{8,12},{20,16},{24,28},{5,1},{9,13},{21,17},{25,29},{6,2},{1... | collective-permute-start | bytes 1572872 | tf_op jit(solution)/shard_map/ppermute | solution.py:776
  560.7 37.6 %collective-permute-start.51 = (bf16[256,3072]{1,0:T(8,128)(2,1)}, bf16[256,3072]{1,0:T(8,128)(2,1)}, u32[]{:S(2)}, u32[]{:S(2)}) collective-permute-start(bf16[256,3072]{1,0:T(8,128)(2,1)} %fusion.7), channel_id=1, source_target_pairs={{0,8},{8,16},{16,24},{24,28},{28,20},{20,12},{12,4},{4,0},{1,9},{9... | collective-permute-start | bytes 4718600 | tf_op jit(solution)/shard_map/ppermute | solution.py:70
  560.7 37.6 %collective-permute-start.52 = (bf16[256,3072]{1,0:T(8,128)(2,1)}, bf16[256,3072]{1,0:T(8,128)(2,1)}, u32[]{:S(2)}, u32[]{:S(2)}) collective-permute-start(bf16[256,3072]{1,0:T(8,128)(2,1)} %fusion.8), channel_id=1, source_target_pairs={{0,4},{8,0},{16,8},{24,16},{28,24},{20,28},{12,20},{4,12},{1,5},{9... | collective-permute-start | bytes 4718600 | tf_op jit(solution)/shard_map/ppermute | solution.py:70
  577.8 32.6 %collective-permute-start.49 = (bf16[256,768]{1,0:T(8,128)(2,1)S(1)}, bf16[256,768]{1,0:T(8,128)(2,1)S(1)}, u32[]{:S(2)}, u32[]{:S(2)}) collective-permute-start(bf16[256,768]{1,0:T(8,128)(2,1)S(1)} %slice.526), channel_id=1, source_target_pairs={{0,8},{8,16},{16,24},{24,28},{28,20},{20,12},{12,4},{4,0},{1,9},{9... | collective-permute-start | bytes 1179656 | tf_op jit(solution)/shard_map/ppermute | solution.py:70
  577.8 32.5 %collective-permute-start.50 = (bf16[256,896]{1,0:T(8,128)(2,1)S(1)}, bf16[256,896]{1,0:T(8,128)(2,1)S(1)}, u32[]{:S(2)}, u32[]{:S(2)}) collective-permute-start(bf16[256,896]{1,0:T(8,128)(2,1)S(1)} %pad_maximum_fusion.11), channel_id=1, source_target_pairs={{0,4},{8,0},{16,8},{24,16},{28,24},{20,28},{12,20},{4,12},{1,5},{9... | collective-permute-start | bytes 1376264 | tf_op jit(solution)/shard_map/ppermute | solution.py:70
  604.2 5.7 collective-permute-start.55
  610.8 26.1 %collective-permute-start.60 = (bf16[256,2048]{1,0:T(8,128)(2,1)S(1)}, bf16[256,2048]{1,0:T(8,128)(2,1)S(1)}, u32[]{:S(2)}, u32[]{:S(2)}) collective-permute-start(bf16[256,2048]{1,0:T(8,128)(2,1)S(1)} %add_convert_fusion.1), channel_id=1, source_target_pairs={{0,2},{1,3},{2,0},{3,1},{4,6},{5,7},{6,4},{7,5},{8,10},{9,11},{10,... | collective-permute-start | bytes 3145736 | tf_op jit(solution)/shard_map/ppermute | solution.py:195
  612.3 21.4 %collective-permute-start.56 = (bf16[256,1664]{1,0:T(8,128)(2,1)S(1)}, bf16[256,1664]{1,0:T(8,128)(2,1)S(1)}, u32[]{:S(2)}, u32[]{:S(2)}) collective-permute-start(bf16[256,1664]{1,0:T(8,128)(2,1)S(1)} %fusion.27), channel_id=1, source_target_pairs={{0,8},{8,16},{16,24},{24,28},{28,20},{20,12},{12,4},{4,0},{1,9},{9... | collective-permute-start | bytes 2555912 | tf_op jit(solution)/shard_map/ppermute | solution.py:70
  614.2 20.7 %collective-permute-start.57 = (bf16[256,1664]{1,0:T(8,128)(2,1)S(1)}, bf16[256,1664]{1,0:T(8,128)(2,1)S(1)}, u32[]{:S(2)}, u32[]{:S(2)}) collective-permute-start(bf16[256,1664]{1,0:T(8,128)(2,1)S(1)} %fusion.28), channel_id=1, source_target_pairs={{0,4},{8,0},{16,8},{24,16},{28,24},{20,28},{12,20},{4,12},{1,5},{9... | collective-permute-start | bytes 2555912 | tf_op jit(solution)/shard_map/ppermute | solution.py:70
  616.9 16.8 %collective-permute-start.58 = (f32[2,128]{1,0:T(2,128)S(1)}, f32[2,128]{1,0:T(2,128)S(1)}, u32[]{:S(2)}, u32[]{:S(2)}) collective-permute-start(f32[2,128]{1,0:T(2,128)S(1)} %fusion.173), channel_id=1, source_target_pairs={{0,4},{4,0},{8,12},{12,8},{16,20},{20,16},{24,28},{28,24},{1,5},{5... | collective-permute-start | bytes 3080 | tf_op jit(solution)/shard_map/ppermute | solution.py:200
  619.7 39.1 %collective-permute-start.64 = (bf16[256,2048]{1,0:T(8,128)(2,1)S(1)}, bf16[256,2048]{1,0:T(8,128)(2,1)S(1)}, u32[]{:S(2)}, u32[]{:S(2)}) collective-permute-start(bf16[256,2048]{1,0:T(8,128)(2,1)S(1)} %add_convert_fusion.2), channel_id=1, source_target_pairs={{0,2},{1,3},{2,0},{3,1},{4,6},{5,7},{6,4},{7,5},{8,10},{9,11},{10,... | collective-permute-start | bytes 3145736 | tf_op jit(solution)/shard_map/ppermute | solution.py:195
  637.3 21.6 %collective-permute-start.61 = (bf16[256,1664]{1,0:T(8,128)(2,1)S(1)}, bf16[256,1664]{1,0:T(8,128)(2,1)S(1)}, u32[]{:S(2)}, u32[]{:S(2)}) collective-permute-start(bf16[256,1664]{1,0:T(8,128)(2,1)S(1)} %fusion.26), channel_id=1, source_target_pairs={{0,8},{8,16},{16,24},{24,28},{28,20},{20,12},{12,4},{4,0},{1,9},{9... | collective-permute-start | bytes 2555912 | tf_op jit(solution)/shard_map/ppermute | solution.py:70
  639.2 19.6 %collective-permute-start.62 = (bf16[256,1664]{1,0:T(8,128)(2,1)S(1)}, bf16[256,1664]{1,0:T(8,128)(2,1)S(1)}, u32[]{:S(2)}, u32[]{:S(2)}) collective-permute-start(bf16[256,1664]{1,0:T(8,128)(2,1)S(1)} %fusion.29), channel_id=1, source_target_pairs={{0,4},{8,0},{16,8},{24,16},{28,24},{20,28},{12,20},{4,12},{1,5},{9... | collective-permute-start | bytes 2555912 | tf_op jit(solution)/shard_map/ppermute | solution.py:70
  641.9 17.0 %collective-permute-start.63 = (f32[2,128]{1,0:T(2,128)S(1)}, f32[2,128]{1,0:T(2,128)S(1)}, u32[]{:S(2)}, u32[]{:S(2)}) collective-permute-start(f32[2,128]{1,0:T(2,128)S(1)} %add.450), channel_id=1, source_target_pairs={{0,8},{4,12},{8,0},{12,4},{16,24},{20,28},{24,16},{28,20},{1,9},{5... | collective-permute-start | bytes 3080 | tf_op jit(solution)/shard_map/ppermute | solution.py:200
  665.4 19.6 %collective-permute-start.68 = (f32[2,256,2048]{2,1,0:T(8,128)S(1)}, f32[2,256,2048]{2,1,0:T(8,128)}, u32[]{:S(2)}, u32[]{:S(2)}) collective-permute-start(f32[2,256,2048]{2,1,0:T(8,128)S(1)} %pad_maximum_fusion.2.own_ref), channel_id=1, source_target_pairs={{0,1},{1,0},{2,3},{3,2},{4,5},{5,4},{6,7},{7,6},{8,9},{9,8},{10,11... | collective-permute-start | bytes 12582920 | tf_op jit(solution)/shard_map/ppermute | solution.py:191
  675.4 22.1 %collective-permute-start.65 = (bf16[256,1664]{1,0:T(8,128)(2,1)}, bf16[256,1664]{1,0:T(8,128)(2,1)S(1)}, u32[]{:S(2)}, u32[]{:S(2)}) collective-permute-start(bf16[256,1664]{1,0:T(8,128)(2,1)} %fusion.25), channel_id=1, source_target_pairs={{0,8},{8,16},{16,24},{24,28},{28,20},{20,12},{12,4},{4,0},{1,9},{9... | collective-permute-start | bytes 2555912 | tf_op jit(solution)/shard_map/ppermute | solution.py:70
  677.3 20.5 %collective-permute-start.66 = (bf16[256,1664]{1,0:T(8,128)(2,1)}, bf16[256,1664]{1,0:T(8,128)(2,1)}, u32[]{:S(2)}, u32[]{:S(2)}) collective-permute-start(bf16[256,1664]{1,0:T(8,128)(2,1)} %fusion.30), channel_id=1, source_target_pairs={{0,4},{8,0},{16,8},{24,16},{28,24},{20,28},{12,20},{4,12},{1,5},{9... | collective-permute-start | bytes 2555912 | tf_op jit(solution)/shard_map/ppermute | solution.py:70
  681.6 15.8 %collective-permute-start.67 = (f32[2,128]{1,0:T(2,128)S(1)}, f32[2,128]{1,0:T(2,128)S(1)}, u32[]{:S(2)}, u32[]{:S(2)}) collective-permute-start(f32[2,128]{1,0:T(2,128)S(1)} %add.453), channel_id=1, source_target_pairs={{0,16},{4,20},{8,24},{12,28},{16,0},{20,4},{24,8},{28,12},{1,17},{... | collective-permute-start | bytes 3080 | tf_op jit(solution)/shard_map/ppermute | solution.py:200
  (98 other events, 1292.6 us)

commit v3 on v2

--- a/solution.py
+++ b/solution.py
@@ -244,6 +244,20 @@
     out_ref[:, pl.ds(1 - core, 1)] = other_ref[...][:, None]
 
 
+def place_rows_kernel(columns_ref, core_ref, *refs):
+    core, out_ref = core_ref[0], refs[-1]
+    for micro in range(MICRO_BATCHES):
+        out_ref[micro, pl.ds(core, 1)] = refs[micro][...][None]
+        out_ref[micro, pl.ds(1 - core, 1)] = refs[MICRO_BATCHES + micro][...][None]
+
+
+def input_back_kernel(input_ref, chip_ref, other_ref, gain_ref, base_ref, out_ref):
+    values = input_ref[...].astype(f32)
+    gradient = chip_ref[...].astype(f32) + other_ref[...].astype(f32)
+    back, _ = rms_back(values, recip_rms(values), gain_ref[...], gradient)
+    out_ref[...] = base_ref[...] + back
+
+
 def heads_kernel(sizes, proj_ref, cos_ref, sin_ref, gain_ref, q_ref, kv_ref, gate_ref):
     query_cols, key_cols, head_dim = sizes
     cosine, sine = cos_ref[...], sin_ref[...]
@@ -315,9 +329,23 @@
     micro, head_dim, key_cols, kv_heads, repeat_heads, scale = sizes
     no_far = jnp.where(flag_ref[micro] == 1, masked, 0.0)
     columns, rows = col_ref[...], row_ref[0]
-    own = (columns[:, 0:1] == rows[0:1]) & (rows[1:2] <= columns[:, 1:2])
+    own = (columns[:, 0:1] == rows[0:1]) & (columns[:, 1:2] <= rows[1:2])
     cosine, sine, gain = cos_ref[...], sin_ref[...], gain_ref[0:1]
     logit_ref[...] = jnp.zeros_like(logit_ref)
+    lane = lax.broadcasted_iota(jnp.int32, lse_ref.shape, 1)
+    deltas = jnp.zeros(lse_ref.shape, f32)
+    lows = []
+    for head in range(kv_heads * repeat_heads):
+        here = slice(head * head_dim, (head + 1) * head_dim)
+        gate = gate_ref[:, head : head + 1]
+        gated_grad, attended = grad_ref[:, here], att_ref[:, here]
+        weighted = jnp.sum(gated_grad * attended, axis=-1, keepdims=True)
+        logit_ref[:, head : head + 1] = (weighted * gate * (1.0 - gate)).astype(bf16)
+        low = (gated_grad * gate).astype(bf16)
+        delta = jnp.sum(low.astype(f32) * attended, axis=-1, keepdims=True)
+        deltas = jnp.where(lane == head, delta, deltas)
+        lows.append(low)
+    deltas, totals_log = deltas.T, lse_ref[...].T
     gain_sum = jnp.zeros((1, head_dim), f32)
     for kv_head in range(kv_heads):
         at = slice(kv_head * head_dim, (kv_head + 1) * head_dim)
@@ -325,24 +353,19 @@
         totals = [0.0, 0.0, 0.0, 0.0]
         for head in range(kv_head * repeat_heads, (kv_head + 1) * repeat_heads):
             here = slice(head * head_dim, (head + 1) * head_dim)
-            queries = q_ref[:, here]
-            gate = gate_ref[:, head : head + 1]
-            gated_grad, attended = grad_ref[:, here], att_ref[:, here]
-            weighted = jnp.sum(gated_grad * attended, axis=-1, keepdims=True)
-            logit_ref[:, head : head + 1] = (weighted * gate * (1.0 - gate)).astype(bf16)
-            low = (gated_grad * gate).astype(bf16)
-            delta = jnp.sum(low.astype(f32) * attended, axis=-1, keepdims=True)
-            log_total = lse_ref[:, head : head + 1]
-            far = jnp.exp(by_transpose(queries, far_ref[:, at]) * scale + (no_far - log_total))
-            near = by_transpose(queries, kv_ref[:, at]) * scale
+            queries, low = q_ref[:, here], lows[head]
+            delta, log_total = deltas[head : head + 1], totals_log[head : head + 1]
+            far = jnp.exp(by_transpose(far_ref[:, at], queries) * scale + (no_far - log_total))
+            near = by_transpose(kv_ref[:, at], queries) * scale
             near = jnp.exp(jnp.where(own, near - log_total, masked))
-            far_low = (far * (by_transpose(low, far_ref[:, at_value]) - delta)).astype(bf16)
-            near_low = (near * (by_transpose(low, kv_ref[:, at_value]) - delta)).astype(bf16)
-            totals[0] = totals[0] + transpose_by(far_low, queries)
-            totals[1] = totals[1] + transpose_by(far.astype(bf16), low)
-            totals[2] = totals[2] + transpose_by(near_low, queries)
-            totals[3] = totals[3] + transpose_by(near.astype(bf16), low)
-            back = (product(far_low, far_ref[:, at]) + product(near_low, kv_ref[:, at])) * scale
+            far_low = (far * (by_transpose(far_ref[:, at_value], low) - delta)).astype(bf16)
+            near_low = (near * (by_transpose(kv_ref[:, at_value], low) - delta)).astype(bf16)
+            totals[0] = totals[0] + product(far_low, queries)
+            totals[1] = totals[1] + product(far.astype(bf16), low)
+            totals[2] = totals[2] + product(near_low, queries)
+            totals[3] = totals[3] + product(near.astype(bf16), low)
+            back = transpose_by(far_low, far_ref[:, at]) + transpose_by(near_low, kv_ref[:, at])
+            back = back * scale
             values = proj_ref[:, here]
             back, terms = rms_back(
                 values, recip_rms(values), gain, turned(back, cosine, -sine)
@@ -650,8 +673,8 @@
     normed_two = drain(mlp_ring, normed_two)
     gate_up_full = mlp_ring.gathered(0, 2 * hidden_units)
     down_turned = mlp_ring.gathered(2 * hidden_units, 3 * hidden_units)
-    pre = product(normed_two, gate_up_full)
-    gate_pre, up_pre = pre[:, :hidden_units], pre[:, hidden_units:]
+    pre = product(normed_two, gate_up_full).astype(bf16)
+    gate_pre, up_pre = pre[:, :hidden_units].astype(f32), pre[:, hidden_units:].astype(f32)
     sigmoid_gate = jax.nn.sigmoid(gate_pre)
     swish_gate = gate_pre * sigmoid_gate
     hidden_low = (swish_gate * up_pre).astype(bf16)
@@ -831,8 +854,13 @@
         )
         in_grads.append(in_grad)
         key_gain_sums.append(key_terms[0])
+    query_gain, key_gain_sum = query_gain[0] + query_gain[1], key_gain_sums[0] + key_gain_sums[1]
+    head_gains = jnp.stack([query_gain, key_gain_sum])
+    head_gains = head_gains + swap_core(head_gains)
+    head_gains = head_gains + swap_x(head_gains)
+    first, second, head_gains = settle(gate_up_back, *in_grads, head_gains)
     in_back = Scatter(
-        lambda slot, right=jnp.concatenate(in_grads), middle_low=jnp.concatenate(
+        lambda slot, right=jnp.concatenate((first, second)), middle_low=jnp.concatenate(
             middle_lows
         ): jnp.concatenate(
             [
@@ -843,44 +871,81 @@
         ),
         count,
     )
-    in_grads = in_back.issue(*in_grads)
-    query_gain, key_gain_sum = query_gain[0] + query_gain[1], key_gain_sums[0] + key_gain_sums[1]
-    head_gains = jnp.stack([query_gain, key_gain_sum])
-    head_gains = head_gains + swap_core(head_gains)
-    head_gains = head_gains + swap_x(head_gains)
-    first, second, head_gains = settle(gate_up_back, *in_grads, head_gains)
+    first, second = in_back.issue(first, second)
     first = by_transpose(first, in_full).astype(bf16)
     second = by_transpose(second, in_full).astype(bf16)
     chips = [chip_sum(partial[own_rows:], partial[:own_rows]) for partial in (first, second)]
     from_x = [swap_x(chip) for chip in chips]
     chips[1], head_gains = pump(in_back, chips[1], head_gains)
-    level, turn = 1, 0
-    while level < count // 2:
-        arrived_gains, from_x[turn] = pump(in_back, swap_dp(head_gains, level), from_x[turn])
-        head_gains = head_gains + arrived_gains
-        level, turn = 2 * level, min(turn + 1, MICRO_BATCHES - 1)
-    input_rows = []
-    for micro in range(MICRO_BATCHES):
-        own = slice(micro * block_rows, micro * block_rows + own_rows)
-        summed = chips[micro].astype(f32) + from_x[micro].astype(f32)
-        input_back, _ = rms_back(inputs[own], recip_one[own], gain_attn, summed)
-        input_rows.append(middle_grads[micro] + input_back)
-    input_own = jnp.stack(input_rows)
-    tokens_grad = place_back(input_own, swap_core(input_own), True, "place_tokens")
-
-    arrived_gains, tokens_grad = pump(in_back, swap_dp(head_gains, level), tokens_grad)
-    head_gains = head_gains + arrived_gains
-    tokens_grad = drain(in_back, tokens_grad)
     drain(gate_up_back)
-
+    drain(down_back)
     gate_up_grad = gate_up_back.total()
-    in_total = in_back.total()
-    in_weight_grad, out_weight_grad = in_total[:, :joined], in_total[:, joined:].T
+    down_grad = down_back.total()
     mlp_sum = jnp.sum(
         gate_up_grad[:, :hidden_units] * gate_weight.astype(f32)
         + gate_up_grad[:, hidden_units:] * up_weight.astype(f32),
         axis=1,
     )
+    gate_grad, up_grad = gate_up_grad[:, :hidden_units], gate_up_grad[:, hidden_units:]
+    level, turn = 1, 0
+    while level < count // 2:
+        if turn == 1:
+            from_x[1], gate_grad, up_grad, down_grad, mlp_sum = order(
+                from_x[1], gate_grad, up_grad, down_grad, mlp_sum
+            )
+        late = min(turn, MICRO_BATCHES - 1)
+        arrived_gains, from_x[late] = pump(in_back, swap_dp(head_gains, level), from_x[late])
+        head_gains = head_gains + arrived_gains
+        level, turn = 2 * level, turn + 1
+    input_rows = []
+    for micro in range(MICRO_BATCHES):
+        part = pl.BlockSpec((own_rows // 2, width), lambda i: (i, 0))
+        input_rows.append(
+            pl.pallas_call(
+                input_back_kernel,
+                out_shape=jax.ShapeDtypeStruct((own_rows, width), f32),
+                grid=(2,),
+                in_specs=[
+                    pl.BlockSpec(
+                        (own_rows // 2, width), lambda i, micro=micro: (4 * micro + i, 0)
+                    ),
+                    part,
+                    part,
+                    whole(1, width),
+                    part,
+                ],
+                out_specs=part,
+                compiler_params=params,
+                cost_estimate=cost(1024, 1024),
+                name="input_back",
+            )(inputs_low, chips[micro], from_x[micro], gain_attn, middle_grads[micro])
+        )
+    other_rows = [swap_core(rows) for rows in input_rows]
+    if depth % 128:
+        tokens_grad = place_back(jnp.stack(input_rows), jnp.stack(other_rows), True, "place_tokens")
+    else:
+        tokens_grad = pl.pallas_call(
+            place_rows_kernel,
+            out_shape=jax.ShapeDtypeStruct((MICRO_BATCHES, 2, own_rows, width), f32),
+            grid_spec=pltpu.PrefetchScalarGridSpec(
+                num_scalar_prefetch=2,
+                grid=(count,),
+                in_specs=[pl.BlockSpec((own_rows, depth), lambda i, cols, core: (0, i))]
+                * (2 * MICRO_BATCHES),
+                out_specs=pl.BlockSpec(
+                    (MICRO_BATCHES, 2, own_rows, depth), lambda i, cols, core: (0, 0, 0, cols[i])
+                ),
+            ),
+            compiler_params=params,
+            cost_estimate=cost(1024, 1024),
+            name="place_tokens",
+        )(column_places, core_place, *input_rows, *other_rows).reshape(total_rows, width)
+
+    arrived_gains, tokens_grad = pump(in_back, swap_dp(head_gains, level), tokens_grad)
+    head_gains = head_gains + arrived_gains
+    tokens_grad = drain(in_back, tokens_grad)
+    in_total = in_back.total()
+    in_weight_grad, out_weight_grad = in_total[:, :joined], in_total[:, joined:].T
     used = first_gain
     attn_sum = jnp.sum(in_weight_grad[:, :used] * packed[:, :used].astype(f32), axis=1)
     gains = jnp.stack([attn_sum, mlp_sum])
@@ -894,9 +959,9 @@
         in_weight_grad[:, query_cols + key_cols : query_cols + 2 * key_cols],
         in_weight_grad[:, query_cols + 2 * key_cols : query_cols + 2 * key_cols + head_count],
         out_weight_grad,
-        gate_up_grad[:, :hidden_units],
-        gate_up_grad[:, hidden_units:],
-        down_back.total(),
+        gate_grad,
+        up_grad,
+        down_grad,
         gains[0] / norm_attn.astype(f32),
         gains[1] / norm_mlp.astype(f32),
         head_gains[0],

time: 717 us -> 712 us (level)
    pallas_call x0 -> x3, Pallas kernels: none -> 18.3 us  [the longest x1 9.54 us: on_device(): pl.pallas_call(place_rows_kernel, out_shape=jax.ShapeDtypeStruct((MICRO_B...]
    dot_general x32, matrix products: 59.8 us -> 71.6 us  [transpose_by(): lax.dot_general(left_side, right_side, (((0,), (0,)), ((), ())), preferre...]
    pallas_call x2 -> x1, Pallas kernels: 16.9 us -> 7.24 us  [place_back(): pl.pallas_call(place_kernel, out_shape=jax.ShapeDtypeStruct((MICRO_BATCHE...]
  transfers between devices with their start and end apart: 71 -> 72, of which waited for: 39 -> 39; matrix products, arithmetic and copies ran while one was open for 30% -> 31% of each run, Pallas kernels for 13% -> 14%
where the time goes in v3:
time: 712 us; the launch traced here: 702 us
  waiting for transfers between devices  255 us (36%)
  matrix products  149 us (21%)
  Pallas kernels  96.9 us (14%)
  starting transfers between devices  72.5 us (10%)
  other arithmetic  63 us (9%)
  local copies, waits for them, and re-layouts  61.9 us (9%)
    ppermute x39, waiting for transfers between devices, ring_step(): return lax.ppermute(block, 'dp', route)  121 us
    ppermute x9, waiting for transfers between devices, swap_x(): lax.ppermute(block, 'mp', [(i, i ^ 2) for i in range(lax.axis_size('mp'))])  71.8 us
    dot_general x32, matrix products, transpose_by(): lax.dot_general(left_side, right_side, (((0,), (0,)), ((), ())), preferre...  71.6 us
    unnamed x223, local copies, waits for them, and re-layouts  51.4 us
    ppermute x39, starting transfers between devices, ring_step(): return lax.ppermute(block, 'dp', route)  42.8 us
    dot_general x5, matrix products, product(): return jnp.dot(left_side, right_side, preferred_element_type=f32)  39.4 us
    dot_general x9, matrix products, by_transpose(): lax.dot_general(left_side, right_side, (((1,), (1,)), ((), ())), preferre...  38.4 us
    ppermute x1, waiting for transfers between devices, on_device(): by_both = lax.ppermute(sent, 'dp', group_route(3, (0, 3)))  34.6 us
  transfers between devices with their start and end apart: 72, of which 39 were waited for; matrix products, arithmetic and copies ran while one was open for 31% of the time, Pallas kernels for 14%

profile of v3, /device:TPU:0, one launch (start us, length us, event | category | flops | bytes accessed | tf_op | source)
XLA Modules:
  0.0 701.7 jit_solution(523158130559955145)
XLA Ops:
  9.7 3.0 collective-permute-start.1
  17.6 7.4 %bring_tokens.1 = bf16[2,2,256,2048]{3,2,1,0:T(8,128)(2,1)} custom-call(s32[8]{0:T(128)} %gather_fusion, s32[1]{0:T(128)} %bitcast.1.core_ref, bf16[2,2,256,2048]{3,2,1,0:T(8,128)(2,1)} %bitcast.137), custom_call_target="tpu_custom_call" | custom-call | bytes 8388608 | tf_op jit(solution)/shard_map/bring_tokens/pallas_call | solution.py:495
  25.8 6.1 collective-permute-done.1
  37.3 3.1 multiply_reduce_fusion
  40.4 12.7 %collective-permute-done.2 = bf16[256,1664]{1,0:T(8,128)(2,1)S(1)} collective-permute-done((bf16[256,1664]{1,0:T(8,128)(2,1)}, bf16[256,1664]{1,0:T(8,128)(2,1)S(1)}, u32[]{:S(2)}, u32[]{:S(2)}) %collective-permute-start.2) | collective-permute-done | bytes 852000 | tf_op jit(solution)/shard_map/ppermute | solution.py:70
  57.7 14.4 %collective-permute-done.4 = bf16[256,1664]{1,0:T(8,128)(2,1)S(1)} collective-permute-done((bf16[256,1664]{1,0:T(8,128)(2,1)S(1)}, bf16[256,1664]{1,0:T(8,128)(2,1)S(1)}, u32[]{:S(2)}, u32[]{:S(2)}) %collective-permute-start.4) | collective-permute-done | bytes 852000 | tf_op jit(solution)/shard_map/ppermute | solution.py:70
  81.2 4.6 collective-permute-done.7
  91.9 7.3 %fusion.124.proj_ref = f32[1024,1152]{1,0:T(8,128)} fusion(bf16[1024,2048]{1,0:T(8,128)(2,1)S(1)} %multiply_convert_fusion, bf16[2048,1152]{1,0:T(8,128)(2,1)S(1)} %fusion.47), kind=kOutput, calls=%fused_computation.309 | convolution fusion | flops 4831838208 | bytes 13631488 | tf_op jit(solution)/shard_map/dot_general | solution.py:21
  99.2 6.5 heads.1
  114.8 34.6 %collective-permute-done.12 = bf16[512,512]{1,0:T(8,128)(2,1)S(1)} collective-permute-done((bf16[512,512]{1,0:T(8,128)(2,1)}, bf16[512,512]{1,0:T(8,128)(2,1)S(1)}, u32[]{:S(2)}, u32[]{:S(2)}) %collective-permute-start.12) | collective-permute-done | bytes 524320 | tf_op jit(solution)/shard_map/ppermute | solution.py:614
  149.4 7.2 %collective-permute-done.11 = bf16[512,512]{1,0:T(8,128)(2,1)} collective-permute-done((bf16[512,512]{1,0:T(8,128)(2,1)}, bf16[512,512]{1,0:T(8,128)(2,1)}, u32[]{:S(2)}, u32[]{:S(2)}) %collective-permute-start.11) | collective-permute-done | bytes 524320 | tf_op jit(solution)/shard_map/ppermute | solution.py:613
  159.2 2.5 collective-permute-start.13
  170.2 14.1 %attend.1 = (bf16[1024,512]{1,0:T(8,128)(2,1)}, f32[1024,512]{1,0:T(8,128)}, f32[1024,128]{1,0:T(8,128)}) custom-call(s32[2]{0:T(128)} %add_convert_fusion.5.flag_ref, bf16[1024,512]{1,0:T(8,128)(2,1)} %get-tuple-element.190.q_ref, bf16[1024,512]{1,0:T(8,128)(2,1)} %get-tuple-element.186.kv_ref, bf16[1024,512]{1,0:T(8,128)(2,1)} %pad_maximum_fusion.5.far_ref, ...), custom_call_target="tpu_custom_call" | custom-call | flops 2147483648 | bytes 6291456 | tf_op jit(solution)/shard_map/attend/pallas_call | solution.py:624
  184.2 7.4 %bring_cotangent.1 = bf16[2,2,256,2048]{3,2,1,0:T(8,128)(2,1)} custom-call(s32[8]{0:T(128)} %gather_fusion, s32[1]{0:T(128)} %bitcast.1.core_ref, bf16[2,2,256,2048]{3,2,1,0:T(8,128)(2,1)} %bitcast.138), custom_call_target="tpu_custom_call" | custom-call | bytes 8388608 | tf_op jit(solution)/shard_map/bring_cotangent/pallas_call | solution.py:495
  191.6 12.7 %collective-permute-done.13 = bf16[256,4608]{0,1:T(8,128)(2,1)} collective-permute-done((bf16[256,4608]{0,1:T(8,128)(2,1)}, bf16[256,4608]{0,1:T(8,128)(2,1)}, u32[]{:S(2)}, u32[]{:S(2)}) %collective-permute-start.13) | collective-permute-done | bytes 2359328 | tf_op jit(solution)/shard_map/ppermute | solution.py:70
  215.2 19.5 %collective-permute-done.16 = bf16[256,2048]{1,0:T(8,128)(2,1)S(1)} collective-permute-done((bf16[256,2048]{1,0:T(8,128)(2,1)S(1)}, bf16[256,2048]{1,0:T(8,128)(2,1)S(1)}, u32[]{:S(2)}, u32[]{:S(2)}) %collective-permute-start.16) | collective-permute-done | bytes 1048608 | tf_op jit(solution)/shard_map/ppermute | solution.py:195
  234.7 21.7 %collective-permute-done.18 = bf16[256,2048]{1,0:T(8,128)(2,1)S(1)} collective-permute-done((bf16[256,2048]{1,0:T(8,128)(2,1)S(1)}, bf16[256,2048]{1,0:T(8,128)(2,1)S(1)}, u32[]{:S(2)}, u32[]{:S(2)}) %collective-permute-start.18) | collective-permute-done | bytes 1048608 | tf_op jit(solution)/shard_map/ppermute | solution.py:195
  259.6 5.6 collective-permute-done.19
  276.3 2.8 slice_dynamic-update-slice_fusion.5
  279.1 2.7 slice_dynamic-update-slice_fusion.4
  283.1 2.7 slice_dynamic-update-slice_fusion.2
  285.8 2.7 slice_dynamic-update-slice_fusion.1
  292.5 4.6 collective-permute-done.22
  299.0 15.8 %convolution_convert_fusion = bf16[1024,3072]{1,0:T(8,128)(2,1)S(1)} fusion(bf16[1024,2048]{1,0:T(8,128)(2,1)S(1)} %pad_maximum_fusion, bf16[2048,3072]{0,1:T(8,128)(2,1)} %fusion.39), kind=kOutput, calls=%fused_computation.17 | convolution fusion | flops 12888047616 | bytes 23068672 | tf_op jit(solution)/shard_map/dot_general | solution.py:21
  322.2 11.8 %multiply_convert_fusion.1 = (bf16[1024,1536]{1,0:T(8,128)(2,1)S(1)}, bf16[1024,1536]{1,0:T(8,128)(2,1)}) fusion(bf16[1024,3072]{1,0:T(8,128)(2,1)S(1)} %convolution_convert_fusion, bf16[1024,2048]{1,0:T(8,128)(2,1)S(1)} %bitcast.126, bf16[2048,1536]{0,1:T(8,128)(2,1)} %slice_dynamic-update-slice_fusion.7), kind=kOutput, calls=%fused_computation.16 | convolution fusion | flops 6466043904 | bytes 23068672 | tf_op jit(solution)/shard_map/dot_general | solution.py:21
  334.0 5.0 collective-permute-done.25
  345.6 17.8 %convolution_convert_fusion.2 = bf16[1024,2048]{1,0:T(8,128)(2,1)S(1)} fusion(bf16[1024,3072]{1,0:T(8,128)(2,1)S(1)} %constant_dynamic-update-slice_fusion.7, bf16[2048,3072]{0,1:T(8,128)(2,1)} %fusion.39), kind=kOutput, calls=%fused_computation.39 | convolution fusion | flops 12886999040 | bytes 23068672 | tf_op jit(solution)/shard_map/dot_general | solution.py:25
  371.6 4.8 convolution_convert_fusion.1
  378.6 11.3 %collective-permute-done.29 = bf16[1536,256]{1,0:T(8,128)(2,1)S(1)} collective-permute-done((bf16[1536,256]{1,0:T(8,128)(2,1)}, bf16[1536,256]{1,0:T(8,128)(2,1)S(1)}, u32[]{:S(2)}, u32[]{:S(2)}) %collective-permute-start.29) | collective-permute-done | bytes 786464 | tf_op jit(solution)/shard_map/ppermute | solution.py:70
  398.2 3.6 convolution_convert_fusion.5
  402.0 18.4 %collective-permute-done.37 = bf16[256,2048]{1,0:T(8,128)(2,1)S(1)} collective-permute-done((bf16[256,2048]{1,0:T(8,128)(2,1)S(1)}, bf16[256,2048]{1,0:T(8,128)(2,1)S(1)}, u32[]{:S(2)}, u32[]{:S(2)}) %collective-permute-start.37) | collective-permute-done | bytes 1048608 | tf_op jit(solution)/shard_map/ppermute | solution.py:195
  421.8 2.5 collective-permute-done.35
  424.3 4.3 fusion.11
  428.6 4.2 fusion.12
  433.1 3.3 fusion.115
  438.4 5.0 add_convert_fusion
  448.5 13.2 %attend_back.2 = (bf16[512,512]{1,0:T(8,128)(2,1)}, bf16[512,512]{1,0:T(8,128)(2,1)}, f32[512,512]{1,0:T(8,128)}, bf16[512,128]{1,0:T(8,128)(2,1)}, f32[8,128]{1,0:T(8,128)}) custom-call(s32[2]{0:T(128)} %add_convert_fusion.5.flag_ref, bf16[1024,512]{1,0:T(8,128)(2,1)} %get-tuple-element.190.q_ref, bf16[1024,512]{1,0:T(8,128)(2,1)} %get-tuple-element.186.kv_ref, ...), custom_call_target="tpu_custom_call" | custom-call | flops 2684354560 | bytes 7864320 | tf_op jit(solution)/shard_map/attend_back/pallas_call | solution.py:737
  461.8 11.7 %collective-permute-done.38 = bf16[256,3072]{1,0:T(8,128)(2,1)} collective-permute-done((bf16[256,3072]{1,0:T(8,128)(2,1)}, bf16[256,3072]{1,0:T(8,128)(2,1)}, u32[]{:S(2)}, u32[]{:S(2)}) %collective-permute-start.38) | collective-permute-done | bytes 1572896 | tf_op jit(solution)/shard_map/ppermute | solution.py:70
  474.8 4.6 fusion.10
  479.4 4.9 fusion.13
  485.0 3.4 fusion.114
  488.3 3.6 fusion.16
  494.0 5.0 convert_add_fusion
  502.2 13.1 %attend_back.3 = (bf16[512,512]{1,0:T(8,128)(2,1)}, bf16[512,512]{1,0:T(8,128)(2,1)}, f32[512,512]{1,0:T(8,128)}, bf16[512,128]{1,0:T(8,128)(2,1)}, f32[8,128]{1,0:T(8,128)}) custom-call(s32[2]{0:T(128)} %add_convert_fusion.5.flag_ref, bf16[1024,512]{1,0:T(8,128)(2,1)} %get-tuple-element.190.q_ref, bf16[1024,512]{1,0:T(8,128)(2,1)} %get-tuple-element.186.kv_ref, ...), custom_call_target="tpu_custom_call" | custom-call | flops 2684354560 | bytes 7864320 | tf_op jit(solution)/shard_map/attend_back/pallas_call | solution.py:737
  515.4 4.2 fusion.8
  530.0 3.5 collective-permute-start.48
  536.1 4.6 fusion.14
  540.7 4.6 fusion.15
  545.3 7.2 %place_layer.1 = bf16[2,2,256,2048]{3,2,1,0:T(8,128)(2,1)} custom-call(s32[8]{0:T(128)} %gather_fusion, s32[1]{0:T(128)} %bitcast.1.core_ref, bf16[2,256,2048]{2,1,0:T(8,128)(2,1)} %bitcast.132, bf16[2,256,2048]{2,1,0:T(8,128)(2,1)} %collective-permute-done.43.other_ref), custom_call_target="tpu_custom_call" | custom-call | flops 1024 | bytes 1024 | tf_op jit(solution)/shard_map/place_layer/pallas_call | solution.py:528
  552.6 4.8 collective-permute-done.46.one_ref
  559.4 2.7 fusion.70
  562.8 4.7 join.2
  567.5 4.9 join.3
  579.2 14.8 %collective-permute-done.49 = bf16[256,3072]{1,0:T(8,128)(2,1)} collective-permute-done((bf16[256,3072]{1,0:T(8,128)(2,1)}, bf16[256,3072]{1,0:T(8,128)(2,1)}, u32[]{:S(2)}, u32[]{:S(2)}) %collective-permute-start.49) | collective-permute-done | bytes 1572896 | tf_op jit(solution)/shard_map/ppermute | solution.py:70
  599.2 5.9 convolution_convert_fusion.4
  605.3 3.1 convolution_convert_fusion.3
  616.3 4.2 fusion.9
  624.2 10.7 %collective-permute-done.58 = f32[2,128]{1,0:T(2,128)S(1)} collective-permute-done((f32[2,128]{1,0:T(2,128)S(1)}, f32[2,128]{1,0:T(2,128)S(1)}, u32[]{:S(2)}, u32[]{:S(2)}) %collective-permute-start.58) | collective-permute-done | bytes 1056 | tf_op jit(solution)/shard_map/ppermute | solution.py:200
  636.2 2.7 collective-permute-done.60.other_ref
  647.6 4.4 input_back.2.refs_0_
  652.1 8.3 %collective-permute-done.64.other_ref = bf16[256,2048]{1,0:T(8,128)(2,1)S(1)} collective-permute-done((bf16[256,2048]{1,0:T(8,128)(2,1)S(1)}, bf16[256,2048]{1,0:T(8,128)(2,1)S(1)}, u32[]{:S(2)}, u32[]{:S(2)}) %collective-permute-start.64) | collective-permute-done | bytes 1048608 | tf_op jit(solution)/shard_map/ppermute | solution.py:195
  665.2 4.3 input_back.3.refs_1_
  679.3 9.5 %place_tokens.1 = f32[2,2,256,2048]{3,2,1,0:T(8,128)} custom-call(s32[8]{0:T(128)} %gather_fusion, s32[1]{0:T(128)} %bitcast.1.core_ref, f32[256,2048]{1,0:T(8,128)} %input_back.2.refs_0_, f32[256,2048]{1,0:T(8,128)} %input_back.3.refs_1_, f32[256,2048]{1,0:T(8,128)} %copy-done.35, f32[256,2048]{1,0:T(8,128)} %copy-done.36), custom_call_target="tpu_custom_call" | custom-call | flops 1024 | bytes 1024 | tf_op jit(solution)/shard_map/place_tokens/pallas_call | solution.py:927
  688.9 3.4 collective-permute-done.67
  (485 shorter events, 213.5 us)
Async XLA Ops:
  9.7 22.3 %collective-permute-start.1 = (bf16[256,1664]{1,0:T(8,128)(2,1)}, bf16[256,1664]{1,0:T(8,128)(2,1)}, u32[]{:S(2)}, u32[]{:S(2)}) collective-permute-start(bf16[256,1664]{1,0:T(8,128)(2,1)} %bitcast_dynamic-update-slice_fusion.1), channel_id=1, source_target_pairs={{0,4},{8,0},{16,8},{24,16},{28,24},{20,28},{12,20},{4,12},{1,5},{9... | collective-permute-start | bytes 2555912 | tf_op jit(solution)/shard_map/ppermute | solution.py:70
  12.7 20.7 %collective-permute-start = (bf16[256,1664]{1,0:T(8,128)(2,1)}, bf16[256,1664]{1,0:T(8,128)(2,1)}, u32[]{:S(2)}, u32[]{:S(2)}) collective-permute-start(bf16[256,1664]{1,0:T(8,128)(2,1)} %bitcast_dynamic-update-slice_fusion.1), channel_id=1, source_target_pairs={{0,8},{8,16},{16,24},{24,28},{28,20},{20,12},{12,4},{4,0},{1,9},{9... | collective-permute-start | bytes 2555912 | tf_op jit(solution)/shard_map/ppermute | solution.py:70
  33.4 19.7 %collective-permute-start.2 = (bf16[256,1664]{1,0:T(8,128)(2,1)}, bf16[256,1664]{1,0:T(8,128)(2,1)S(1)}, u32[]{:S(2)}, u32[]{:S(2)}) collective-permute-start(bf16[256,1664]{1,0:T(8,128)(2,1)} %collective-permute-done), channel_id=1, source_target_pairs={{0,8},{8,16},{16,24},{24,28},{28,20},{20,12},{12,4},{4,0},{1,9},{9... | collective-permute-start | bytes 2555912 | tf_op jit(solution)/shard_map/ppermute | solution.py:70
  33.7 19.7 %collective-permute-start.3 = (bf16[256,1664]{1,0:T(8,128)(2,1)}, bf16[256,1664]{1,0:T(8,128)(2,1)S(1)}, u32[]{:S(2)}, u32[]{:S(2)}) collective-permute-start(bf16[256,1664]{1,0:T(8,128)(2,1)} %collective-permute-done.1), channel_id=1, source_target_pairs={{0,4},{8,0},{16,8},{24,16},{28,24},{20,28},{12,20},{4,12},{1,5},{9... | collective-permute-start | bytes 2555912 | tf_op jit(solution)/shard_map/ppermute | solution.py:70
  53.5 18.6 %collective-permute-start.4 = (bf16[256,1664]{1,0:T(8,128)(2,1)S(1)}, bf16[256,1664]{1,0:T(8,128)(2,1)S(1)}, u32[]{:S(2)}, u32[]{:S(2)}) collective-permute-start(bf16[256,1664]{1,0:T(8,128)(2,1)S(1)} %collective-permute-done.2), channel_id=1, source_target_pairs={{0,8},{8,16},{16,24},{24,28},{28,20},{20,12},{12,4},{4,0},{1,9},{9... | collective-permute-start | bytes 2555912 | tf_op jit(solution)/shard_map/ppermute | solution.py:70
  55.0 18.2 %collective-permute-start.5 = (bf16[256,1664]{1,0:T(8,128)(2,1)S(1)}, bf16[256,1664]{1,0:T(8,128)(2,1)S(1)}, u32[]{:S(2)}, u32[]{:S(2)}) collective-permute-start(bf16[256,1664]{1,0:T(8,128)(2,1)S(1)} %collective-permute-done.3), channel_id=1, source_target_pairs={{0,4},{8,0},{16,8},{24,16},{28,24},{20,28},{12,20},{4,12},{1,5},{9... | collective-permute-start | bytes 2555912 | tf_op jit(solution)/shard_map/ppermute | solution.py:70
  73.3 7.8 %collective-permute-start.6 = (bf16[256,768]{1,0:T(8,128)(2,1)S(1)}, bf16[256,768]{1,0:T(8,128)(2,1)S(1)}, u32[]{:S(2)}, u32[]{:S(2)}) collective-permute-start(bf16[256,768]{1,0:T(8,128)(2,1)S(1)} %slice.375), channel_id=1, source_target_pairs={{0,8},{8,16},{16,24},{24,28},{28,20},{20,12},{12,4},{4,0},{1,9},{9... | collective-permute-start | bytes 1179656 | tf_op jit(solution)/shard_map/ppermute | solution.py:70
  75.0 10.7 %collective-permute-start.7 = (bf16[256,896]{1,0:T(8,128)(2,1)S(1)}, bf16[256,896]{1,0:T(8,128)(2,1)S(1)}, u32[]{:S(2)}, u32[]{:S(2)}) collective-permute-start(bf16[256,896]{1,0:T(8,128)(2,1)S(1)} %slice.376), channel_id=1, source_target_pairs={{0,4},{8,0},{16,8},{24,16},{28,24},{20,28},{12,20},{4,12},{1,5},{9... | collective-permute-start | bytes 1376264 | tf_op jit(solution)/shard_map/ppermute | solution.py:70
  85.7 73.5 %collective-permute-start.9 = (bf16[256,4608]{0,1:T(8,128)(2,1)S(1)}, bf16[256,4608]{0,1:T(8,128)(2,1)}, u32[]{:S(2)}, u32[]{:S(2)}) collective-permute-start(bf16[256,4608]{0,1:T(8,128)(2,1)S(1)} %pad_maximum_fusion.2), channel_id=1, source_target_pairs={{0,4},{8,0},{16,8},{24,16},{28,24},{20,28},{12,20},{4,12},{1,5},{9... | collective-permute-start | bytes 7077896 | tf_op jit(solution)/shard_map/ppermute | solution.py:70
  86.2 73.0 %collective-permute-start.8 = (bf16[256,4608]{0,1:T(8,128)(2,1)S(1)}, bf16[256,4608]{0,1:T(8,128)(2,1)}, u32[]{:S(2)}, u32[]{:S(2)}) collective-permute-start(bf16[256,4608]{0,1:T(8,128)(2,1)S(1)} %pad_maximum_fusion.2), channel_id=1, source_target_pairs={{0,8},{8,16},{16,24},{24,28},{28,20},{20,12},{12,4},{4,0},{1,9},{9... | collective-permute-start | bytes 7077896 | tf_op jit(solution)/shard_map/ppermute | solution.py:70
  107.8 41.6 %collective-permute-start.12 = (bf16[512,512]{1,0:T(8,128)(2,1)}, bf16[512,512]{1,0:T(8,128)(2,1)S(1)}, u32[]{:S(2)}, u32[]{:S(2)}) collective-permute-start(bf16[512,512]{1,0:T(8,128)(2,1)} %slice_select_fusion), channel_id=1, source_target_pairs={{0,12},{12,0},{16,28},{28,16},{1,13},{13,1},{17,29},{29,17},{2,14}... | collective-permute-start | bytes 1572872 | tf_op jit(solution)/shard_map/ppermute | solution.py:614
  110.2 46.4 %collective-permute-start.11 = (bf16[512,512]{1,0:T(8,128)(2,1)}, bf16[512,512]{1,0:T(8,128)(2,1)}, u32[]{:S(2)}, u32[]{:S(2)}) collective-permute-start(bf16[512,512]{1,0:T(8,128)(2,1)} %slice_select_fusion), channel_id=1, source_target_pairs={{0,8},{12,4},{16,24},{28,20},{1,9},{13,5},{17,25},{29,21},{2,10},{... | collective-permute-start | bytes 1572872 | tf_op jit(solution)/shard_map/ppermute | solution.py:613
  112.7 44.0 %collective-permute-start.10 = (bf16[512,512]{1,0:T(8,128)(2,1)}, bf16[512,512]{1,0:T(8,128)(2,1)}, u32[]{:S(2)}, u32[]{:S(2)}) collective-permute-start(bf16[512,512]{1,0:T(8,128)(2,1)} %slice_select_fusion), channel_id=1, source_target_pairs={{0,4},{12,8},{16,20},{28,24},{1,5},{13,9},{17,21},{29,25},{2,6},{1... | collective-permute-start | bytes 1572872 | tf_op jit(solution)/shard_map/ppermute | solution.py:612
  159.2 45.2 %collective-permute-start.13 = (bf16[256,4608]{0,1:T(8,128)(2,1)}, bf16[256,4608]{0,1:T(8,128)(2,1)}, u32[]{:S(2)}, u32[]{:S(2)}) collective-permute-start(bf16[256,4608]{0,1:T(8,128)(2,1)} %collective-permute-done.8), channel_id=1, source_target_pairs={{0,8},{8,16},{16,24},{24,28},{28,20},{20,12},{12,4},{4,0},{1,9},{9... | collective-permute-start | bytes 7077896 | tf_op jit(solution)/shard_map/ppermute | solution.py:70
  161.7 42.6 %collective-permute-start.14 = (bf16[256,4608]{0,1:T(8,128)(2,1)}, bf16[256,4608]{0,1:T(8,128)(2,1)}, u32[]{:S(2)}, u32[]{:S(2)}) collective-permute-start(bf16[256,4608]{0,1:T(8,128)(2,1)} %collective-permute-done.9), channel_id=1, source_target_pairs={{0,4},{8,0},{16,8},{24,16},{28,24},{20,28},{12,20},{4,12},{1,5},{9... | collective-permute-start | bytes 7077896 | tf_op jit(solution)/shard_map/ppermute | solution.py:70
  208.6 26.1 %collective-permute-start.16 = (bf16[256,2048]{1,0:T(8,128)(2,1)S(1)}, bf16[256,2048]{1,0:T(8,128)(2,1)S(1)}, u32[]{:S(2)}, u32[]{:S(2)}) collective-permute-start(bf16[256,2048]{1,0:T(8,128)(2,1)S(1)} %fusion.17), channel_id=1, source_target_pairs={{0,2},{1,3},{2,0},{3,1},{4,6},{5,7},{6,4},{7,5},{8,10},{9,11},{10,... | collective-permute-start | bytes 3145736 | tf_op jit(solution)/shard_map/ppermute | solution.py:195
  210.9 45.4 %collective-permute-start.18 = (bf16[256,2048]{1,0:T(8,128)(2,1)S(1)}, bf16[256,2048]{1,0:T(8,128)(2,1)S(1)}, u32[]{:S(2)}, u32[]{:S(2)}) collective-permute-start(bf16[256,2048]{1,0:T(8,128)(2,1)S(1)} %fusion.18), channel_id=1, source_target_pairs={{0,2},{1,3},{2,0},{3,1},{4,6},{5,7},{6,4},{7,5},{8,10},{9,11},{10,... | collective-permute-start | bytes 3145736 | tf_op jit(solution)/shard_map/ppermute | solution.py:195
  211.6 53.5 %collective-permute-start.19 = (bf16[256,4608]{0,1:T(8,128)(2,1)}, bf16[256,4608]{0,1:T(8,128)(2,1)S(1)}, u32[]{:S(2)}, u32[]{:S(2)}) collective-permute-start(bf16[256,4608]{0,1:T(8,128)(2,1)} %collective-permute-done.13), channel_id=1, source_target_pairs={{0,8},{8,16},{16,24},{24,28},{28,20},{20,12},{12,4},{4,0},{1,9},{9... | collective-permute-start | bytes 7077896 | tf_op jit(solution)/shard_map/ppermute | solution.py:70
  214.1 52.9 %collective-permute-start.20 = (bf16[256,4608]{0,1:T(8,128)(2,1)}, bf16[256,4608]{0,1:T(8,128)(2,1)S(1)}, u32[]{:S(2)}, u32[]{:S(2)}) collective-permute-start(bf16[256,4608]{0,1:T(8,128)(2,1)} %collective-permute-done.14), channel_id=1, source_target_pairs={{0,4},{8,0},{16,8},{24,16},{28,24},{20,28},{12,20},{4,12},{1,5},{9... | collective-permute-start | bytes 7077896 | tf_op jit(solution)/shard_map/ppermute | solution.py:70
  259.6 30.5 %collective-permute-start.24 = (bf16[256,2048]{1,0:T(8,128)(2,1)S(1)}, bf16[256,2048]{1,0:T(8,128)(2,1)S(1)}, u32[]{:S(2)}, u32[]{:S(2)}) collective-permute-start(bf16[256,2048]{1,0:T(8,128)(2,1)S(1)} %get-tuple-element.422), channel_id=1, source_target_pairs={{0,1},{1,0},{2,3},{3,2},{4,5},{5,4},{6,7},{7,6},{8,9},{9,8},{10,11... | collective-permute-start | bytes 3145736 | tf_op jit(solution)/shard_map/ppermute | solution.py:191
  268.6 23.2 %collective-permute-start.23 = (bf16[256,2048]{1,0:T(8,128)(2,1)S(1)}, bf16[256,2048]{1,0:T(8,128)(2,1)S(1)}, u32[]{:S(2)}, u32[]{:S(2)}) collective-permute-start(bf16[256,2048]{1,0:T(8,128)(2,1)S(1)} %get-tuple-element.202), channel_id=1, source_target_pairs={{0,1},{1,0},{2,3},{3,2},{4,5},{5,4},{6,7},{7,6},{8,9},{9,8},{10,11... | collective-permute-start | bytes 3145736 | tf_op jit(solution)/shard_map/ppermute | solution.py:191
  268.7 28.4 %collective-permute-start.22 = (bf16[256,2304]{0,1:T(8,128)(2,1)S(1)}, bf16[256,2304]{0,1:T(8,128)(2,1)S(1)}, u32[]{:S(2)}, u32[]{:S(2)}) collective-permute-start(bf16[256,2304]{0,1:T(8,128)(2,1)S(1)} %slice.403), channel_id=1, source_target_pairs={{0,4},{8,0},{16,8},{24,16},{28,24},{20,28},{12,20},{4,12},{1,5},{9... | collective-permute-start | bytes 3538952 | tf_op jit(solution)/shard_map/ppermute | solution.py:70
  269.0 28.7 %collective-permute-start.21 = (bf16[256,2304]{0,1:T(8,128)(2,1)S(1)}, bf16[256,2304]{0,1:T(8,128)(2,1)S(1)}, u32[]{:S(2)}, u32[]{:S(2)}) collective-permute-start(bf16[256,2304]{0,1:T(8,128)(2,1)S(1)} %slice.402), channel_id=1, source_target_pairs={{0,8},{8,16},{16,24},{24,28},{28,20},{20,12},{12,4},{4,0},{1,9},{9... | collective-permute-start | bytes 3538952 | tf_op jit(solution)/shard_map/ppermute | solution.py:70
  320.0 18.9 %collective-permute-start.25 = (bf16[1536,256]{1,0:T(8,128)(2,1)S(1)}, bf16[1536,256]{1,0:T(8,128)(2,1)S(1)}, u32[]{:S(2)}, u32[]{:S(2)}) collective-permute-start(bf16[1536,256]{1,0:T(8,128)(2,1)S(1)} %convolution_convert_fusion.11), channel_id=1, source_target_pairs={{0,8},{8,16},{16,24},{24,28},{28,20},{20,12},{12,4},{4,0},{1,9},{9... | collective-permute-start | bytes 2359304 | tf_op jit(solution)/shard_map/ppermute | solution.py:70
  321.7 18.7 %collective-permute-start.26 = (bf16[1536,256]{1,0:T(8,128)(2,1)S(1)}, bf16[1536,256]{1,0:T(8,128)(2,1)S(1)}, u32[]{:S(2)}, u32[]{:S(2)}) collective-permute-start(bf16[1536,256]{1,0:T(8,128)(2,1)S(1)} %convolution_convert_fusion.10), channel_id=1, source_target_pairs={{0,4},{8,0},{16,8},{24,16},{28,24},{20,28},{12,20},{4,12},{1,5},{9... | collective-permute-start | bytes 2359304 | tf_op jit(solution)/shard_map/ppermute | solution.py:70
  342.5 20.9 %collective-permute-start.27 = (bf16[1536,256]{1,0:T(8,128)(2,1)S(1)}, bf16[1536,256]{1,0:T(8,128)(2,1)S(1)}, u32[]{:S(2)}, u32[]{:S(2)}) collective-permute-start(bf16[1536,256]{1,0:T(8,128)(2,1)S(1)} %fusion.21), channel_id=1, source_target_pairs={{0,8},{8,16},{16,24},{24,28},{28,20},{20,12},{12,4},{4,0},{1,9},{9... | collective-permute-start | bytes 2359304 | tf_op jit(solution)/shard_map/ppermute | solution.py:70
  343.8 19.7 %collective-permute-start.28 = (bf16[1536,256]{1,0:T(8,128)(2,1)S(1)}, bf16[1536,256]{1,0:T(8,128)(2,1)S(1)}, u32[]{:S(2)}, u32[]{:S(2)}) collective-permute-start(bf16[1536,256]{1,0:T(8,128)(2,1)S(1)} %fusion.22), channel_id=1, source_target_pairs={{0,4},{8,0},{16,8},{24,16},{28,24},{20,28},{12,20},{4,12},{1,5},{9... | collective-permute-start | bytes 2359304 | tf_op jit(solution)/shard_map/ppermute | solution.py:70
  369.3 25.1 %collective-permute-start.36 = (bf16[512,2048]{1,0:T(8,128)(2,1)}, bf16[512,2048]{1,0:T(8,128)(2,1)}, u32[]{:S(2)}, u32[]{:S(2)}) collective-permute-start(bf16[512,2048]{1,0:T(8,128)(2,1)} %pad_maximum_fusion.3), channel_id=1, source_target_pairs={{0,1},{1,0},{2,3},{3,2},{4,5},{5,4},{6,7},{7,6},{8,9},{9,8},{10,11... | collective-permute-start | bytes 6291464 | tf_op jit(solution)/shard_map/ppermute | solution.py:191
  369.3 20.5 %collective-permute-start.29 = (bf16[1536,256]{1,0:T(8,128)(2,1)}, bf16[1536,256]{1,0:T(8,128)(2,1)S(1)}, u32[]{:S(2)}, u32[]{:S(2)}) collective-permute-start(bf16[1536,256]{1,0:T(8,128)(2,1)} %fusion.20), channel_id=1, source_target_pairs={{0,8},{8,16},{16,24},{24,28},{28,20},{20,12},{12,4},{4,0},{1,9},{9... | collective-permute-start | bytes 2359304 | tf_op jit(solution)/shard_map/ppermute | solution.py:70
  370.5 20.8 %collective-permute-start.30 = (bf16[1536,256]{1,0:T(8,128)(2,1)}, bf16[1536,256]{1,0:T(8,128)(2,1)S(1)}, u32[]{:S(2)}, u32[]{:S(2)}) collective-permute-start(bf16[1536,256]{1,0:T(8,128)(2,1)} %fusion.23), channel_id=1, source_target_pairs={{0,4},{8,0},{16,8},{24,16},{28,24},{20,28},{12,20},{4,12},{1,5},{9... | collective-permute-start | bytes 2359304 | tf_op jit(solution)/shard_map/ppermute | solution.py:70
  376.5 47.8 %collective-permute-start.33 = (bf16[256,1536]{1,0:T(8,128)(2,1)S(1)}, bf16[256,1536]{1,0:T(8,128)(2,1)S(1)}, u32[]{:S(2)}, u32[]{:S(2)}) collective-permute-start(bf16[256,1536]{1,0:T(8,128)(2,1)S(1)} %get-tuple-element.231), channel_id=1, source_target_pairs={{0,8},{8,16},{16,24},{24,28},{28,20},{20,12},{12,4},{4,0},{1,9},{9... | collective-permute-start | bytes 2359304 | tf_op jit(solution)/shard_map/ppermute | solution.py:70
  377.7 46.6 %collective-permute-start.34 = (bf16[256,1536]{1,0:T(8,128)(2,1)S(1)}, bf16[256,1536]{1,0:T(8,128)(2,1)S(1)}, u32[]{:S(2)}, u32[]{:S(2)}) collective-permute-start(bf16[256,1536]{1,0:T(8,128)(2,1)S(1)} %get-tuple-element.232), channel_id=1, source_target_pairs={{0,4},{8,0},{16,8},{24,16},{28,24},{20,28},{12,20},{4,12},{1,5},{9... | collective-permute-start | bytes 2359304 | tf_op jit(solution)/shard_map/ppermute | solution.py:70
  393.6 30.8 %collective-permute-start.35 = (bf16[1536,256]{1,0:T(8,128)(2,1)S(1)}, bf16[1536,256]{1,0:T(8,128)(2,1)S(1)}, u32[]{:S(2)}, u32[]{:S(2)}) collective-permute-start(bf16[1536,256]{1,0:T(8,128)(2,1)S(1)} %fusion.19), channel_id=1, source_target_pairs={{0,4},{8,0},{16,8},{24,16},{28,24},{20,28},{12,20},{4,12},{1,5},{9... | collective-permute-start | bytes 2359304 | tf_op jit(solution)/shard_map/ppermute | solution.py:70
  396.8 23.6 %collective-permute-start.37 = (bf16[256,2048]{1,0:T(8,128)(2,1)S(1)}, bf16[256,2048]{1,0:T(8,128)(2,1)S(1)}, u32[]{:S(2)}, u32[]{:S(2)}) collective-permute-start(bf16[256,2048]{1,0:T(8,128)(2,1)S(1)} %get-tuple-element.397), channel_id=1, source_target_pairs={{0,2},{1,3},{2,0},{3,1},{4,6},{5,7},{6,4},{7,5},{8,10},{9,11},{10,... | collective-permute-start | bytes 3145736 | tf_op jit(solution)/shard_map/ppermute | solution.py:195
  401.9 36.5 %collective-permute-start.31 = (bf16[512,2048]{1,0:T(8,128)(2,1)S(1)}, bf16[512,2048]{1,0:T(8,128)(2,1)S(1)}, u32[]{:S(2)}, u32[]{:S(2)}) collective-permute-start(bf16[512,2048]{1,0:T(8,128)(2,1)S(1)} %convolution_convert_fusion.5), channel_id=1, source_target_pairs={{0,1},{1,0},{2,3},{3,2},{4,5},{5,4},{6,7},{7,6},{8,9},{9,8},{10,11... | collective-permute-start | bytes 6291464 | tf_op jit(solution)/shard_map/ppermute | solution.py:191
  420.3 24.2 %collective-permute-start.41 = (bf16[256,2048]{1,0:T(8,128)(2,1)S(1)}, bf16[256,2048]{1,0:T(8,128)(2,1)S(1)}, u32[]{:S(2)}, u32[]{:S(2)}) collective-permute-start(bf16[256,2048]{1,0:T(8,128)(2,1)S(1)} %get-tuple-element.396), channel_id=1, source_target_pairs={{0,2},{1,3},{2,0},{3,1},{4,6},{5,7},{6,4},{7,5},{8,10},{9,11},{10,... | collective-permute-start | bytes 3145736 | tf_op jit(solution)/shard_map/ppermute | solution.py:195
  436.4 9.9 %collective-permute-start.40 = (bf16[256,2048]{1,0:T(8,128)(2,1)S(1)}, bf16[256,2048]{1,0:T(8,128)(2,1)S(1)}, u32[]{:S(2)}, u32[]{:S(2)}) collective-permute-start(bf16[256,2048]{1,0:T(8,128)(2,1)S(1)} %get-tuple-element.382), channel_id=1, source_target_pairs={{0,1},{1,0},{2,3},{3,2},{4,5},{5,4},{6,7},{7,6},{8,9},{9,8},{10,11... | collective-permute-start | bytes 3145736 | tf_op jit(solution)/shard_map/ppermute | solution.py:191
  436.4 37.1 %collective-permute-start.38 = (bf16[256,3072]{1,0:T(8,128)(2,1)}, bf16[256,3072]{1,0:T(8,128)(2,1)}, u32[]{:S(2)}, u32[]{:S(2)}) collective-permute-start(bf16[256,3072]{1,0:T(8,128)(2,1)} %fusion.11), channel_id=1, source_target_pairs={{0,8},{8,16},{16,24},{24,28},{28,20},{20,12},{12,4},{4,0},{1,9},{9... | collective-permute-start | bytes 4718600 | tf_op jit(solution)/shard_map/ppermute | solution.py:70
  437.9 36.8 %collective-permute-start.39 = (bf16[256,3072]{1,0:T(8,128)(2,1)}, bf16[256,3072]{1,0:T(8,128)(2,1)}, u32[]{:S(2)}, u32[]{:S(2)}) collective-permute-start(bf16[256,3072]{1,0:T(8,128)(2,1)} %fusion.12), channel_id=1, source_target_pairs={{0,4},{8,0},{16,8},{24,16},{28,24},{20,28},{12,20},{4,12},{1,5},{9... | collective-permute-start | bytes 4718600 | tf_op jit(solution)/shard_map/ppermute | solution.py:70
  443.4 50.5 %collective-permute-start.32 = (bf16[512,2048]{1,0:T(8,128)(2,1)}, bf16[512,2048]{1,0:T(8,128)(2,1)}, u32[]{:S(2)}, u32[]{:S(2)}) collective-permute-start(bf16[512,2048]{1,0:T(8,128)(2,1)} %add_convert_fusion), channel_id=1, source_target_pairs={{0,2},{1,3},{2,0},{3,1},{4,6},{5,7},{6,4},{7,5},{8,10},{9,11},{10,... | collective-permute-start | bytes 6291464 | tf_op jit(solution)/shard_map/ppermute | solution.py:195
  488.3 10.7 %collective-permute-start.42 = (bf16[256,2048]{1,0:T(8,128)(2,1)S(1)}, bf16[256,2048]{1,0:T(8,128)(2,1)S(1)}, u32[]{:S(2)}, u32[]{:S(2)}) collective-permute-start(bf16[256,2048]{1,0:T(8,128)(2,1)S(1)} %get-tuple-element.380), channel_id=1, source_target_pairs={{0,1},{1,0},{2,3},{3,2},{4,5},{5,4},{6,7},{7,6},{8,9},{9,8},{10,11... | collective-permute-start | bytes 3145736 | tf_op jit(solution)/shard_map/ppermute | solution.py:191
  491.9 36.7 %collective-permute-start.44 = (bf16[256,3072]{1,0:T(8,128)(2,1)}, bf16[256,3072]{1,0:T(8,128)(2,1)}, u32[]{:S(2)}, u32[]{:S(2)}) collective-permute-start(bf16[256,3072]{1,0:T(8,128)(2,1)} %fusion.10), channel_id=1, source_target_pairs={{0,8},{8,16},{16,24},{24,28},{28,20},{20,12},{12,4},{4,0},{1,9},{9... | collective-permute-start | bytes 4718600 | tf_op jit(solution)/shard_map/ppermute | solution.py:70
  492.2 36.5 %collective-permute-start.45 = (bf16[256,3072]{1,0:T(8,128)(2,1)}, bf16[256,3072]{1,0:T(8,128)(2,1)}, u32[]{:S(2)}, u32[]{:S(2)}) collective-permute-start(bf16[256,3072]{1,0:T(8,128)(2,1)} %fusion.13), channel_id=1, source_target_pairs={{0,4},{8,0},{16,8},{24,16},{28,24},{20,28},{12,20},{4,12},{1,5},{9... | collective-permute-start | bytes 4718600 | tf_op jit(solution)/shard_map/ppermute | solution.py:70
  519.6 25.7 %collective-permute-start.43 = (bf16[2,256,2048]{2,1,0:T(8,128)(2,1)S(1)}, bf16[2,256,2048]{2,1,0:T(8,128)(2,1)}, u32[]{:S(2)}, u32[]{:S(2)}) collective-permute-start(bf16[2,256,2048]{2,1,0:T(8,128)(2,1)S(1)} %bitcast.131), channel_id=1, source_target_pairs={{0,1},{1,0},{2,3},{3,2},{4,5},{5,4},{6,7},{7,6},{8,9},{9,8},{10,11... | collective-permute-start | bytes 6291464 | tf_op jit(solution)/shard_map/ppermute | solution.py:191
  530.0 22.5 %collective-permute-start.48 = (bf16[512,512]{1,0:T(8,128)(2,1)}, bf16[512,512]{1,0:T(8,128)(2,1)S(1)}, u32[]{:S(2)}, u32[]{:S(2)}) collective-permute-start(bf16[512,512]{1,0:T(8,128)(2,1)} %get-tuple-element.415), channel_id=1, source_target_pairs={{12,0},{0,12},{28,16},{16,28},{13,1},{1,13},{29,17},{17,29},{14,2}... | collective-permute-start | bytes 1572872 | tf_op jit(solution)/shard_map/ppermute | solution.py:799
  533.5 19.0 %collective-permute-start.47 = (bf16[512,512]{1,0:T(8,128)(2,1)}, bf16[512,512]{1,0:T(8,128)(2,1)S(1)}, u32[]{:S(2)}, u32[]{:S(2)}) collective-permute-start(bf16[512,512]{1,0:T(8,128)(2,1)} %get-tuple-element.416), channel_id=1, source_target_pairs={{8,0},{4,12},{24,16},{20,28},{9,1},{5,13},{25,17},{21,29},{10,2},{... | collective-permute-start | bytes 1572872 | tf_op jit(solution)/shard_map/ppermute | solution.py:799
  534.8 22.5 %collective-permute-start.46 = (bf16[512,512]{1,0:T(8,128)(2,1)}, bf16[512,512]{1,0:T(8,128)(2,1)S(1)}, u32[]{:S(2)}, u32[]{:S(2)}) collective-permute-start(bf16[512,512]{1,0:T(8,128)(2,1)} %get-tuple-element.417), channel_id=1, source_target_pairs={{4,0},{8,12},{20,16},{24,28},{5,1},{9,13},{21,17},{25,29},{6,2},{1... | collective-permute-start | bytes 1572872 | tf_op jit(solution)/shard_map/ppermute | solution.py:799
  557.4 36.6 %collective-permute-start.49 = (bf16[256,3072]{1,0:T(8,128)(2,1)}, bf16[256,3072]{1,0:T(8,128)(2,1)}, u32[]{:S(2)}, u32[]{:S(2)}) collective-permute-start(bf16[256,3072]{1,0:T(8,128)(2,1)} %fusion.14), channel_id=1, source_target_pairs={{0,8},{8,16},{16,24},{24,28},{28,20},{20,12},{12,4},{4,0},{1,9},{9... | collective-permute-start | bytes 4718600 | tf_op jit(solution)/shard_map/ppermute | solution.py:70
  557.4 36.6 %collective-permute-start.50 = (bf16[256,3072]{1,0:T(8,128)(2,1)}, bf16[256,3072]{1,0:T(8,128)(2,1)}, u32[]{:S(2)}, u32[]{:S(2)}) collective-permute-start(bf16[256,3072]{1,0:T(8,128)(2,1)} %fusion.15), channel_id=1, source_target_pairs={{0,4},{8,0},{16,8},{24,16},{28,24},{20,28},{12,20},{4,12},{1,5},{9... | collective-permute-start | bytes 4718600 | tf_op jit(solution)/shard_map/ppermute | solution.py:70
  597.2 15.1 %collective-permute-start.53 = (bf16[256,768]{1,0:T(8,128)(2,1)S(1)}, bf16[256,768]{1,0:T(8,128)(2,1)S(1)}, u32[]{:S(2)}, u32[]{:S(2)}) collective-permute-start(bf16[256,768]{1,0:T(8,128)(2,1)S(1)} %slice.516), channel_id=1, source_target_pairs={{0,8},{8,16},{16,24},{24,28},{28,20},{20,12},{12,4},{4,0},{1,9},{9... | collective-permute-start | bytes 1179656 | tf_op jit(solution)/shard_map/ppermute | solution.py:70
  598.8 13.5 %collective-permute-start.54 = (bf16[256,896]{1,0:T(8,128)(2,1)S(1)}, bf16[256,896]{1,0:T(8,128)(2,1)S(1)}, u32[]{:S(2)}, u32[]{:S(2)}) collective-permute-start(bf16[256,896]{1,0:T(8,128)(2,1)S(1)} %pad_maximum_fusion.10), channel_id=1, source_target_pairs={{0,4},{8,0},{16,8},{24,16},{28,24},{20,28},{12,20},{4,12},{1,5},{9... | collective-permute-start | bytes 1376264 | tf_op jit(solution)/shard_map/ppermute | solution.py:70
  612.7 26.1 %collective-permute-start.60 = (bf16[256,2048]{1,0:T(8,128)(2,1)S(1)}, bf16[256,2048]{1,0:T(8,128)(2,1)S(1)}, u32[]{:S(2)}, u32[]{:S(2)}) collective-permute-start(bf16[256,2048]{1,0:T(8,128)(2,1)S(1)} %add_convert_fusion.1.chip_ref), channel_id=1, source_target_pairs={{0,2},{1,3},{2,0},{3,1},{4,6},{5,7},{6,4},{7,5},{8,10},{9,11},{10,... | collective-permute-start | bytes 3145736 | tf_op jit(solution)/shard_map/ppermute | solution.py:195
  614.2 20.7 %collective-permute-start.56 = (bf16[256,1664]{1,0:T(8,128)(2,1)S(1)}, bf16[256,1664]{1,0:T(8,128)(2,1)S(1)}, u32[]{:S(2)}, u32[]{:S(2)}) collective-permute-start(bf16[256,1664]{1,0:T(8,128)(2,1)S(1)} %fusion.34), channel_id=1, source_target_pairs={{0,8},{8,16},{16,24},{24,28},{28,20},{20,12},{12,4},{4,0},{1,9},{9... | collective-permute-start | bytes 2555912 | tf_op jit(solution)/shard_map/ppermute | solution.py:70
  615.8 20.3 %collective-permute-start.57 = (bf16[256,1664]{1,0:T(8,128)(2,1)S(1)}, bf16[256,1664]{1,0:T(8,128)(2,1)S(1)}, u32[]{:S(2)}, u32[]{:S(2)}) collective-permute-start(bf16[256,1664]{1,0:T(8,128)(2,1)S(1)} %fusion.35), channel_id=1, source_target_pairs={{0,4},{8,0},{16,8},{24,16},{28,24},{20,28},{12,20},{4,12},{1,5},{9... | collective-permute-start | bytes 2555912 | tf_op jit(solution)/shard_map/ppermute | solution.py:70
  620.5 14.4 %collective-permute-start.58 = (f32[2,128]{1,0:T(2,128)S(1)}, f32[2,128]{1,0:T(2,128)S(1)}, u32[]{:S(2)}, u32[]{:S(2)}) collective-permute-start(f32[2,128]{1,0:T(2,128)S(1)} %fusion.178), channel_id=1, source_target_pairs={{0,4},{4,0},{8,12},{12,8},{16,20},{20,16},{24,28},{28,24},{1,5},{5... | collective-permute-start | bytes 3080 | tf_op jit(solution)/shard_map/ppermute | solution.py:200
  623.2 37.2 %collective-permute-start.64 = (bf16[256,2048]{1,0:T(8,128)(2,1)S(1)}, bf16[256,2048]{1,0:T(8,128)(2,1)S(1)}, u32[]{:S(2)}, u32[]{:S(2)}) collective-permute-start(bf16[256,2048]{1,0:T(8,128)(2,1)S(1)} %add_convert_fusion.2.chip_ref), channel_id=1, source_target_pairs={{0,2},{1,3},{2,0},{3,1},{4,6},{5,7},{6,4},{7,5},{8,10},{9,11},{10,... | collective-permute-start | bytes 3145736 | tf_op jit(solution)/shard_map/ppermute | solution.py:195
  640.1 20.6 %collective-permute-start.61 = (bf16[256,1664]{1,0:T(8,128)(2,1)}, bf16[256,1664]{1,0:T(8,128)(2,1)}, u32[]{:S(2)}, u32[]{:S(2)}) collective-permute-start(bf16[256,1664]{1,0:T(8,128)(2,1)} %fusion.33), channel_id=1, source_target_pairs={{0,8},{8,16},{16,24},{24,28},{28,20},{20,12},{12,4},{4,0},{1,9},{9... | collective-permute-start | bytes 2555912 | tf_op jit(solution)/shard_map/ppermute | solution.py:70
  641.8 19.0 %collective-permute-start.62 = (bf16[256,1664]{1,0:T(8,128)(2,1)S(1)}, bf16[256,1664]{1,0:T(8,128)(2,1)}, u32[]{:S(2)}, u32[]{:S(2)}) collective-permute-start(bf16[256,1664]{1,0:T(8,128)(2,1)S(1)} %fusion.36), channel_id=1, source_target_pairs={{0,4},{8,0},{16,8},{24,16},{28,24},{20,28},{12,20},{4,12},{1,5},{9... | collective-permute-start | bytes 2555912 | tf_op jit(solution)/shard_map/ppermute | solution.py:70
  645.1 15.6 %collective-permute-start.63 = (f32[2,128]{1,0:T(2,128)S(1)}, f32[2,128]{1,0:T(2,128)S(1)}, u32[]{:S(2)}, u32[]{:S(2)}) collective-permute-start(f32[2,128]{1,0:T(2,128)S(1)} %add.438), channel_id=1, source_target_pairs={{0,8},{4,12},{8,0},{12,4},{16,24},{20,28},{24,16},{28,20},{1,9},{5... | collective-permute-start | bytes 3080 | tf_op jit(solution)/shard_map/ppermute | solution.py:200
  660.4 16.2 %collective-permute-start.68 = (f32[256,2048]{1,0:T(8,128)}, f32[256,2048]{1,0:T(8,128)S(1)}, u32[]{:S(2)}, u32[]{:S(2)}) collective-permute-start(f32[256,2048]{1,0:T(8,128)} %input_back.2.refs_0_), channel_id=1, source_target_pairs={{0,1},{1,0},{2,3},{3,2},{4,5},{5,4},{6,7},{7,6},{8,9},{9,8},{10,11... | collective-permute-start | bytes 6291464 | tf_op jit(solution)/shard_map/ppermute | solution.py:191
  669.6 7.0 %collective-permute-start.69 = (f32[256,2048]{1,0:T(8,128)}, f32[256,2048]{1,0:T(8,128)S(1)}, u32[]{:S(2)}, u32[]{:S(2)}) collective-permute-start(f32[256,2048]{1,0:T(8,128)} %input_back.3.refs_1_), channel_id=1, source_target_pairs={{0,1},{1,0},{2,3},{3,2},{4,5},{5,4},{6,7},{7,6},{8,9},{9,8},{10,11... | collective-permute-start | bytes 6291464 | tf_op jit(solution)/shard_map/ppermute | solution.py:191
  669.7 22.5 %collective-permute-start.65 = (bf16[256,1664]{1,0:T(8,128)(2,1)}, bf16[256,1664]{1,0:T(8,128)(2,1)}, u32[]{:S(2)}, u32[]{:S(2)}) collective-permute-start(bf16[256,1664]{1,0:T(8,128)(2,1)} %fusion.32), channel_id=1, source_target_pairs={{0,8},{8,16},{16,24},{24,28},{28,20},{20,12},{12,4},{4,0},{1,9},{9... | collective-permute-start | bytes 2555912 | tf_op jit(solution)/shard_map/ppermute | solution.py:70
  671.4 21.3 %collective-permute-start.66 = (bf16[256,1664]{1,0:T(8,128)(2,1)}, bf16[256,1664]{1,0:T(8,128)(2,1)}, u32[]{:S(2)}, u32[]{:S(2)}) collective-permute-start(bf16[256,1664]{1,0:T(8,128)(2,1)} %fusion.37), channel_id=1, source_target_pairs={{0,4},{8,0},{16,8},{24,16},{28,24},{20,28},{12,20},{4,12},{1,5},{9... | collective-permute-start | bytes 2555912 | tf_op jit(solution)/shard_map/ppermute | solution.py:70
  673.3 19.0 %collective-permute-start.67 = (f32[2,128]{1,0:T(2,128)S(1)}, f32[2,128]{1,0:T(2,128)S(1)}, u32[]{:S(2)}, u32[]{:S(2)}) collective-permute-start(f32[2,128]{1,0:T(2,128)S(1)} %add.446), channel_id=1, source_target_pairs={{0,16},{4,20},{8,24},{12,28},{16,0},{20,4},{24,8},{28,12},{1,17},{... | collective-permute-start | bytes 3080 | tf_op jit(solution)/shard_map/ppermute | solution.py:200
  (99 other events, 856.8 us)

commit v4 on v3

--- a/solution.py
+++ b/solution.py
@@ -256,6 +256,15 @@
     gradient = chip_ref[...].astype(f32) + other_ref[...].astype(f32)
     back, _ = rms_back(values, recip_rms(values), gain_ref[...], gradient)
     out_ref[...] = base_ref[...] + back
+
+
+def pack_kernel(*refs):
+    out_ref, start = refs[-1], 0
+    for ref in refs[:-2]:
+        end = start + ref.shape[1]
+        out_ref[:, start:end] = ref[...]
+        start = end
+    out_ref[:, start:] = refs[-2][...].T
 
 
 def heads_kernel(sizes, proj_ref, cos_ref, sin_ref, gain_ref, q_ref, kv_ref, gate_ref):
@@ -468,8 +477,17 @@
     small = jnp.pad(head_gate_weight, ((0, 0), (0, extra - head_count)))
     small = jnp.where(lane == head_count, norm_attn[:, None], small)
     small = jnp.where(lane == head_count + 1, norm_mlp[:, None], small)
-    packed = jnp.concatenate([query_weight, key_matrix, value_matrix, small], axis=1)
-    in_ring = Gather(jnp.concatenate([packed, out_weight.T], axis=1), count)
+    parts = (query_weight, key_matrix, value_matrix, small)
+    packed_cols = sum(part.shape[1] for part in parts)
+    in_block = pl.pallas_call(
+        pack_kernel,
+        out_shape=jax.ShapeDtypeStruct((depth, packed_cols + out_weight.shape[0]), bf16),
+        compiler_params=pltpu.CompilerParams(vmem_limit_bytes=vmem_bytes),
+        cost_estimate=cost(1024, 1024),
+        name="pack",
+    )(*parts, out_weight)
+    packed = in_block[:, :packed_cols]
+    in_ring = Gather(in_block, count)
     in_ring.issue()
 
     params = pltpu.CompilerParams(vmem_limit_bytes=vmem_bytes)

time: 712 us -> 708 us (level)
    unnamed x223 -> x214, local copies, waits for them, and re-layouts: 51.4 us -> 45.5 us
where the time goes in v4:
time: 708 us; the launch traced here: 697 us
  waiting for transfers between devices  255 us (36%)
  matrix products  150 us (21%)
  Pallas kernels  99.1 us (14%)
  starting transfers between devices  73.2 us (10%)
  other arithmetic  62.1 us (9%)
  local copies, waits for them, and re-layouts  55.3 us (8%)
    ppermute x39, waiting for transfers between devices, ring_step(): return lax.ppermute(block, 'dp', route)  122 us
    ppermute x9, waiting for transfers between devices, swap_x(): lax.ppermute(block, 'mp', [(i, i ^ 2) for i in range(lax.axis_size('mp'))])  71.8 us
    dot_general x32, matrix products, transpose_by(): lax.dot_general(left_side, right_side, (((0,), (0,)), ((), ())), preferre...  71.7 us
    unnamed x214, local copies, waits for them, and re-layouts  45.5 us
    ppermute x39, starting transfers between devices, ring_step(): return lax.ppermute(block, 'dp', route)  42.7 us
    dot_general x5, matrix products, product(): return jnp.dot(left_side, right_side, preferred_element_type=f32)  39.4 us
    dot_general x9, matrix products, by_transpose(): lax.dot_general(left_side, right_side, (((1,), (1,)), ((), ())), preferre...  38.5 us
    ppermute x1, waiting for transfers between devices, on_device(): by_both = lax.ppermute(sent, 'dp', group_route(3, (0, 3)))  33.9 us
  transfers between devices with their start and end apart: 72, of which 39 were waited for; matrix products, arithmetic and copies ran while one was open for 31% of the time, Pallas kernels for 14%

profile of v4, /device:TPU:0, one launch (start us, length us, event | category | flops | bytes accessed | tf_op | source)
XLA Modules:
  0.0 697.2 jit_solution(17388497392147219167)
XLA Ops:
  5.3 3.0 collective-permute-start.1
  13.2 7.5 %bring_tokens.1 = bf16[2,2,256,2048]{3,2,1,0:T(8,128)(2,1)} custom-call(s32[8]{0:T(128)} %gather_fusion, s32[1]{0:T(128)} %bitcast.1.core_ref, bf16[2,2,256,2048]{3,2,1,0:T(8,128)(2,1)} %bitcast.134), custom_call_target="tpu_custom_call" | custom-call | bytes 8388608 | tf_op jit(solution)/shard_map/bring_tokens/pallas_call | solution.py:513
  21.5 6.1 collective-permute-done.1
  32.9 3.1 multiply_reduce_fusion
  36.0 12.7 %collective-permute-done.2 = bf16[256,1664]{1,0:T(8,128)(2,1)S(1)} collective-permute-done((bf16[256,1664]{1,0:T(8,128)(2,1)}, bf16[256,1664]{1,0:T(8,128)(2,1)S(1)}, u32[]{:S(2)}, u32[]{:S(2)}) %collective-permute-start.2) | collective-permute-done | bytes 852000 | tf_op jit(solution)/shard_map/ppermute | solution.py:70
  53.3 14.4 %collective-permute-done.4 = bf16[256,1664]{1,0:T(8,128)(2,1)S(1)} collective-permute-done((bf16[256,1664]{1,0:T(8,128)(2,1)S(1)}, bf16[256,1664]{1,0:T(8,128)(2,1)S(1)}, u32[]{:S(2)}, u32[]{:S(2)}) %collective-permute-start.4) | collective-permute-done | bytes 852000 | tf_op jit(solution)/shard_map/ppermute | solution.py:70
  73.7 3.0 collective-permute-done.6
  76.7 4.6 collective-permute-done.7
  87.5 7.3 %fusion.124.proj_ref = f32[1024,1152]{1,0:T(8,128)} fusion(bf16[1024,2048]{1,0:T(8,128)(2,1)S(1)} %multiply_convert_fusion, bf16[2048,1152]{1,0:T(8,128)(2,1)S(1)} %fusion.47), kind=kOutput, calls=%fused_computation.303 | convolution fusion | flops 4831838208 | bytes 13631488 | tf_op jit(solution)/shard_map/dot_general | solution.py:21
  94.8 6.5 heads.1
  105.8 3.3 collective-permute-start.11
  111.3 33.9 %collective-permute-done.12 = bf16[512,512]{1,0:T(8,128)(2,1)} collective-permute-done((bf16[512,512]{1,0:T(8,128)(2,1)}, bf16[512,512]{1,0:T(8,128)(2,1)}, u32[]{:S(2)}, u32[]{:S(2)}) %collective-permute-start.12) | collective-permute-done | bytes 524320 | tf_op jit(solution)/shard_map/ppermute | solution.py:632
  145.2 7.1 %collective-permute-done.11 = bf16[512,512]{1,0:T(8,128)(2,1)} collective-permute-done((bf16[512,512]{1,0:T(8,128)(2,1)}, bf16[512,512]{1,0:T(8,128)(2,1)}, u32[]{:S(2)}, u32[]{:S(2)}) %collective-permute-start.11) | collective-permute-done | bytes 524320 | tf_op jit(solution)/shard_map/ppermute | solution.py:631
  165.8 14.0 %attend.1 = (bf16[1024,512]{1,0:T(8,128)(2,1)}, f32[1024,512]{1,0:T(8,128)}, f32[1024,128]{1,0:T(8,128)}) custom-call(s32[2]{0:T(128)} %add_convert_fusion.5.flag_ref, bf16[1024,512]{1,0:T(8,128)(2,1)} %get-tuple-element.190.q_ref, bf16[1024,512]{1,0:T(8,128)(2,1)} %get-tuple-element.186.kv_ref, bf16[1024,512]{1,0:T(8,128)(2,1)} %pad_maximum_fusion.5.far_ref, ...), custom_call_target="tpu_custom_call" | custom-call | flops 2147483648 | bytes 6291456 | tf_op jit(solution)/shard_map/attend/pallas_call | solution.py:642
  179.8 7.4 %bring_cotangent.1 = bf16[2,2,256,2048]{3,2,1,0:T(8,128)(2,1)} custom-call(s32[8]{0:T(128)} %gather_fusion, s32[1]{0:T(128)} %bitcast.1.core_ref, bf16[2,2,256,2048]{3,2,1,0:T(8,128)(2,1)} %bitcast.135), custom_call_target="tpu_custom_call" | custom-call | bytes 8388608 | tf_op jit(solution)/shard_map/bring_cotangent/pallas_call | solution.py:513
  187.2 12.7 %collective-permute-done.13 = bf16[256,4608]{0,1:T(8,128)(2,1)} collective-permute-done((bf16[256,4608]{0,1:T(8,128)(2,1)}, bf16[256,4608]{0,1:T(8,128)(2,1)}, u32[]{:S(2)}, u32[]{:S(2)}) %collective-permute-start.13) | collective-permute-done | bytes 2359328 | tf_op jit(solution)/shard_map/ppermute | solution.py:70
  210.8 19.5 %collective-permute-done.16 = bf16[256,2048]{1,0:T(8,128)(2,1)S(1)} collective-permute-done((bf16[256,2048]{1,0:T(8,128)(2,1)S(1)}, bf16[256,2048]{1,0:T(8,128)(2,1)S(1)}, u32[]{:S(2)}, u32[]{:S(2)}) %collective-permute-start.16) | collective-permute-done | bytes 1048608 | tf_op jit(solution)/shard_map/ppermute | solution.py:195
  230.2 21.7 %collective-permute-done.18 = bf16[256,2048]{1,0:T(8,128)(2,1)S(1)} collective-permute-done((bf16[256,2048]{1,0:T(8,128)(2,1)S(1)}, bf16[256,2048]{1,0:T(8,128)(2,1)S(1)}, u32[]{:S(2)}, u32[]{:S(2)}) %collective-permute-start.18) | collective-permute-done | bytes 1048608 | tf_op jit(solution)/shard_map/ppermute | solution.py:195
  255.2 5.6 collective-permute-done.19
  271.9 2.7 slice_dynamic-update-slice_fusion.5
  274.6 2.7 slice_dynamic-update-slice_fusion.4
  278.6 2.7 slice_dynamic-update-slice_fusion.2
  281.4 2.8 slice_dynamic-update-slice_fusion.1
  288.1 4.6 collective-permute-done.22
  294.5 15.8 %convolution_convert_fusion = bf16[1024,3072]{1,0:T(8,128)(2,1)S(1)} fusion(bf16[1024,2048]{1,0:T(8,128)(2,1)S(1)} %pad_maximum_fusion, bf16[2048,3072]{0,1:T(8,128)(2,1)} %fusion.39), kind=kOutput, calls=%fused_computation.17 | convolution fusion | flops 12888047616 | bytes 23068672 | tf_op jit(solution)/shard_map/dot_general | solution.py:21
  317.8 11.8 %multiply_convert_fusion.1 = (bf16[1024,1536]{1,0:T(8,128)(2,1)S(1)}, bf16[1024,1536]{1,0:T(8,128)(2,1)}) fusion(bf16[1024,3072]{1,0:T(8,128)(2,1)S(1)} %convolution_convert_fusion, bf16[1024,2048]{1,0:T(8,128)(2,1)S(1)} %bitcast.123, bf16[2048,1536]{0,1:T(8,128)(2,1)} %slice_dynamic-update-slice_fusion.7), kind=kOutput, calls=%fused_computation.16 | convolution fusion | flops 6466043904 | bytes 23068672 | tf_op jit(solution)/shard_map/dot_general | solution.py:21
  329.6 5.0 collective-permute-done.25
  341.1 17.8 %convolution_convert_fusion.2 = bf16[1024,2048]{1,0:T(8,128)(2,1)S(1)} fusion(bf16[1024,3072]{1,0:T(8,128)(2,1)S(1)} %constant_dynamic-update-slice_fusion.2, bf16[2048,3072]{0,1:T(8,128)(2,1)} %fusion.39), kind=kOutput, calls=%fused_computation.39 | convolution fusion | flops 12886999040 | bytes 23068672 | tf_op jit(solution)/shard_map/dot_general | solution.py:25
  367.1 4.8 convolution_convert_fusion.1
  374.1 11.3 %collective-permute-done.29 = bf16[1536,256]{1,0:T(8,128)(2,1)S(1)} collective-permute-done((bf16[1536,256]{1,0:T(8,128)(2,1)}, bf16[1536,256]{1,0:T(8,128)(2,1)S(1)}, u32[]{:S(2)}, u32[]{:S(2)}) %collective-permute-start.29) | collective-permute-done | bytes 786464 | tf_op jit(solution)/shard_map/ppermute | solution.py:70
  393.8 3.6 convolution_convert_fusion.5
  397.5 18.4 %collective-permute-done.37 = bf16[256,2048]{1,0:T(8,128)(2,1)S(1)} collective-permute-done((bf16[256,2048]{1,0:T(8,128)(2,1)S(1)}, bf16[256,2048]{1,0:T(8,128)(2,1)S(1)}, u32[]{:S(2)}, u32[]{:S(2)}) %collective-permute-start.37) | collective-permute-done | bytes 1048608 | tf_op jit(solution)/shard_map/ppermute | solution.py:195
  420.0 4.3 fusion.11
  424.3 4.2 fusion.12
  428.7 3.2 fusion.115
  434.0 5.0 add_convert_fusion
  444.1 13.1 %attend_back.2 = (bf16[512,512]{1,0:T(8,128)(2,1)}, bf16[512,512]{1,0:T(8,128)(2,1)}, f32[512,512]{1,0:T(8,128)}, bf16[512,128]{1,0:T(8,128)(2,1)}, f32[8,128]{1,0:T(8,128)}) custom-call(s32[2]{0:T(128)} %add_convert_fusion.5.flag_ref, bf16[1024,512]{1,0:T(8,128)(2,1)} %get-tuple-element.190.q_ref, bf16[1024,512]{1,0:T(8,128)(2,1)} %get-tuple-element.186.kv_ref, ...), custom_call_target="tpu_custom_call" | custom-call | flops 2684354560 | bytes 7864320 | tf_op jit(solution)/shard_map/attend_back/pallas_call | solution.py:755
  457.2 11.9 %collective-permute-done.38 = bf16[256,3072]{1,0:T(8,128)(2,1)} collective-permute-done((bf16[256,3072]{1,0:T(8,128)(2,1)}, bf16[256,3072]{1,0:T(8,128)(2,1)}, u32[]{:S(2)}, u32[]{:S(2)}) %collective-permute-start.38) | collective-permute-done | bytes 1572896 | tf_op jit(solution)/shard_map/ppermute | solution.py:70
  470.4 4.6 fusion.10
  474.9 4.9 fusion.13
  480.5 3.3 fusion.114
  483.9 3.6 fusion.16
  489.5 5.0 convert_add_fusion
  497.8 13.1 %attend_back.3 = (bf16[512,512]{1,0:T(8,128)(2,1)}, bf16[512,512]{1,0:T(8,128)(2,1)}, f32[512,512]{1,0:T(8,128)}, bf16[512,128]{1,0:T(8,128)(2,1)}, f32[8,128]{1,0:T(8,128)}) custom-call(s32[2]{0:T(128)} %add_convert_fusion.5.flag_ref, bf16[1024,512]{1,0:T(8,128)(2,1)} %get-tuple-element.190.q_ref, bf16[1024,512]{1,0:T(8,128)(2,1)} %get-tuple-element.186.kv_ref, ...), custom_call_target="tpu_custom_call" | custom-call | flops 2684354560 | bytes 7864320 | tf_op jit(solution)/shard_map/attend_back/pallas_call | solution.py:755
  510.9 4.2 fusion.8
  525.6 3.6 collective-permute-start.48
  531.7 4.6 fusion.14
  536.3 4.6 fusion.15
  540.9 7.2 %place_layer.1 = bf16[2,2,256,2048]{3,2,1,0:T(8,128)(2,1)} custom-call(s32[8]{0:T(128)} %gather_fusion, s32[1]{0:T(128)} %bitcast.1.core_ref, bf16[2,256,2048]{2,1,0:T(8,128)(2,1)} %bitcast.129, bf16[2,256,2048]{2,1,0:T(8,128)(2,1)} %collective-permute-done.43.other_ref), custom_call_target="tpu_custom_call" | custom-call | flops 1024 | bytes 1024 | tf_op jit(solution)/shard_map/place_layer/pallas_call | solution.py:546
  548.2 4.8 collective-permute-done.46.one_ref
  554.9 2.7 fusion.70
  558.3 4.8 join.2
  563.1 4.9 join.3
  574.8 14.8 %collective-permute-done.49 = bf16[256,3072]{1,0:T(8,128)(2,1)} collective-permute-done((bf16[256,3072]{1,0:T(8,128)(2,1)}, bf16[256,3072]{1,0:T(8,128)(2,1)}, u32[]{:S(2)}, u32[]{:S(2)}) %collective-permute-start.49) | collective-permute-done | bytes 1572896 | tf_op jit(solution)/shard_map/ppermute | solution.py:70
  594.8 5.9 convolution_convert_fusion.4
  600.9 3.1 convolution_convert_fusion.3
  611.8 4.2 fusion.9
  619.8 10.7 %collective-permute-done.58 = f32[2,128]{1,0:T(2,128)S(1)} collective-permute-done((f32[2,128]{1,0:T(2,128)S(1)}, f32[2,128]{1,0:T(2,128)S(1)}, u32[]{:S(2)}, u32[]{:S(2)}) %collective-permute-start.58) | collective-permute-done | bytes 1056 | tf_op jit(solution)/shard_map/ppermute | solution.py:200
  631.7 2.6 collective-permute-done.60.other_ref
  643.2 4.5 input_back.2.refs_0_
  647.7 8.2 %collective-permute-done.64.other_ref = bf16[256,2048]{1,0:T(8,128)(2,1)S(1)} collective-permute-done((bf16[256,2048]{1,0:T(8,128)(2,1)S(1)}, bf16[256,2048]{1,0:T(8,128)(2,1)S(1)}, u32[]{:S(2)}, u32[]{:S(2)}) %collective-permute-start.64) | collective-permute-done | bytes 1048608 | tf_op jit(solution)/shard_map/ppermute | solution.py:195
  660.8 4.3 input_back.3.refs_1_
  674.8 9.5 %place_tokens.1 = f32[2,2,256,2048]{3,2,1,0:T(8,128)} custom-call(s32[8]{0:T(128)} %gather_fusion, s32[1]{0:T(128)} %bitcast.1.core_ref, f32[256,2048]{1,0:T(8,128)} %input_back.2.refs_0_, f32[256,2048]{1,0:T(8,128)} %input_back.3.refs_1_, f32[256,2048]{1,0:T(8,128)} %copy-done.36, f32[256,2048]{1,0:T(8,128)} %copy-done.37), custom_call_target="tpu_custom_call" | custom-call | flops 1024 | bytes 1024 | tf_op jit(solution)/shard_map/place_tokens/pallas_call | solution.py:945
  684.4 3.4 collective-permute-done.67
  (475 shorter events, 208.6 us)
Async XLA Ops:
  5.3 22.3 %collective-permute-start.1 = (bf16[256,1664]{1,0:T(8,128)(2,1)}, bf16[256,1664]{1,0:T(8,128)(2,1)}, u32[]{:S(2)}, u32[]{:S(2)}) collective-permute-start(bf16[256,1664]{1,0:T(8,128)(2,1)} %pack.1), channel_id=1, source_target_pairs={{0,4},{8,0},{16,8},{24,16},{28,24},{20,28},{12,20},{4,12},{1,5},{9... | collective-permute-start | bytes 2555912 | tf_op jit(solution)/shard_map/ppermute | solution.py:70
  8.3 20.7 %collective-permute-start = (bf16[256,1664]{1,0:T(8,128)(2,1)}, bf16[256,1664]{1,0:T(8,128)(2,1)}, u32[]{:S(2)}, u32[]{:S(2)}) collective-permute-start(bf16[256,1664]{1,0:T(8,128)(2,1)} %pack.1), channel_id=1, source_target_pairs={{0,8},{8,16},{16,24},{24,28},{28,20},{20,12},{12,4},{4,0},{1,9},{9... | collective-permute-start | bytes 2555912 | tf_op jit(solution)/shard_map/ppermute | solution.py:70
  29.0 19.7 %collective-permute-start.2 = (bf16[256,1664]{1,0:T(8,128)(2,1)}, bf16[256,1664]{1,0:T(8,128)(2,1)S(1)}, u32[]{:S(2)}, u32[]{:S(2)}) collective-permute-start(bf16[256,1664]{1,0:T(8,128)(2,1)} %collective-permute-done), channel_id=1, source_target_pairs={{0,8},{8,16},{16,24},{24,28},{28,20},{20,12},{12,4},{4,0},{1,9},{9... | collective-permute-start | bytes 2555912 | tf_op jit(solution)/shard_map/ppermute | solution.py:70
  29.3 19.7 %collective-permute-start.3 = (bf16[256,1664]{1,0:T(8,128)(2,1)}, bf16[256,1664]{1,0:T(8,128)(2,1)S(1)}, u32[]{:S(2)}, u32[]{:S(2)}) collective-permute-start(bf16[256,1664]{1,0:T(8,128)(2,1)} %collective-permute-done.1), channel_id=1, source_target_pairs={{0,4},{8,0},{16,8},{24,16},{28,24},{20,28},{12,20},{4,12},{1,5},{9... | collective-permute-start | bytes 2555912 | tf_op jit(solution)/shard_map/ppermute | solution.py:70
  49.1 18.6 %collective-permute-start.4 = (bf16[256,1664]{1,0:T(8,128)(2,1)S(1)}, bf16[256,1664]{1,0:T(8,128)(2,1)S(1)}, u32[]{:S(2)}, u32[]{:S(2)}) collective-permute-start(bf16[256,1664]{1,0:T(8,128)(2,1)S(1)} %collective-permute-done.2), channel_id=1, source_target_pairs={{0,8},{8,16},{16,24},{24,28},{28,20},{20,12},{12,4},{4,0},{1,9},{9... | collective-permute-start | bytes 2555912 | tf_op jit(solution)/shard_map/ppermute | solution.py:70
  50.7 18.2 %collective-permute-start.5 = (bf16[256,1664]{1,0:T(8,128)(2,1)S(1)}, bf16[256,1664]{1,0:T(8,128)(2,1)S(1)}, u32[]{:S(2)}, u32[]{:S(2)}) collective-permute-start(bf16[256,1664]{1,0:T(8,128)(2,1)S(1)} %collective-permute-done.3), channel_id=1, source_target_pairs={{0,4},{8,0},{16,8},{24,16},{28,24},{20,28},{12,20},{4,12},{1,5},{9... | collective-permute-start | bytes 2555912 | tf_op jit(solution)/shard_map/ppermute | solution.py:70
  68.9 7.8 %collective-permute-start.6 = (bf16[256,768]{1,0:T(8,128)(2,1)S(1)}, bf16[256,768]{1,0:T(8,128)(2,1)S(1)}, u32[]{:S(2)}, u32[]{:S(2)}) collective-permute-start(bf16[256,768]{1,0:T(8,128)(2,1)S(1)} %slice.383), channel_id=1, source_target_pairs={{0,8},{8,16},{16,24},{24,28},{28,20},{20,12},{12,4},{4,0},{1,9},{9... | collective-permute-start | bytes 1179656 | tf_op jit(solution)/shard_map/ppermute | solution.py:70
  70.6 10.7 %collective-permute-start.7 = (bf16[256,896]{1,0:T(8,128)(2,1)S(1)}, bf16[256,896]{1,0:T(8,128)(2,1)S(1)}, u32[]{:S(2)}, u32[]{:S(2)}) collective-permute-start(bf16[256,896]{1,0:T(8,128)(2,1)S(1)} %slice.384), channel_id=1, source_target_pairs={{0,4},{8,0},{16,8},{24,16},{28,24},{20,28},{12,20},{4,12},{1,5},{9... | collective-permute-start | bytes 1376264 | tf_op jit(solution)/shard_map/ppermute | solution.py:70
  81.3 73.5 %collective-permute-start.9 = (bf16[256,4608]{0,1:T(8,128)(2,1)S(1)}, bf16[256,4608]{0,1:T(8,128)(2,1)}, u32[]{:S(2)}, u32[]{:S(2)}) collective-permute-start(bf16[256,4608]{0,1:T(8,128)(2,1)S(1)} %pad_maximum_fusion.2), channel_id=1, source_target_pairs={{0,4},{8,0},{16,8},{24,16},{28,24},{20,28},{12,20},{4,12},{1,5},{9... | collective-permute-start | bytes 7077896 | tf_op jit(solution)/shard_map/ppermute | solution.py:70
  81.8 73.1 %collective-permute-start.8 = (bf16[256,4608]{0,1:T(8,128)(2,1)S(1)}, bf16[256,4608]{0,1:T(8,128)(2,1)}, u32[]{:S(2)}, u32[]{:S(2)}) collective-permute-start(bf16[256,4608]{0,1:T(8,128)(2,1)S(1)} %pad_maximum_fusion.2), channel_id=1, source_target_pairs={{0,8},{8,16},{16,24},{24,28},{28,20},{20,12},{12,4},{4,0},{1,9},{9... | collective-permute-start | bytes 7077896 | tf_op jit(solution)/shard_map/ppermute | solution.py:70
  103.4 41.8 %collective-permute-start.12 = (bf16[512,512]{1,0:T(8,128)(2,1)}, bf16[512,512]{1,0:T(8,128)(2,1)}, u32[]{:S(2)}, u32[]{:S(2)}) collective-permute-start(bf16[512,512]{1,0:T(8,128)(2,1)} %slice_select_fusion), channel_id=1, source_target_pairs={{0,12},{12,0},{16,28},{28,16},{1,13},{13,1},{17,29},{29,17},{2,14}... | collective-permute-start | bytes 1572872 | tf_op jit(solution)/shard_map/ppermute | solution.py:632
  105.8 46.4 %collective-permute-start.11 = (bf16[512,512]{1,0:T(8,128)(2,1)}, bf16[512,512]{1,0:T(8,128)(2,1)}, u32[]{:S(2)}, u32[]{:S(2)}) collective-permute-start(bf16[512,512]{1,0:T(8,128)(2,1)} %slice_select_fusion), channel_id=1, source_target_pairs={{0,8},{12,4},{16,24},{28,20},{1,9},{13,5},{17,25},{29,21},{2,10},{... | collective-permute-start | bytes 1572872 | tf_op jit(solution)/shard_map/ppermute | solution.py:631
  109.1 43.1 %collective-permute-start.10 = (bf16[512,512]{1,0:T(8,128)(2,1)}, bf16[512,512]{1,0:T(8,128)(2,1)}, u32[]{:S(2)}, u32[]{:S(2)}) collective-permute-start(bf16[512,512]{1,0:T(8,128)(2,1)} %slice_select_fusion), channel_id=1, source_target_pairs={{0,4},{12,8},{16,20},{28,24},{1,5},{13,9},{17,21},{29,25},{2,6},{1... | collective-permute-start | bytes 1572872 | tf_op jit(solution)/shard_map/ppermute | solution.py:630
  154.8 45.1 %collective-permute-start.13 = (bf16[256,4608]{0,1:T(8,128)(2,1)}, bf16[256,4608]{0,1:T(8,128)(2,1)}, u32[]{:S(2)}, u32[]{:S(2)}) collective-permute-start(bf16[256,4608]{0,1:T(8,128)(2,1)} %collective-permute-done.8), channel_id=1, source_target_pairs={{0,8},{8,16},{16,24},{24,28},{28,20},{20,12},{12,4},{4,0},{1,9},{9... | collective-permute-start | bytes 7077896 | tf_op jit(solution)/shard_map/ppermute | solution.py:70
  157.3 42.6 %collective-permute-start.14 = (bf16[256,4608]{0,1:T(8,128)(2,1)}, bf16[256,4608]{0,1:T(8,128)(2,1)}, u32[]{:S(2)}, u32[]{:S(2)}) collective-permute-start(bf16[256,4608]{0,1:T(8,128)(2,1)} %collective-permute-done.9), channel_id=1, source_target_pairs={{0,4},{8,0},{16,8},{24,16},{28,24},{20,28},{12,20},{4,12},{1,5},{9... | collective-permute-start | bytes 7077896 | tf_op jit(solution)/shard_map/ppermute | solution.py:70
  204.2 26.1 %collective-permute-start.16 = (bf16[256,2048]{1,0:T(8,128)(2,1)S(1)}, bf16[256,2048]{1,0:T(8,128)(2,1)S(1)}, u32[]{:S(2)}, u32[]{:S(2)}) collective-permute-start(bf16[256,2048]{1,0:T(8,128)(2,1)S(1)} %fusion.17), channel_id=1, source_target_pairs={{0,2},{1,3},{2,0},{3,1},{4,6},{5,7},{6,4},{7,5},{8,10},{9,11},{10,... | collective-permute-start | bytes 3145736 | tf_op jit(solution)/shard_map/ppermute | solution.py:195
  206.5 45.4 %collective-permute-start.18 = (bf16[256,2048]{1,0:T(8,128)(2,1)S(1)}, bf16[256,2048]{1,0:T(8,128)(2,1)S(1)}, u32[]{:S(2)}, u32[]{:S(2)}) collective-permute-start(bf16[256,2048]{1,0:T(8,128)(2,1)S(1)} %fusion.18), channel_id=1, source_target_pairs={{0,2},{1,3},{2,0},{3,1},{4,6},{5,7},{6,4},{7,5},{8,10},{9,11},{10,... | collective-permute-start | bytes 3145736 | tf_op jit(solution)/shard_map/ppermute | solution.py:195
  207.2 53.6 %collective-permute-start.19 = (bf16[256,4608]{0,1:T(8,128)(2,1)}, bf16[256,4608]{0,1:T(8,128)(2,1)S(1)}, u32[]{:S(2)}, u32[]{:S(2)}) collective-permute-start(bf16[256,4608]{0,1:T(8,128)(2,1)} %collective-permute-done.13), channel_id=1, source_target_pairs={{0,8},{8,16},{16,24},{24,28},{28,20},{20,12},{12,4},{4,0},{1,9},{9... | collective-permute-start | bytes 7077896 | tf_op jit(solution)/shard_map/ppermute | solution.py:70
  209.7 52.9 %collective-permute-start.20 = (bf16[256,4608]{0,1:T(8,128)(2,1)}, bf16[256,4608]{0,1:T(8,128)(2,1)S(1)}, u32[]{:S(2)}, u32[]{:S(2)}) collective-permute-start(bf16[256,4608]{0,1:T(8,128)(2,1)} %collective-permute-done.14), channel_id=1, source_target_pairs={{0,4},{8,0},{16,8},{24,16},{28,24},{20,28},{12,20},{4,12},{1,5},{9... | collective-permute-start | bytes 7077896 | tf_op jit(solution)/shard_map/ppermute | solution.py:70
  255.2 30.5 %collective-permute-start.24 = (bf16[256,2048]{1,0:T(8,128)(2,1)S(1)}, bf16[256,2048]{1,0:T(8,128)(2,1)S(1)}, u32[]{:S(2)}, u32[]{:S(2)}) collective-permute-start(bf16[256,2048]{1,0:T(8,128)(2,1)S(1)} %get-tuple-element.418), channel_id=1, source_target_pairs={{0,1},{1,0},{2,3},{3,2},{4,5},{5,4},{6,7},{7,6},{8,9},{9,8},{10,11... | collective-permute-start | bytes 3145736 | tf_op jit(solution)/shard_map/ppermute | solution.py:191
  264.2 23.3 %collective-permute-start.23 = (bf16[256,2048]{1,0:T(8,128)(2,1)S(1)}, bf16[256,2048]{1,0:T(8,128)(2,1)S(1)}, u32[]{:S(2)}, u32[]{:S(2)}) collective-permute-start(bf16[256,2048]{1,0:T(8,128)(2,1)S(1)} %get-tuple-element.202), channel_id=1, source_target_pairs={{0,1},{1,0},{2,3},{3,2},{4,5},{5,4},{6,7},{7,6},{8,9},{9,8},{10,11... | collective-permute-start | bytes 3145736 | tf_op jit(solution)/shard_map/ppermute | solution.py:191
  264.2 28.4 %collective-permute-start.22 = (bf16[256,2304]{0,1:T(8,128)(2,1)S(1)}, bf16[256,2304]{0,1:T(8,128)(2,1)S(1)}, u32[]{:S(2)}, u32[]{:S(2)}) collective-permute-start(bf16[256,2304]{0,1:T(8,128)(2,1)S(1)} %slice.413), channel_id=1, source_target_pairs={{0,4},{8,0},{16,8},{24,16},{28,24},{20,28},{12,20},{4,12},{1,5},{9... | collective-permute-start | bytes 3538952 | tf_op jit(solution)/shard_map/ppermute | solution.py:70
  264.6 28.7 %collective-permute-start.21 = (bf16[256,2304]{0,1:T(8,128)(2,1)S(1)}, bf16[256,2304]{0,1:T(8,128)(2,1)S(1)}, u32[]{:S(2)}, u32[]{:S(2)}) collective-permute-start(bf16[256,2304]{0,1:T(8,128)(2,1)S(1)} %slice.412), channel_id=1, source_target_pairs={{0,8},{8,16},{16,24},{24,28},{28,20},{20,12},{12,4},{4,0},{1,9},{9... | collective-permute-start | bytes 3538952 | tf_op jit(solution)/shard_map/ppermute | solution.py:70
  315.6 18.9 %collective-permute-start.25 = (bf16[1536,256]{1,0:T(8,128)(2,1)S(1)}, bf16[1536,256]{1,0:T(8,128)(2,1)S(1)}, u32[]{:S(2)}, u32[]{:S(2)}) collective-permute-start(bf16[1536,256]{1,0:T(8,128)(2,1)S(1)} %convolution_convert_fusion.11), channel_id=1, source_target_pairs={{0,8},{8,16},{16,24},{24,28},{28,20},{20,12},{12,4},{4,0},{1,9},{9... | collective-permute-start | bytes 2359304 | tf_op jit(solution)/shard_map/ppermute | solution.py:70
  317.2 18.7 %collective-permute-start.26 = (bf16[1536,256]{1,0:T(8,128)(2,1)S(1)}, bf16[1536,256]{1,0:T(8,128)(2,1)S(1)}, u32[]{:S(2)}, u32[]{:S(2)}) collective-permute-start(bf16[1536,256]{1,0:T(8,128)(2,1)S(1)} %convolution_convert_fusion.10), channel_id=1, source_target_pairs={{0,4},{8,0},{16,8},{24,16},{28,24},{20,28},{12,20},{4,12},{1,5},{9... | collective-permute-start | bytes 2359304 | tf_op jit(solution)/shard_map/ppermute | solution.py:70
  338.1 20.9 %collective-permute-start.27 = (bf16[1536,256]{1,0:T(8,128)(2,1)S(1)}, bf16[1536,256]{1,0:T(8,128)(2,1)S(1)}, u32[]{:S(2)}, u32[]{:S(2)}) collective-permute-start(bf16[1536,256]{1,0:T(8,128)(2,1)S(1)} %fusion.21), channel_id=1, source_target_pairs={{0,8},{8,16},{16,24},{24,28},{28,20},{20,12},{12,4},{4,0},{1,9},{9... | collective-permute-start | bytes 2359304 | tf_op jit(solution)/shard_map/ppermute | solution.py:70
  339.3 19.7 %collective-permute-start.28 = (bf16[1536,256]{1,0:T(8,128)(2,1)S(1)}, bf16[1536,256]{1,0:T(8,128)(2,1)S(1)}, u32[]{:S(2)}, u32[]{:S(2)}) collective-permute-start(bf16[1536,256]{1,0:T(8,128)(2,1)S(1)} %fusion.22), channel_id=1, source_target_pairs={{0,4},{8,0},{16,8},{24,16},{28,24},{20,28},{12,20},{4,12},{1,5},{9... | collective-permute-start | bytes 2359304 | tf_op jit(solution)/shard_map/ppermute | solution.py:70
  364.9 25.1 %collective-permute-start.36 = (bf16[512,2048]{1,0:T(8,128)(2,1)}, bf16[512,2048]{1,0:T(8,128)(2,1)}, u32[]{:S(2)}, u32[]{:S(2)}) collective-permute-start(bf16[512,2048]{1,0:T(8,128)(2,1)} %pad_maximum_fusion.3), channel_id=1, source_target_pairs={{0,1},{1,0},{2,3},{3,2},{4,5},{5,4},{6,7},{7,6},{8,9},{9,8},{10,11... | collective-permute-start | bytes 6291464 | tf_op jit(solution)/shard_map/ppermute | solution.py:191
  364.9 20.5 %collective-permute-start.29 = (bf16[1536,256]{1,0:T(8,128)(2,1)}, bf16[1536,256]{1,0:T(8,128)(2,1)S(1)}, u32[]{:S(2)}, u32[]{:S(2)}) collective-permute-start(bf16[1536,256]{1,0:T(8,128)(2,1)} %fusion.20), channel_id=1, source_target_pairs={{0,8},{8,16},{16,24},{24,28},{28,20},{20,12},{12,4},{4,0},{1,9},{9... | collective-permute-start | bytes 2359304 | tf_op jit(solution)/shard_map/ppermute | solution.py:70
  366.1 20.8 %collective-permute-start.30 = (bf16[1536,256]{1,0:T(8,128)(2,1)}, bf16[1536,256]{1,0:T(8,128)(2,1)S(1)}, u32[]{:S(2)}, u32[]{:S(2)}) collective-permute-start(bf16[1536,256]{1,0:T(8,128)(2,1)} %fusion.23), channel_id=1, source_target_pairs={{0,4},{8,0},{16,8},{24,16},{28,24},{20,28},{12,20},{4,12},{1,5},{9... | collective-permute-start | bytes 2359304 | tf_op jit(solution)/shard_map/ppermute | solution.py:70
  372.1 47.9 %collective-permute-start.33 = (bf16[256,1536]{1,0:T(8,128)(2,1)S(1)}, bf16[256,1536]{1,0:T(8,128)(2,1)S(1)}, u32[]{:S(2)}, u32[]{:S(2)}) collective-permute-start(bf16[256,1536]{1,0:T(8,128)(2,1)S(1)} %get-tuple-element.231), channel_id=1, source_target_pairs={{0,8},{8,16},{16,24},{24,28},{28,20},{20,12},{12,4},{4,0},{1,9},{9... | collective-permute-start | bytes 2359304 | tf_op jit(solution)/shard_map/ppermute | solution.py:70
  373.3 46.6 %collective-permute-start.34 = (bf16[256,1536]{1,0:T(8,128)(2,1)S(1)}, bf16[256,1536]{1,0:T(8,128)(2,1)S(1)}, u32[]{:S(2)}, u32[]{:S(2)}) collective-permute-start(bf16[256,1536]{1,0:T(8,128)(2,1)S(1)} %get-tuple-element.232), channel_id=1, source_target_pairs={{0,4},{8,0},{16,8},{24,16},{28,24},{20,28},{12,20},{4,12},{1,5},{9... | collective-permute-start | bytes 2359304 | tf_op jit(solution)/shard_map/ppermute | solution.py:70
  389.2 30.8 %collective-permute-start.35 = (bf16[1536,256]{1,0:T(8,128)(2,1)S(1)}, bf16[1536,256]{1,0:T(8,128)(2,1)S(1)}, u32[]{:S(2)}, u32[]{:S(2)}) collective-permute-start(bf16[1536,256]{1,0:T(8,128)(2,1)S(1)} %fusion.19), channel_id=1, source_target_pairs={{0,4},{8,0},{16,8},{24,16},{28,24},{20,28},{12,20},{4,12},{1,5},{9... | collective-permute-start | bytes 2359304 | tf_op jit(solution)/shard_map/ppermute | solution.py:70
  392.3 23.6 %collective-permute-start.37 = (bf16[256,2048]{1,0:T(8,128)(2,1)S(1)}, bf16[256,2048]{1,0:T(8,128)(2,1)S(1)}, u32[]{:S(2)}, u32[]{:S(2)}) collective-permute-start(bf16[256,2048]{1,0:T(8,128)(2,1)S(1)} %get-tuple-element.395), channel_id=1, source_target_pairs={{0,2},{1,3},{2,0},{3,1},{4,6},{5,7},{6,4},{7,5},{8,10},{9,11},{10,... | collective-permute-start | bytes 3145736 | tf_op jit(solution)/shard_map/ppermute | solution.py:195
  397.5 36.5 %collective-permute-start.31 = (bf16[512,2048]{1,0:T(8,128)(2,1)S(1)}, bf16[512,2048]{1,0:T(8,128)(2,1)S(1)}, u32[]{:S(2)}, u32[]{:S(2)}) collective-permute-start(bf16[512,2048]{1,0:T(8,128)(2,1)S(1)} %convolution_convert_fusion.5), channel_id=1, source_target_pairs={{0,1},{1,0},{2,3},{3,2},{4,5},{5,4},{6,7},{7,6},{8,9},{9,8},{10,11... | collective-permute-start | bytes 6291464 | tf_op jit(solution)/shard_map/ppermute | solution.py:191
  415.9 24.2 %collective-permute-start.41 = (bf16[256,2048]{1,0:T(8,128)(2,1)S(1)}, bf16[256,2048]{1,0:T(8,128)(2,1)S(1)}, u32[]{:S(2)}, u32[]{:S(2)}) collective-permute-start(bf16[256,2048]{1,0:T(8,128)(2,1)S(1)} %get-tuple-element.394), channel_id=1, source_target_pairs={{0,2},{1,3},{2,0},{3,1},{4,6},{5,7},{6,4},{7,5},{8,10},{9,11},{10,... | collective-permute-start | bytes 3145736 | tf_op jit(solution)/shard_map/ppermute | solution.py:195
  432.0 9.9 %collective-permute-start.40 = (bf16[256,2048]{1,0:T(8,128)(2,1)S(1)}, bf16[256,2048]{1,0:T(8,128)(2,1)S(1)}, u32[]{:S(2)}, u32[]{:S(2)}) collective-permute-start(bf16[256,2048]{1,0:T(8,128)(2,1)S(1)} %get-tuple-element.382), channel_id=1, source_target_pairs={{0,1},{1,0},{2,3},{3,2},{4,5},{5,4},{6,7},{7,6},{8,9},{9,8},{10,11... | collective-permute-start | bytes 3145736 | tf_op jit(solution)/shard_map/ppermute | solution.py:191
  432.0 37.1 %collective-permute-start.38 = (bf16[256,3072]{1,0:T(8,128)(2,1)}, bf16[256,3072]{1,0:T(8,128)(2,1)}, u32[]{:S(2)}, u32[]{:S(2)}) collective-permute-start(bf16[256,3072]{1,0:T(8,128)(2,1)} %fusion.11), channel_id=1, source_target_pairs={{0,8},{8,16},{16,24},{24,28},{28,20},{20,12},{12,4},{4,0},{1,9},{9... | collective-permute-start | bytes 4718600 | tf_op jit(solution)/shard_map/ppermute | solution.py:70
  433.5 36.8 %collective-permute-start.39 = (bf16[256,3072]{1,0:T(8,128)(2,1)}, bf16[256,3072]{1,0:T(8,128)(2,1)}, u32[]{:S(2)}, u32[]{:S(2)}) collective-permute-start(bf16[256,3072]{1,0:T(8,128)(2,1)} %fusion.12), channel_id=1, source_target_pairs={{0,4},{8,0},{16,8},{24,16},{28,24},{20,28},{12,20},{4,12},{1,5},{9... | collective-permute-start | bytes 4718600 | tf_op jit(solution)/shard_map/ppermute | solution.py:70
  439.0 50.5 %collective-permute-start.32 = (bf16[512,2048]{1,0:T(8,128)(2,1)}, bf16[512,2048]{1,0:T(8,128)(2,1)}, u32[]{:S(2)}, u32[]{:S(2)}) collective-permute-start(bf16[512,2048]{1,0:T(8,128)(2,1)} %add_convert_fusion), channel_id=1, source_target_pairs={{0,2},{1,3},{2,0},{3,1},{4,6},{5,7},{6,4},{7,5},{8,10},{9,11},{10,... | collective-permute-start | bytes 6291464 | tf_op jit(solution)/shard_map/ppermute | solution.py:195
  483.9 10.7 %collective-permute-start.42 = (bf16[256,2048]{1,0:T(8,128)(2,1)S(1)}, bf16[256,2048]{1,0:T(8,128)(2,1)S(1)}, u32[]{:S(2)}, u32[]{:S(2)}) collective-permute-start(bf16[256,2048]{1,0:T(8,128)(2,1)S(1)} %get-tuple-element.380), channel_id=1, source_target_pairs={{0,1},{1,0},{2,3},{3,2},{4,5},{5,4},{6,7},{7,6},{8,9},{9,8},{10,11... | collective-permute-start | bytes 3145736 | tf_op jit(solution)/shard_map/ppermute | solution.py:191
  487.5 36.7 %collective-permute-start.44 = (bf16[256,3072]{1,0:T(8,128)(2,1)}, bf16[256,3072]{1,0:T(8,128)(2,1)}, u32[]{:S(2)}, u32[]{:S(2)}) collective-permute-start(bf16[256,3072]{1,0:T(8,128)(2,1)} %fusion.10), channel_id=1, source_target_pairs={{0,8},{8,16},{16,24},{24,28},{28,20},{20,12},{12,4},{4,0},{1,9},{9... | collective-permute-start | bytes 4718600 | tf_op jit(solution)/shard_map/ppermute | solution.py:70
  487.8 36.5 %collective-permute-start.45 = (bf16[256,3072]{1,0:T(8,128)(2,1)}, bf16[256,3072]{1,0:T(8,128)(2,1)}, u32[]{:S(2)}, u32[]{:S(2)}) collective-permute-start(bf16[256,3072]{1,0:T(8,128)(2,1)} %fusion.13), channel_id=1, source_target_pairs={{0,4},{8,0},{16,8},{24,16},{28,24},{20,28},{12,20},{4,12},{1,5},{9... | collective-permute-start | bytes 4718600 | tf_op jit(solution)/shard_map/ppermute | solution.py:70
  515.2 25.7 %collective-permute-start.43 = (bf16[2,256,2048]{2,1,0:T(8,128)(2,1)S(1)}, bf16[2,256,2048]{2,1,0:T(8,128)(2,1)}, u32[]{:S(2)}, u32[]{:S(2)}) collective-permute-start(bf16[2,256,2048]{2,1,0:T(8,128)(2,1)S(1)} %bitcast.128), channel_id=1, source_target_pairs={{0,1},{1,0},{2,3},{3,2},{4,5},{5,4},{6,7},{7,6},{8,9},{9,8},{10,11... | collective-permute-start | bytes 6291464 | tf_op jit(solution)/shard_map/ppermute | solution.py:191
  525.6 22.6 %collective-permute-start.48 = (bf16[512,512]{1,0:T(8,128)(2,1)}, bf16[512,512]{1,0:T(8,128)(2,1)S(1)}, u32[]{:S(2)}, u32[]{:S(2)}) collective-permute-start(bf16[512,512]{1,0:T(8,128)(2,1)} %get-tuple-element.413), channel_id=1, source_target_pairs={{12,0},{0,12},{28,16},{16,28},{13,1},{1,13},{29,17},{17,29},{14,2}... | collective-permute-start | bytes 1572872 | tf_op jit(solution)/shard_map/ppermute | solution.py:817
  529.1 19.0 %collective-permute-start.47 = (bf16[512,512]{1,0:T(8,128)(2,1)}, bf16[512,512]{1,0:T(8,128)(2,1)S(1)}, u32[]{:S(2)}, u32[]{:S(2)}) collective-permute-start(bf16[512,512]{1,0:T(8,128)(2,1)} %get-tuple-element.414), channel_id=1, source_target_pairs={{8,0},{4,12},{24,16},{20,28},{9,1},{5,13},{25,17},{21,29},{10,2},{... | collective-permute-start | bytes 1572872 | tf_op jit(solution)/shard_map/ppermute | solution.py:817
  530.4 22.5 %collective-permute-start.46 = (bf16[512,512]{1,0:T(8,128)(2,1)}, bf16[512,512]{1,0:T(8,128)(2,1)S(1)}, u32[]{:S(2)}, u32[]{:S(2)}) collective-permute-start(bf16[512,512]{1,0:T(8,128)(2,1)} %get-tuple-element.415), channel_id=1, source_target_pairs={{4,0},{8,12},{20,16},{24,28},{5,1},{9,13},{21,17},{25,29},{6,2},{1... | collective-permute-start | bytes 1572872 | tf_op jit(solution)/shard_map/ppermute | solution.py:817
  552.9 36.6 %collective-permute-start.49 = (bf16[256,3072]{1,0:T(8,128)(2,1)}, bf16[256,3072]{1,0:T(8,128)(2,1)}, u32[]{:S(2)}, u32[]{:S(2)}) collective-permute-start(bf16[256,3072]{1,0:T(8,128)(2,1)} %fusion.14), channel_id=1, source_target_pairs={{0,8},{8,16},{16,24},{24,28},{28,20},{20,12},{12,4},{4,0},{1,9},{9... | collective-permute-start | bytes 4718600 | tf_op jit(solution)/shard_map/ppermute | solution.py:70
  552.9 36.6 %collective-permute-start.50 = (bf16[256,3072]{1,0:T(8,128)(2,1)}, bf16[256,3072]{1,0:T(8,128)(2,1)}, u32[]{:S(2)}, u32[]{:S(2)}) collective-permute-start(bf16[256,3072]{1,0:T(8,128)(2,1)} %fusion.15), channel_id=1, source_target_pairs={{0,4},{8,0},{16,8},{24,16},{28,24},{20,28},{12,20},{4,12},{1,5},{9... | collective-permute-start | bytes 4718600 | tf_op jit(solution)/shard_map/ppermute | solution.py:70
  592.7 15.1 %collective-permute-start.53 = (bf16[256,768]{1,0:T(8,128)(2,1)S(1)}, bf16[256,768]{1,0:T(8,128)(2,1)S(1)}, u32[]{:S(2)}, u32[]{:S(2)}) collective-permute-start(bf16[256,768]{1,0:T(8,128)(2,1)S(1)} %slice.528), channel_id=1, source_target_pairs={{0,8},{8,16},{16,24},{24,28},{28,20},{20,12},{12,4},{4,0},{1,9},{9... | collective-permute-start | bytes 1179656 | tf_op jit(solution)/shard_map/ppermute | solution.py:70
  594.4 13.5 %collective-permute-start.54 = (bf16[256,896]{1,0:T(8,128)(2,1)S(1)}, bf16[256,896]{1,0:T(8,128)(2,1)S(1)}, u32[]{:S(2)}, u32[]{:S(2)}) collective-permute-start(bf16[256,896]{1,0:T(8,128)(2,1)S(1)} %pad_maximum_fusion.9), channel_id=1, source_target_pairs={{0,4},{8,0},{16,8},{24,16},{28,24},{20,28},{12,20},{4,12},{1,5},{9... | collective-permute-start | bytes 1376264 | tf_op jit(solution)/shard_map/ppermute | solution.py:70
  608.3 26.1 %collective-permute-start.60 = (bf16[256,2048]{1,0:T(8,128)(2,1)S(1)}, bf16[256,2048]{1,0:T(8,128)(2,1)S(1)}, u32[]{:S(2)}, u32[]{:S(2)}) collective-permute-start(bf16[256,2048]{1,0:T(8,128)(2,1)S(1)} %add_convert_fusion.1.chip_ref), channel_id=1, source_target_pairs={{0,2},{1,3},{2,0},{3,1},{4,6},{5,7},{6,4},{7,5},{8,10},{9,11},{10,... | collective-permute-start | bytes 3145736 | tf_op jit(solution)/shard_map/ppermute | solution.py:195
  609.7 20.7 %collective-permute-start.56 = (bf16[256,1664]{1,0:T(8,128)(2,1)S(1)}, bf16[256,1664]{1,0:T(8,128)(2,1)S(1)}, u32[]{:S(2)}, u32[]{:S(2)}) collective-permute-start(bf16[256,1664]{1,0:T(8,128)(2,1)S(1)} %fusion.34), channel_id=1, source_target_pairs={{0,8},{8,16},{16,24},{24,28},{28,20},{20,12},{12,4},{4,0},{1,9},{9... | collective-permute-start | bytes 2555912 | tf_op jit(solution)/shard_map/ppermute | solution.py:70
  611.4 20.3 %collective-permute-start.57 = (bf16[256,1664]{1,0:T(8,128)(2,1)S(1)}, bf16[256,1664]{1,0:T(8,128)(2,1)S(1)}, u32[]{:S(2)}, u32[]{:S(2)}) collective-permute-start(bf16[256,1664]{1,0:T(8,128)(2,1)S(1)} %fusion.35), channel_id=1, source_target_pairs={{0,4},{8,0},{16,8},{24,16},{28,24},{20,28},{12,20},{4,12},{1,5},{9... | collective-permute-start | bytes 2555912 | tf_op jit(solution)/shard_map/ppermute | solution.py:70
  616.1 14.4 %collective-permute-start.58 = (f32[2,128]{1,0:T(2,128)S(1)}, f32[2,128]{1,0:T(2,128)S(1)}, u32[]{:S(2)}, u32[]{:S(2)}) collective-permute-start(f32[2,128]{1,0:T(2,128)S(1)} %fusion.178), channel_id=1, source_target_pairs={{0,4},{4,0},{8,12},{12,8},{16,20},{20,16},{24,28},{28,24},{1,5},{5... | collective-permute-start | bytes 3080 | tf_op jit(solution)/shard_map/ppermute | solution.py:200
  618.8 37.2 %collective-permute-start.64 = (bf16[256,2048]{1,0:T(8,128)(2,1)S(1)}, bf16[256,2048]{1,0:T(8,128)(2,1)S(1)}, u32[]{:S(2)}, u32[]{:S(2)}) collective-permute-start(bf16[256,2048]{1,0:T(8,128)(2,1)S(1)} %add_convert_fusion.2.chip_ref), channel_id=1, source_target_pairs={{0,2},{1,3},{2,0},{3,1},{4,6},{5,7},{6,4},{7,5},{8,10},{9,11},{10,... | collective-permute-start | bytes 3145736 | tf_op jit(solution)/shard_map/ppermute | solution.py:195
  635.7 20.6 %collective-permute-start.61 = (bf16[256,1664]{1,0:T(8,128)(2,1)}, bf16[256,1664]{1,0:T(8,128)(2,1)}, u32[]{:S(2)}, u32[]{:S(2)}) collective-permute-start(bf16[256,1664]{1,0:T(8,128)(2,1)} %fusion.33), channel_id=1, source_target_pairs={{0,8},{8,16},{16,24},{24,28},{28,20},{20,12},{12,4},{4,0},{1,9},{9... | collective-permute-start | bytes 2555912 | tf_op jit(solution)/shard_map/ppermute | solution.py:70
  637.3 19.0 %collective-permute-start.62 = (bf16[256,1664]{1,0:T(8,128)(2,1)S(1)}, bf16[256,1664]{1,0:T(8,128)(2,1)}, u32[]{:S(2)}, u32[]{:S(2)}) collective-permute-start(bf16[256,1664]{1,0:T(8,128)(2,1)S(1)} %fusion.36), channel_id=1, source_target_pairs={{0,4},{8,0},{16,8},{24,16},{28,24},{20,28},{12,20},{4,12},{1,5},{9... | collective-permute-start | bytes 2555912 | tf_op jit(solution)/shard_map/ppermute | solution.py:70
  640.7 15.6 %collective-permute-start.63 = (f32[2,128]{1,0:T(2,128)S(1)}, f32[2,128]{1,0:T(2,128)S(1)}, u32[]{:S(2)}, u32[]{:S(2)}) collective-permute-start(f32[2,128]{1,0:T(2,128)S(1)} %add.438), channel_id=1, source_target_pairs={{0,8},{4,12},{8,0},{12,4},{16,24},{20,28},{24,16},{28,20},{1,9},{5... | collective-permute-start | bytes 3080 | tf_op jit(solution)/shard_map/ppermute | solution.py:200
  655.9 16.2 %collective-permute-start.68 = (f32[256,2048]{1,0:T(8,128)}, f32[256,2048]{1,0:T(8,128)S(1)}, u32[]{:S(2)}, u32[]{:S(2)}) collective-permute-start(f32[256,2048]{1,0:T(8,128)} %input_back.2.refs_0_), channel_id=1, source_target_pairs={{0,1},{1,0},{2,3},{3,2},{4,5},{5,4},{6,7},{7,6},{8,9},{9,8},{10,11... | collective-permute-start | bytes 6291464 | tf_op jit(solution)/shard_map/ppermute | solution.py:191
  665.1 7.0 %collective-permute-start.69 = (f32[256,2048]{1,0:T(8,128)}, f32[256,2048]{1,0:T(8,128)S(1)}, u32[]{:S(2)}, u32[]{:S(2)}) collective-permute-start(f32[256,2048]{1,0:T(8,128)} %input_back.3.refs_1_), channel_id=1, source_target_pairs={{0,1},{1,0},{2,3},{3,2},{4,5},{5,4},{6,7},{7,6},{8,9},{9,8},{10,11... | collective-permute-start | bytes 6291464 | tf_op jit(solution)/shard_map/ppermute | solution.py:191
  665.3 22.5 %collective-permute-start.65 = (bf16[256,1664]{1,0:T(8,128)(2,1)}, bf16[256,1664]{1,0:T(8,128)(2,1)}, u32[]{:S(2)}, u32[]{:S(2)}) collective-permute-start(bf16[256,1664]{1,0:T(8,128)(2,1)} %fusion.32), channel_id=1, source_target_pairs={{0,8},{8,16},{16,24},{24,28},{28,20},{20,12},{12,4},{4,0},{1,9},{9... | collective-permute-start | bytes 2555912 | tf_op jit(solution)/shard_map/ppermute | solution.py:70
  666.9 21.3 %collective-permute-start.66 = (bf16[256,1664]{1,0:T(8,128)(2,1)}, bf16[256,1664]{1,0:T(8,128)(2,1)}, u32[]{:S(2)}, u32[]{:S(2)}) collective-permute-start(bf16[256,1664]{1,0:T(8,128)(2,1)} %fusion.37), channel_id=1, source_target_pairs={{0,4},{8,0},{16,8},{24,16},{28,24},{20,28},{12,20},{4,12},{1,5},{9... | collective-permute-start | bytes 2555912 | tf_op jit(solution)/shard_map/ppermute | solution.py:70
  668.8 19.0 %collective-permute-start.67 = (f32[2,128]{1,0:T(2,128)S(1)}, f32[2,128]{1,0:T(2,128)S(1)}, u32[]{:S(2)}, u32[]{:S(2)}) collective-permute-start(f32[2,128]{1,0:T(2,128)S(1)} %add.446), channel_id=1, source_target_pairs={{0,16},{4,20},{8,24},{12,28},{16,0},{20,4},{24,8},{28,12},{1,17},{... | collective-permute-start | bytes 3080 | tf_op jit(solution)/shard_map/ppermute | solution.py:200
  (96 other events, 825.0 us)
